TPU v7x, 32 devices: a whole 2x2x4 slice. The times are simulated.
32 devices in a mesh: seq: 2 (over x), dp: 16 (over z, y, core).
Axes of the slice: x: 2, y: 2, z: 4, core: 2. Of those that a mesh axis runs over, the one named last changes fastest.
Arguments:
- tokens: bfloat16 [16, 1024, 768], P('dp', 'seq'), may hold values from -6 to 6
- timesteps: int32 [16], P('dp'), may hold values from 0 to 999
- starts: int32 [16, 2], P('dp'), may hold values from 0 to 768, as said below
- cotangent: bfloat16 [16, 1024, 768], P('dp', 'seq'), may hold values from -6 to 6
- ln1_gain: bfloat16 [768], P(('seq', 'dp')), may hold values from 0.099609375 to 1.8984375
- ln1_bias: bfloat16 [768], P(('seq', 'dp')), may hold values from -3 to 3
- w_qkv: bfloat16 [768, 2304], P(('seq', 'dp')), may hold values from -0.21875 to 0.21875
- bias_query: bfloat16 [768], P(('seq', 'dp')), may hold values from -3 to 3
- bias_value: bfloat16 [768], P(('seq', 'dp')), may hold values from -3 to 3
- w_out: bfloat16 [768, 768], P(('seq', 'dp')), may hold values from -3 to 3
- bias_out: bfloat16 [768], P(('seq', 'dp')), may hold values from -3 to 3
- ln2_gain: bfloat16 [768], P(('seq', 'dp')), may hold values from 0.099609375 to 1.8984375
- ln2_bias: bfloat16 [768], P(('seq', 'dp')), may hold values from -3 to 3
- w_up: bfloat16 [768, 3072], P(('seq', 'dp')), may hold values from -0.21875 to 0.21875
- bias_up: bfloat16 [3072], P(('seq', 'dp')), may hold values from -3 to 3
- w_down: bfloat16 [3072, 768], P(('seq', 'dp')), may hold values from -0.109375 to 0.109375
- bias_down: bfloat16 [768], P(('seq', 'dp')), may hold values from -3 to 3
- time_table: bfloat16 [1000, 768], P(None, ('seq', 'dp')), may hold values from -6 to 6
Outputs:
- block_out: bfloat16 [16, 1024, 768], P('dp', 'seq')
- grad_tokens: bfloat16 [16, 1024, 768], P('dp', 'seq')
- grad_ln1_gain: float32 [768], P(('seq', 'dp'))
- grad_ln1_bias: float32 [768], P(('seq', 'dp'))
- grad_w_qkv: float32 [768, 2304], P(('seq', 'dp'))
- grad_bias_query: float32 [768], P(('seq', 'dp'))
- grad_bias_value: float32 [768], P(('seq', 'dp'))
- grad_w_out: float32 [768, 768], P(('seq', 'dp'))
- grad_bias_out: float32 [768], P(('seq', 'dp'))
- grad_ln2_gain: float32 [768], P(('seq', 'dp'))
- grad_ln2_bias: float32 [768], P(('seq', 'dp'))
- grad_w_up: float32 [768, 3072], P(('seq', 'dp'))
- grad_bias_up: float32 [3072], P(('seq', 'dp'))
- grad_w_down: float32 [3072, 768], P(('seq', 'dp'))
- grad_bias_down: float32 [768], P(('seq', 'dp'))
- grad_time_table: float32 [1000, 768], P(None, ('seq', 'dp'))
Inputs may be any that keep to these rules, and one draw needn't show every extreme that they name: The 2 pieces of a sequence do not intersect; piece k starts in positions k * 512 to (k + 1) * 512 - 256.
All inputs are finite; a program needn't handle non-finite values.
Results may differ from a plain program's by a relative error of at most 0.035.
Values may be sent and summed in bfloat16 or wider, within the bound.
No kernel may reach another device: no remote copies, remote signals or barrier semaphores. Data moves between devices by JAX's collectives and lax.ppermute only.
A program may use at most 192 MiB of HBM per device.

v0:
```python
import jax
import jax.numpy as jnp
from jax import lax
from jax.experimental import pallas as pl
from jax.experimental.pallas import tpu as pltpu
from jax.sharding import PartitionSpec as P


D = 768
HEADS = 12
HD = 64
TSTEPS = 1000
PIC = 256
NPIC = 2


epsilon = 1e-05


def layer_norm(values, gain, shift):
    average = jnp.mean(values, axis=-1, keepdims=True)
    centred = values - average
    spread = jnp.mean(centred * centred, axis=-1, keepdims=True)
    return centred * lax.rsqrt(spread + epsilon) * gain + shift


def piece_label(starts, places):
    inside = (places[None, None, :] >= starts[:, :, None]) & (
        places[None, None, :] < starts[:, :, None] + PIC
    )
    number = jnp.arange(1, NPIC + 1, dtype=jnp.int32)
    return jnp.sum(inside.astype(jnp.int32) * number[None, :, None], axis=1)


def visible_mask(starts, query_pos, key_pos):
    label_query = piece_label(starts, query_pos)
    label_key = piece_label(starts, key_pos)
    causal = query_pos[:, None] >= key_pos[None, :]
    return causal[None] | (label_query[:, :, None] == label_key[:, None, :]) & (
        label_query[:, :, None] > 0
    )


def dense(left, right):
    return jnp.dot(left, right, preferred_element_type=jnp.float32)


def dense_left(left, right):
    return lax.dot_general(
        left, right, (((0,), (0,)), ((), ())), preferred_element_type=jnp.float32
    )


def dense_right(left, right):
    return lax.dot_general(
        left, right, (((1,), (1,)), ((), ())), preferred_element_type=jnp.float32
    )


def head_slice(array, index):
    return lax.dynamic_slice_in_dim(array, index * HD, HD, 2)


def merge_heads(stacked):
    head_count, seq_count, row_count, head_size = stacked.shape
    return jnp.transpose(stacked, (1, 2, 0, 3)).reshape(
        seq_count, row_count, head_count * head_size
    )


def shards(
    tokens,
    timesteps,
    starts,
    cotangent,
    ln1_gain,
    ln1_bias,
    w_qkv,
    bias_query,
    bias_value,
    w_out,
    bias_out,
    ln2_gain,
    ln2_bias,
    w_up,
    bias_up,
    w_down,
    bias_down,
    time_table,
):
    gathered = (
        lax.all_gather(ln1_gain, ("seq", "dp"), axis=0, tiled=True),
        lax.all_gather(ln1_bias, ("seq", "dp"), axis=0, tiled=True),
        lax.all_gather(w_qkv, ("seq", "dp"), axis=0, tiled=True),
        lax.all_gather(bias_query, ("seq", "dp"), axis=0, tiled=True),
        lax.all_gather(bias_value, ("seq", "dp"), axis=0, tiled=True),
        lax.all_gather(w_out, ("seq", "dp"), axis=0, tiled=True),
        lax.all_gather(bias_out, ("seq", "dp"), axis=0, tiled=True),
        lax.all_gather(ln2_gain, ("seq", "dp"), axis=0, tiled=True),
        lax.all_gather(ln2_bias, ("seq", "dp"), axis=0, tiled=True),
        lax.all_gather(w_up, ("seq", "dp"), axis=0, tiled=True),
        lax.all_gather(bias_up, ("seq", "dp"), axis=0, tiled=True),
        lax.all_gather(w_down, ("seq", "dp"), axis=0, tiled=True),
        lax.all_gather(bias_down, ("seq", "dp"), axis=0, tiled=True),
        lax.all_gather(time_table, ("seq", "dp"), axis=1, tiled=True),
    )
    (
        gain_one,
        shift_one,
        qkv_full,
        query_shift,
        value_shift,
        out_full,
        out_shift,
        gain_two,
        shift_two,
        up_full,
        up_shift,
        down_full,
        down_shift,
        table_full,
    ) = gathered
    seq_count, row_count, model_width = tokens.shape
    flat_rows = seq_count * row_count
    scale = HD ** (-0.5)
    levels = jnp.arange(TSTEPS, dtype=jnp.int32)
    onehot = timesteps[:, None] == levels[None, :]
    embed = dense(onehot.astype(jnp.bfloat16), table_full)
    start_sum = (tokens.astype(jnp.float32) + embed[:, None, :]).reshape(flat_rows, model_width)
    norm_one, pull_one = jax.vjp(
        layer_norm, start_sum, gain_one.astype(jnp.float32), shift_one.astype(jnp.float32)
    )
    normed_one = norm_one.astype(jnp.bfloat16)
    joined = dense(normed_one, qkv_full)
    query = (
        (joined[:, :D] + query_shift.astype(jnp.float32))
        .astype(jnp.bfloat16)
        .reshape(seq_count, row_count, D)
    )
    keys = joined[:, D : 2 * D].astype(jnp.bfloat16).reshape(seq_count, row_count, D)
    values = (
        (joined[:, 2 * D :] + value_shift.astype(jnp.float32))
        .astype(jnp.bfloat16)
        .reshape(seq_count, row_count, D)
    )
    key_all, value_all = (
        lax.all_gather(keys, "seq", axis=1, tiled=True),
        lax.all_gather(values, "seq", axis=1, tiled=True),
    )
    full_len = key_all.shape[1]
    query_pos = lax.axis_index("seq") * row_count + jnp.arange(row_count, dtype=jnp.int32)
    every_pos = jnp.arange(full_len, dtype=jnp.int32)
    allowed = visible_mask(starts, query_pos, every_pos)

    def head_forward(index):
        query_head = head_slice(query, index)
        key_head = head_slice(key_all, index)
        value_head = head_slice(value_all, index)
        scores = scale * jnp.einsum(
            "sre,ske->srk", query_head, key_head, preferred_element_type=jnp.float32
        )
        scores = jnp.where(allowed, scores, -1e30)
        top = jnp.max(scores, axis=-1, keepdims=True)
        expo = jnp.exp(scores - top)
        total = jnp.sum(expo, axis=-1, keepdims=True)
        probs = expo / total
        result = jnp.einsum(
            "srk,ske->sre",
            probs.astype(jnp.bfloat16),
            value_head,
            preferred_element_type=jnp.float32,
        )
        return (result, top[..., 0] + jnp.log(total[..., 0]))

    head_out, log_total = lax.map(head_forward, jnp.arange(HEADS, dtype=jnp.int32))
    heads_out = merge_heads(head_out).astype(jnp.bfloat16).reshape(flat_rows, D)
    mid = start_sum + dense(heads_out, out_full) + out_shift.astype(jnp.float32)
    norm_two, pull_two = jax.vjp(
        layer_norm, mid, gain_two.astype(jnp.float32), shift_two.astype(jnp.float32)
    )
    normed_two = norm_two.astype(jnp.bfloat16)
    up_pre = dense(normed_two, up_full) + up_shift.astype(jnp.float32)
    act_value, pull_act = jax.vjp(jax.nn.gelu, up_pre)
    act = act_value.astype(jnp.bfloat16)
    block_out = (mid + dense(act, down_full) + down_shift.astype(jnp.float32)).astype(jnp.bfloat16)
    qkv_back, out_back, up_back, down_back = (
        lax.all_gather(w_qkv, ("seq", "dp"), axis=0, tiled=True),
        lax.all_gather(w_out, ("seq", "dp"), axis=0, tiled=True),
        lax.all_gather(w_up, ("seq", "dp"), axis=0, tiled=True),
        lax.all_gather(w_down, ("seq", "dp"), axis=0, tiled=True),
    )
    grad_mlp = cotangent.reshape(flat_rows, D)
    grad_down = dense_left(act, grad_mlp)
    grad_down_shift = jnp.sum(grad_mlp.astype(jnp.float32), axis=0)
    grad_act = dense_right(grad_mlp, down_back)
    (grad_up_pre,) = pull_act(grad_act)
    grad_up_low = grad_up_pre.astype(jnp.bfloat16)
    grad_up = dense_left(normed_two, grad_up_low)
    grad_up_shift = jnp.sum(grad_up_low.astype(jnp.float32), axis=0)
    grad_norm_two = dense_right(grad_up_low, up_back)
    grad_mid_norm, grad_gain_two, grad_shift_two = pull_two(grad_norm_two)
    grad_mid = cotangent.reshape(flat_rows, D).astype(jnp.float32) + grad_mid_norm
    grad_attn = grad_mid.astype(jnp.bfloat16)
    grad_out_w = dense_left(heads_out, grad_attn)
    grad_out_shift = jnp.sum(grad_attn.astype(jnp.float32), axis=0)
    grad_heads = (
        dense_right(grad_attn, out_back).astype(jnp.bfloat16).reshape(seq_count, row_count, D)
    )
    key_back, value_back = (
        lax.all_gather(keys, "seq", axis=1, tiled=True),
        lax.all_gather(values, "seq", axis=1, tiled=True),
    )

    def query_side(index, log_head):
        query_head = head_slice(query, index)
        key_head = head_slice(key_back, index)
        value_head = head_slice(value_back, index)
        grad_head = head_slice(grad_heads, index)
        scores = scale * jnp.einsum(
            "sre,ske->srk", query_head, key_head, preferred_element_type=jnp.float32
        )
        scores = jnp.where(allowed, scores, -1e30)
        probs = jnp.exp(scores - log_head[..., None])
        grad_probs = jnp.einsum(
            "sre,ske->srk", grad_head, value_head, preferred_element_type=jnp.float32
        )
        delta = jnp.sum(probs * grad_probs, axis=-1, keepdims=True)
        grad_scores = (probs * (grad_probs - delta)).astype(jnp.bfloat16)
        grad_query_head = scale * jnp.einsum(
            "srk,ske->sre", grad_scores, key_head, preferred_element_type=jnp.float32
        )
        return (probs, grad_scores, delta[..., 0], grad_query_head)

    def query_only(inputs):
        index, log_head = inputs
        _, _, delta, grad_query_head = query_side(index, log_head)
        return (grad_query_head, delta)

    grad_query_heads, delta_heads = lax.map(
        query_only, (jnp.arange(HEADS, dtype=jnp.int32), log_total)
    )
    query_every, grad_every, log_every, delta_every = (
        lax.all_gather(query, "seq", axis=1, tiled=True),
        lax.all_gather(grad_heads, "seq", axis=1, tiled=True),
        lax.all_gather(log_total.astype(jnp.bfloat16), "seq", axis=2, tiled=True).astype(
            log_total.dtype
        ),
        lax.all_gather(delta_heads.astype(jnp.bfloat16), "seq", axis=2, tiled=True).astype(
            delta_heads.dtype
        ),
    )
    key_allowed = visible_mask(starts, every_pos, query_pos)

    def key_side(inputs):
        index, log_head, delta_head = inputs
        query_head = head_slice(query_every, index)
        grad_head = head_slice(grad_every, index)
        key_head = head_slice(keys, index)
        value_head = head_slice(values, index)
        scores = scale * jnp.einsum(
            "sqe,ske->sqk", query_head, key_head, preferred_element_type=jnp.float32
        )
        scores = jnp.where(key_allowed, scores, -1e30)
        probs = jnp.exp(scores - log_head[..., None])
        grad_probs = jnp.einsum(
            "sqe,ske->sqk", grad_head, value_head, preferred_element_type=jnp.float32
        )
        grad_scores = (probs * (grad_probs - delta_head[..., None])).astype(jnp.bfloat16)
        grad_key_head = scale * jnp.einsum(
            "sqk,sqe->ske", grad_scores, query_head, preferred_element_type=jnp.float32
        )
        grad_value_head = jnp.einsum(
            "sqk,sqe->ske",
            probs.astype(jnp.bfloat16),
            grad_head,
            preferred_element_type=jnp.float32,
        )
        return (grad_key_head, grad_value_head)

    grad_key_heads, grad_value_heads = lax.map(
        key_side, (jnp.arange(HEADS, dtype=jnp.int32), log_every, delta_every)
    )
    grad_key_own = merge_heads(grad_key_heads)
    grad_value_own = merge_heads(grad_value_heads)
    grad_query_low = merge_heads(grad_query_heads).astype(jnp.bfloat16).reshape(flat_rows, D)
    grad_key_low = grad_key_own.astype(jnp.bfloat16).reshape(flat_rows, D)
    grad_value_low = grad_value_own.astype(jnp.bfloat16).reshape(flat_rows, D)
    grad_joined = jnp.concatenate([grad_query_low, grad_key_low, grad_value_low], axis=1)
    grad_qkv = dense_left(normed_one, grad_joined)
    grad_query_shift = jnp.sum(grad_query_low.astype(jnp.float32), axis=0)
    grad_value_shift = jnp.sum(grad_value_low.astype(jnp.float32), axis=0)
    grad_norm_one = dense_right(grad_joined, qkv_back)
    grad_start_norm, grad_gain_one, grad_shift_one = pull_one(grad_norm_one)
    grad_start = grad_mid + grad_start_norm
    grad_tokens = grad_start.astype(jnp.bfloat16).reshape(seq_count, row_count, D)
    seq_sums = jnp.sum(grad_start.reshape(seq_count, row_count, D), axis=1)
    every_sums, every_times = (
        lax.all_gather(seq_sums, ("seq", "dp"), axis=0, tiled=True),
        lax.all_gather(timesteps, ("seq", "dp"), axis=0, tiled=True),
    )
    own_width = D // lax.axis_size(("seq", "dp"))
    own_sums = lax.dynamic_slice_in_dim(
        every_sums, lax.axis_index(("seq", "dp")) * own_width, own_width, 1
    )
    every_onehot = (every_times[None, :] == levels[:, None]).astype(jnp.float32)
    grad_table = jnp.dot(every_onehot, own_sums, precision=lax.Precision.HIGHEST)
    summed = (
        lax.psum_scatter(grad_gain_one, ("seq", "dp"), scatter_dimension=0, tiled=True),
        lax.psum_scatter(grad_shift_one, ("seq", "dp"), scatter_dimension=0, tiled=True),
        lax.psum_scatter(grad_qkv, ("seq", "dp"), scatter_dimension=0, tiled=True),
        lax.psum_scatter(grad_query_shift, ("seq", "dp"), scatter_dimension=0, tiled=True),
        lax.psum_scatter(grad_value_shift, ("seq", "dp"), scatter_dimension=0, tiled=True),
        lax.psum_scatter(grad_out_w, ("seq", "dp"), scatter_dimension=0, tiled=True),
        lax.psum_scatter(grad_out_shift, ("seq", "dp"), scatter_dimension=0, tiled=True),
        lax.psum_scatter(grad_gain_two, ("seq", "dp"), scatter_dimension=0, tiled=True),
        lax.psum_scatter(grad_shift_two, ("seq", "dp"), scatter_dimension=0, tiled=True),
        lax.psum_scatter(grad_up, ("seq", "dp"), scatter_dimension=0, tiled=True),
        lax.psum_scatter(grad_up_shift, ("seq", "dp"), scatter_dimension=0, tiled=True),
        lax.psum_scatter(grad_down, ("seq", "dp"), scatter_dimension=0, tiled=True),
        lax.psum_scatter(grad_down_shift, ("seq", "dp"), scatter_dimension=0, tiled=True),
    )
    return (
        block_out.reshape(seq_count, row_count, D),
        grad_tokens,
        summed[0],
        summed[1],
        summed[2],
        summed[3],
        summed[4],
        summed[5],
        summed[6],
        summed[7],
        summed[8],
        summed[9],
        summed[10],
        summed[11],
        summed[12],
        grad_table,
    )


AXES = ("seq", "dp")
CORE, Y, Z0, Z1, X = 1, 2, 4, 8, 16
DEVICES = 32
QUARTER = 256
ROWS = 512
FF = 3072
TILE = 768
WIDE = 384
MIB = 2**20
F32 = jnp.float32
LOW = jnp.bfloat16

Z_MASKS = (0, Z0, Z1, Z0 | Z1)
X_LAST = tuple((xy | z) >> 1 for xy in (0, Y, X, X | Y) for z in Z_MASKS)
Y_LAST = tuple((xy | z) >> 1 for xy in (0, X, Y, X | Y) for z in Z_MASKS)


def send(array, pairs):
    return lax.ppermute(array, AXES, pairs)


def trade(array, mask):
    return send(array, [(i, i ^ mask) for i in range(DEVICES)])


def exchange(array):
    return lax.all_to_all(array, AXES, 0, 0, tiled=True)


def join(bit, own, other, axis):
    return jnp.where(
        bit == 0,
        jnp.concatenate([own, other], axis=axis),
        jnp.concatenate([other, own], axis=axis),
    )


def spot():
    x = lax.axis_index("seq")
    dp = lax.axis_index("dp")
    return x, dp >> 2, (dp >> 1) & 1, dp & 1


def hop_pairs(first):
    pairs = []
    for base in range(0, 16, 2):
        if first:
            moves = (((0, 0), (0, 1)), ((0, 1), (1, 0)), ((1, 0), (0, 0)))
        else:
            moves = (((1, 0), (0, 1)), ((1, 1), (1, 0)), ((0, 1), (1, 1)))
        for (sx, sc), (tx, tc) in moves:
            pairs.append((sx * 16 + base + sc, tx * 16 + base + tc))
    return pairs


def corners():
    x, _, _, core = spot()
    return (x == 0) & (core == 0), (x == 1) & (core == 1)


def swap_in(array):
    first, last = corners()
    front, back = array[:QUARTER], array[QUARTER:]
    one = send(jnp.where(first, back, front), hop_pairs(True))
    two = send(jnp.where(last, front, back), hop_pairs(False))
    low = jnp.where(first, front, jnp.where(last, two, one))
    high = jnp.where(first, one, jnp.where(last, back, two))
    return jnp.concatenate([low, high], axis=0)


def swap_out(array):
    first, last = corners()
    low, high = array[:QUARTER], array[QUARTER:]
    back_pairs = lambda which: [(t, s) for s, t in hop_pairs(which)]
    one = send(jnp.where(first, high, low), back_pairs(True))
    two = send(jnp.where(last, low, high), back_pairs(False))
    front = jnp.where(first, low, jnp.where(last, two, one))
    back = jnp.where(first, one, jnp.where(last, high, two))
    return jnp.concatenate([front, back], axis=0)


def gather_z(block):
    got = [trade(block, mask) for mask in Z_MASKS[1:]]
    return jnp.stack([block] + got, axis=0)


def gather_z_two(block):
    return grow(grow(block[None], Z0), Z1)


def grow(blocks, mask):
    return jnp.concatenate([blocks, trade(blocks, mask)], axis=0)


def gather_direct(blocks):
    got = [trade(blocks, m) for m in (Y, X, X | Y)]
    return jnp.concatenate([blocks] + got, axis=0)


def add_low(left, right):
    return (left.astype(F32) + right.astype(F32)).astype(LOW)


def scatter_two(keep, got, x_first):
    n = keep.shape[-1]
    cube = lambda array: array.reshape(2, 4, 2, -1, n)
    keep, got = cube(keep), cube(got)
    if x_first:
        away = trade(add_low(keep[1], got[1]), X)
        half = add_low(add_low(keep[0], got[0]), away)
        return add_low(half[:, 0], trade(half[:, 1], Y))
    away = trade(add_low(keep[:, :, 1], got[:, :, 1]), Y)
    half = add_low(add_low(keep[:, :, 0], got[:, :, 0]), away)
    return add_low(half[0], trade(half[1], X))


def scatter_direct(keep, got):
    n = keep.shape[-1]
    cube = lambda array: array.reshape(2, 4, 2, -1, n)
    keep, got = cube(keep), cube(got)
    total = keep[0, :, 0].astype(F32) + got[0, :, 0].astype(F32)
    for mask, a, b in ((Y, 0, 1), (X, 1, 0), (X | Y, 1, 1)):
        away = trade(add_low(keep[a, :, b], got[a, :, b]), mask)
        total = total + away.astype(F32)
    return total.astype(LOW)


def scatter_z(fours):
    total = fours[0].astype(F32)
    for place, mask in enumerate(Z_MASKS[1:], 1):
        total = total + trade(fours[place], mask).astype(F32)
    return total


def scatter_z_two(fours):
    half = add_low(fours[:2], trade(fours[2:], Z1))
    return half[0].astype(F32) + trade(half[1], Z0).astype(F32)


def settle(block, core):
    keep = lax.dynamic_slice_in_dim(block, core * 24, 24, 0)
    away = lax.dynamic_slice_in_dim(block, (1 - core) * 24, 24, 0)
    return keep, trade(away, CORE)


def dot_nt(left, right):
    return lax.dot_general(
        left, right, (((1,), (1,)), ((), ())), preferred_element_type=F32
    )


def dot_nn(left, right):
    return lax.dot_general(
        left, right, (((1,), (0,)), ((), ())), preferred_element_type=F32
    )


def inside_piece(place, start):
    return (place >= start) & (place < start + PIC)


def fill_bias(scalars, low_bias, high_bias):
    core, first, second = scalars[1], scalars[3], scalars[4]

    def fill(ref, chunk, key_start, query_start):
        shape = (QUARTER, QUARTER)
        key = key_start + lax.broadcasted_iota(jnp.int32, shape, 0)
        query = query_start + lax.broadcasted_iota(jnp.int32, shape, 1)
        seen = (
            (key <= query)
            | (inside_piece(key, first) & inside_piece(query, first))
            | (inside_piece(key, second) & inside_piece(query, second))
        )
        ref[pl.ds(chunk * QUARTER, QUARTER), :] = jnp.where(seen, 0.0, -1e30)

    mine, theirs = core * QUARTER, (1 - core) * QUARTER
    fill(low_bias, 0, mine, mine)
    fill(low_bias, 1, theirs, mine)
    half = 2 * QUARTER
    fill(high_bias, 0, mine, half + mine)
    fill(high_bias, 1, half + mine, half + mine)
    fill(high_bias, 2, theirs, half + mine)
    fill(high_bias, 3, half + theirs, half + mine)


def head_lanes(array, head):
    lane = lax.broadcasted_iota(jnp.int32, array.shape, 1)
    return jnp.where((lane >= HD) == (head == 1), array, jnp.zeros_like(array))


def key_sets(own, other):
    high = jnp.concatenate([own[...], other[...]], axis=0)
    low = jnp.concatenate([own[:QUARTER], other[:QUARTER]], axis=0)
    return low, high


def forward_kernel(scalars, q, k_own, k_other, v_own, v_other, out, lse, low_bias, high_bias):
    @pl.when(pl.program_id(0) == 0)
    def _():
        fill_bias(scalars, low_bias, high_bias)

    scale = HD ** (-0.5)
    keys, values = key_sets(k_own, k_other), key_sets(v_own, v_other)
    for part, bias in enumerate((low_bias, high_bias)):
        key, value_t = keys[part], values[part].T
        rows = pl.ds(part * QUARTER, QUARTER)
        query = q[rows, :] * jnp.bfloat16(scale)
        tops = []
        for head in range(2):
            scores = dot_nt(key, head_lanes(query, head)) + bias[...]
            top = jnp.max(scores, axis=0, keepdims=True)
            expo = jnp.exp(scores - top)
            total = jnp.sum(expo, axis=0, keepdims=True)
            mixed = dot_nn(value_t[head * HD : (head + 1) * HD], expo.astype(LOW))
            tops.append(mixed / total)
            lse[0, pl.ds(head, 1), rows] = top + jnp.log(total)
        both = jnp.concatenate(tops, axis=0)
        out[rows, :] = both.T.astype(LOW)


def backward_kernel(
    scalars, q, grad, lse, k_own, k_other, v_own, v_other,
    dq, own, other, low_bias, high_bias,
):
    @pl.when(pl.program_id(0) == 0)
    def _():
        fill_bias(scalars, low_bias, high_bias)

    scale = HD ** (-0.5)
    keys, values = key_sets(k_own, k_other), key_sets(v_own, v_other)
    sums = []
    for part, bias in enumerate((low_bias, high_bias)):
        key, value = keys[part], values[part]
        key_t = key.T
        rows = pl.ds(part * QUARTER, QUARTER)
        query = q[rows, :] * jnp.bfloat16(scale)
        grad_out = grad[rows, :]
        grad_query, grad_key, grad_value = [], 0.0, 0.0
        for head in range(2):
            query_head = head_lanes(query, head)
            grad_head = head_lanes(grad_out, head)
            scores = dot_nt(key, query_head) + bias[...]
            probs = jnp.exp(scores - lse[0, pl.ds(head, 1), rows])
            grad_probs = dot_nt(value, grad_head)
            delta = jnp.sum(probs * grad_probs, axis=0, keepdims=True)
            grad_scores = (probs * (grad_probs - delta)).astype(LOW)
            grad_value += dot_nn(probs.astype(LOW), grad_head)
            grad_key += dot_nn(grad_scores, query_head)
            grad_query.append(
                dot_nn(key_t[head * HD : (head + 1) * HD], grad_scores) * scale
            )
        dq[rows, :] = jnp.concatenate(grad_query, axis=0).T.astype(LOW)
        sums.append((grad_key, grad_value))
    for which in range(2):
        low, high = sums[0][which], sums[1][which]
        own[which, :QUARTER] = (low[:QUARTER] + high[:QUARTER]).astype(LOW)
        own[which, QUARTER:] = high[QUARTER : 2 * QUARTER].astype(LOW)
        other[which, :QUARTER] = (low[QUARTER:] + high[2 * QUARTER : 3 * QUARTER]).astype(LOW)
        other[which, QUARTER:] = high[3 * QUARTER :].astype(LOW)


PAIRS = HEADS // 2


PART = 2


def pair_block(skip=0):
    return pl.BlockSpec((ROWS, 2 * HD), lambda i, s: (0, i + skip))


def lse_block():
    return pl.BlockSpec((1, 2, ROWS), lambda i, s: (i, 0, 0))


def bias_scratch():
    return [
        pltpu.VMEM((2 * QUARTER, QUARTER), F32),
        pltpu.VMEM((4 * QUARTER, QUARTER), F32),
    ]


def cost(flops, size):
    return pl.CostEstimate(flops=flops, bytes_accessed=size, transcendentals=0)


def array(shape, dtype=LOW):
    return jax.ShapeDtypeStruct(shape, dtype)


def attend(scalars, q, kv, kv_other, part):
    skip = part * PART
    block = pair_block(skip)
    value = pair_block(skip + PAIRS)
    return pl.pallas_call(
        forward_kernel,
        grid_spec=pltpu.PrefetchScalarGridSpec(
            num_scalar_prefetch=1,
            grid=(PART,),
            in_specs=[block, block, block, value, value],
            out_specs=[pair_block(), lse_block()],
            scratch_shapes=bias_scratch(),
        ),
        out_shape=[array((ROWS, PART * 2 * HD)), array((PART, 2, ROWS), F32)],
        cost_estimate=cost(10**9, 2 * 10**6),
        compiler_params=pltpu.CompilerParams(vmem_limit_bytes=16 * MIB),
    )(scalars, q, kv, kv_other, kv, kv_other)


def attend_back(scalars, q, grad, lse, kv, kv_other):
    both = pl.BlockSpec((2, ROWS, 2 * HD), lambda i, s: (0, 0, i))
    return pl.pallas_call(
        backward_kernel,
        grid_spec=pltpu.PrefetchScalarGridSpec(
            num_scalar_prefetch=1,
            grid=(PAIRS,),
            in_specs=[pair_block()] * 2
            + [lse_block(), pair_block(), pair_block(), pair_block(PAIRS), pair_block(PAIRS)],
            out_specs=[pair_block(), both, both],
            scratch_shapes=bias_scratch(),
        ),
        out_shape=[array((ROWS, D)), array((2, ROWS, D)), array((2, ROWS, D))],
        cost_estimate=cost(2 * 10**10, 8 * 10**6),
        compiler_params=pltpu.CompilerParams(vmem_limit_bytes=18 * MIB),
        name="attend_back",
    )(scalars, q, grad, lse, kv, kv_other, kv, kv_other)


def fetch(jobs, sems):
    copies = [pltpu.make_async_copy(s, d, sems.at[i]) for i, (s, d) in enumerate(jobs)]
    for copy in copies:
        copy.start()
    return copies


def wait(copies):
    for copy in copies:
        copy.wait()


def column_jobs(scalars, source, other, target, masks, start, width, half, skip=0):
    chip, core = scalars[0], scalars[1]
    jobs = []
    for blocks, side in ((source, core), (other, 1 - core)):
        columns = pl.ds(pl.multiple_of(side * half + skip, 128), width)
        for j, mask in enumerate(masks):
            rows = pl.ds(pl.multiple_of((chip ^ mask) * 48, 16), 48)
            jobs.append((blocks.at[j, :, pl.ds(start, width)], target.at[rows, columns]))
    return jobs


UP_A = 1024


def up_jobs(scalars, pieces, w_up, w_out):
    a, b, a2, b2 = pieces
    jobs = column_jobs(scalars, b, b2, w_out, Y_LAST, 1536 - UP_A, 384, 384)
    jobs += column_jobs(scalars, a, a2, w_up, X_LAST, 0, UP_A, 1536)
    return jobs + column_jobs(scalars, b, b2, w_up, Y_LAST, 0, 1536 - UP_A, 1536, UP_A)


def down_jobs(scalars, pieces, target):
    chip, core = scalars[0], scalars[1]
    a, b, a2, b2 = pieces
    jobs = []
    for blocks, side, masks, half in (
        (a, core, X_LAST, 0), (b, core, Y_LAST, 1), (a2, 1 - core, X_LAST, 0), (b2, 1 - core, Y_LAST, 1)
    ):
        for j, mask in enumerate(masks):
            first = pl.multiple_of((chip ^ mask) * 192 + side * 96, 16)
            jobs.append((blocks.at[j], target.at[pl.ds(first, 96), pl.ds(half * 384, 384)]))
    return jobs


CHUNK = 128


def by_rows(body):
    @pl.loop(0, ROWS // CHUNK)
    def _(step):
        body(pl.ds(pl.multiple_of(step * CHUNK, CHUNK), CHUNK))


def norm_parts(values):
    average = jnp.mean(values, axis=-1, keepdims=True)
    centred = values - average
    rate = lax.rsqrt(jnp.mean(centred * centred, axis=-1, keepdims=True) + epsilon)
    return centred * rate, rate


def norm_back(grad, normal, rate, gain):
    scaled = grad * gain
    return rate * (
        scaled
        - jnp.mean(scaled, axis=-1, keepdims=True)
        - normal * jnp.mean(scaled * normal, axis=-1, keepdims=True)
    )


def full(shape):
    return pl.BlockSpec(shape, lambda i, s: (0,) * len(shape))


def anywhere():
    return pl.BlockSpec(memory_space=pl.ANY)


def spread(shape):
    column = lax.broadcasted_iota(jnp.int32, shape, len(shape) - 1)
    return column, column - column // 24 * 24


def project_kernel(scalars, tok, owned, blocks, other, vec, normed, q, kv, weight, sems):
    step = pl.program_id(0)

    @pl.when(step == 0)
    def _():
        copies = fetch(column_jobs(scalars, blocks, other, weight, X_LAST, 0, 1152, 1152), sems)
        _, inner = spread((24, D))
        place = (inner == lax.broadcasted_iota(jnp.int32, (24, D), 0)).astype(LOW)
        wide = dot_nn(owned[...].reshape(DEVICES * 16, 24), place).reshape(DEVICES, 16, D)
        column, _ = spread((DEVICES, 16, D))
        mine = column // 24 == lax.broadcasted_iota(jnp.int32, (DEVICES, 16, D), 0)
        vec[...] = jnp.sum(jnp.where(mine, wide, 0.0), axis=0)

        def rows_of(rows):
            normal, _ = norm_parts(tok[rows, :].astype(F32) + vec[12:13, :])
            normed[rows, :] = (normal * vec[0:1, :] + vec[1:2, :]).astype(LOW)

        by_rows(rows_of)
        wait(copies)

    columns = pl.ds(pl.multiple_of(step * D, D), D)
    result = dot_nn(normed[...], weight[:, columns])

    @pl.when(step < 1)
    def _():
        q[...] = (result + vec[2:3, :]).astype(LOW)

    @pl.when(step == 1)
    def _():
        kv[...] = result.astype(LOW)

    @pl.when(step == 2)
    def _():
        kv[...] = (result + vec[3:4, :]).astype(LOW)


def project(scalars, tok, owned, blocks, other):
    return pl.pallas_call(
        project_kernel,
        grid_spec=pltpu.PrefetchScalarGridSpec(
            num_scalar_prefetch=1,
            grid=(3,),
            in_specs=[full((ROWS, D)), full((DEVICES, 16, 24)), anywhere(), anywhere()],
            out_specs=[
                full((16, D)),
                full((ROWS, D)),
                full((ROWS, D)),
                pl.BlockSpec((ROWS, D), lambda i, s: (0, jnp.maximum(i - 1, 0))),
            ],
            scratch_shapes=[pltpu.VMEM((D, 3 * D), LOW), pltpu.SemaphoreType.DMA((32,))],
        ),
        out_shape=[array((16, D), F32), array((ROWS, D)), array((ROWS, D)), array((ROWS, 2 * D))],
        cost_estimate=cost(2 * 10**9, 8 * 10**6),
        compiler_params=pltpu.CompilerParams(vmem_limit_bytes=18 * MIB),
        name="project",
    )(scalars, tok, owned, blocks, other)


GELU = 0.7978845608028654


def mlp_up_kernel(
    scalars, heads, tok, vec, up_bias, a, b, a2, b2, mid, normed, act, slope,
    w_up, w_out, sems,
):
    step = pl.program_id(0)

    @pl.when(step == 0)
    def _():
        copies = fetch(up_jobs(scalars, (a, b, a2, b2), w_up, w_out), sems)
        wait(copies[:32])
        mid[...] = dot_nn(heads[...], w_out[...])

        def rows_of(rows):
            total = tok[rows, :].astype(F32) + vec[12:13, :] + mid[rows, :] + vec[4:5, :]
            mid[rows, :] = total
            normal, _ = norm_parts(total)
            normed[rows, :] = (normal * vec[5:6, :] + vec[6:7, :]).astype(LOW)

        by_rows(rows_of)
        wait(copies[32:])

    columns = pl.ds(pl.multiple_of(step * TILE, TILE), TILE)
    v = dot_nn(normed[...], w_up[:, columns]) + up_bias[...]
    square = v * v
    inner = jnp.tanh(GELU * v * (1 + 0.044715 * square))
    half = 0.5 * (1 + inner)
    act[...] = (v * half).astype(LOW)
    slope[...] = (
        half + 0.5 * GELU * v * (1 - inner * inner) * (1 + 3 * 0.044715 * square)
    ).astype(LOW)


def mlp_up(scalars, heads, tok, vec, up_bias, pieces):
    tile = pl.BlockSpec((ROWS, TILE), lambda i, s: (0, i))
    return pl.pallas_call(
        mlp_up_kernel,
        grid_spec=pltpu.PrefetchScalarGridSpec(
            num_scalar_prefetch=1,
            grid=(FF // TILE,),
            in_specs=[
                full((ROWS, D)), full((ROWS, D)), full((16, D)),
                pl.BlockSpec((1, TILE), lambda i, s: (0, i)),
            ] + [anywhere()] * 4,
            out_specs=[full((ROWS, D)), full((ROWS, D)), tile, tile],
            scratch_shapes=[
                pltpu.VMEM((D, FF), LOW), pltpu.VMEM((D, D), LOW), pltpu.SemaphoreType.DMA((96,)),
            ],
        ),
        out_shape=[array((ROWS, D), F32), array((ROWS, D)), array((ROWS, FF)), array((ROWS, FF))],
        cost_estimate=cost(4 * 10**9, 16 * 10**6),
        compiler_params=pltpu.CompilerParams(vmem_limit_bytes=24 * MIB),
        name="mlp_up",
    )(scalars, heads, tok, vec, up_bias, *pieces)


def down_grad_kernel(scalars, act, cot, send, keep):
    chip, core = scalars[0], scalars[1]
    result = lax.dot_general(
        act[...], cot[...], (((0,), (0,)), ((), ())), preferred_element_type=F32
    )
    for index in range(2):
        place = (pl.program_id(0) * 2 + index) ^ chip
        rows = pl.ds(pl.multiple_of(place * 96, 16), 96)
        first = result[index * 192 : index * 192 + 96].astype(LOW)
        second = result[index * 192 + 96 : index * 192 + 192].astype(LOW)
        keep[rows, :] = jnp.where(core == 0, first, second)
        send[rows, :] = jnp.where(core == 0, second, first)


def down_grad(scalars, act, cot):
    return pl.pallas_call(
        down_grad_kernel,
        grid_spec=pltpu.PrefetchScalarGridSpec(
            num_scalar_prefetch=1,
            grid=(8,),
            in_specs=[pl.BlockSpec((ROWS, WIDE), lambda i, s: (0, i)), full((ROWS, D))],
            out_specs=[full((FF // 2, D))] * 2,
        ),
        out_shape=[array((FF // 2, D))] * 2,
        cost_estimate=cost(3 * 10**9, 9 * 10**6),
        compiler_params=pltpu.CompilerParams(vmem_limit_bytes=16 * MIB),
        name="down_grad",
    )(scalars, act, cot)


TILES = FF // TILE


def mlp_mid_kernel(
    scalars, act, slope, mid, cot, vec, da, db, da2, db2, ua, ub, ua2, ub2,
    out, grad_up, bias_sum, grad_mid, grad_attn, grad_heads, sums,
    w_down, w_up, w_out, held, total, down_sems, up_sems,
):
    step = pl.program_id(0)
    down = lambda: [
        pltpu.make_async_copy(s, d, down_sems.at[i])
        for i, (s, d) in enumerate(down_jobs(scalars, (da, db, da2, db2), w_down))
    ]
    up = lambda: [
        pltpu.make_async_copy(s, d, up_sems.at[i])
        for i, (s, d) in enumerate(up_jobs(scalars, (ua, ub, ua2, ub2), w_up, w_out))
    ]

    @pl.when(step == 0)
    def _():
        copies = down()
        for copy in copies + up():
            copy.start()
        total[...] = mid[...] + vec[7:8, :]
        wait(copies)

    @pl.when(step < TILES)
    def _():
        rows = pl.ds(pl.multiple_of(step * TILE, TILE), TILE)
        part = w_down[rows, :]
        total[...] += dot_nn(act[...], part)
        grad = (dot_nt(cot[...], part) * slope[...].astype(F32)).astype(LOW)
        grad_up[...] = grad
        held[step] = grad
        bias_sum[...] = jnp.sum(grad.astype(F32), axis=0, keepdims=True)

    @pl.when(step == TILES)
    def _():
        out[...] = total[...].astype(LOW)
        total[...] = jnp.zeros_like(total)
        wait(up())

    @pl.when(step >= TILES)
    def _():
        local = step - TILES
        columns = pl.ds(pl.multiple_of(local * TILE, TILE), TILE)
        total[...] += dot_nt(held[local], w_up[:, columns])

    @pl.when(step == 2 * TILES - 1)
    def _():
        sums[...] = jnp.zeros_like(sums)

        def rows_of(rows):
            normal, rate = norm_parts(mid[rows, :])
            grad = total[rows, :]
            outer = cot[rows, :].astype(F32)
            back = outer + norm_back(grad, normal, rate, vec[5:6, :])
            grad_mid[rows, :] = back
            low = back.astype(LOW)
            grad_attn[rows, :] = low
            sums[0:1, :] += jnp.sum(grad * normal, axis=0, keepdims=True)
            sums[1:2, :] += jnp.sum(grad, axis=0, keepdims=True)
            sums[2:3, :] += jnp.sum(low.astype(F32), axis=0, keepdims=True)
            sums[3:4, :] += jnp.sum(outer, axis=0, keepdims=True)

        by_rows(rows_of)
        grad_heads[...] = dot_nt(grad_attn[...], w_out[...]).astype(LOW)


def mlp_mid(scalars, act, slope, mid, cot, vec, down_pieces, up_pieces):
    index = lambda i, s: (0, jnp.minimum(i, TILES - 1))
    tile = pl.BlockSpec((ROWS, TILE), index)
    return pl.pallas_call(
        mlp_mid_kernel,
        grid_spec=pltpu.PrefetchScalarGridSpec(
            num_scalar_prefetch=1,
            grid=(2 * TILES,),
            in_specs=[tile, tile, full((ROWS, D)), full((ROWS, D)), full((16, D))]
            + [anywhere()] * 8,
            out_specs=[full((ROWS, D)), tile, pl.BlockSpec((1, TILE), index)]
            + [full((ROWS, D))] * 3
            + [full((8, D))],
            scratch_shapes=[
                pltpu.VMEM((FF, D), LOW), pltpu.VMEM((D, FF), LOW), pltpu.VMEM((D, D), LOW),
                pltpu.VMEM((TILES, ROWS, TILE), LOW), pltpu.VMEM((ROWS, D), F32),
                pltpu.SemaphoreType.DMA((64,)), pltpu.SemaphoreType.DMA((96,)),
            ],
        ),
        out_shape=[
            array((ROWS, D)), array((ROWS, FF)), array((1, FF), F32), array((ROWS, D), F32),
            array((ROWS, D)), array((ROWS, D)), array((8, D), F32),
        ],
        cost_estimate=cost(10**10, 30 * 10**6),
        compiler_params=pltpu.CompilerParams(vmem_limit_bytes=38 * MIB),
        name="mlp_mid",
    )(scalars, act, slope, mid, cot, vec, *down_pieces, *up_pieces)


def place_rows(result, target, chip):
    for index in range(16):
        rows = pl.ds(pl.multiple_of((index ^ chip) * 48, 16), 48)
        target[rows, :] = result[index * 48 : index * 48 + 48].astype(LOW)


def weight_grad_kernel(tiles, lefts, scalars, *refs):
    left_refs, right_refs = refs[: len(lefts)], refs[len(lefts) : 2 * len(lefts)]
    send, keep = refs[2 * len(lefts) : 2 * len(lefts) + 2]
    flipped = refs[2 * len(lefts) + 2 :]
    step = pl.program_id(0)
    chip = scalars[0]

    @pl.when(step == 0)
    def _():
        for left, flip in zip(left_refs, flipped):
            flip[...] = left[...].T

    local = jnp.where(step < tiles, step, step - tiles)
    for which, (first, last) in enumerate(lefts):

        @pl.when((local >= first) & (local < last))
        def _(which=which):
            result = dot_nn(flipped[which][...], right_refs[which][...])

            @pl.when(step < tiles)
            def _():
                place_rows(result, send, chip)

            @pl.when(step >= tiles)
            def _():
                place_rows(result, keep, chip)


def weight_grad(scalars, tiles, parts):
    def right_block(first, count):
        def index(i, s):
            local = jnp.clip(jnp.where(i < tiles, i, i - tiles) - first, 0, count - 1)
            side = jnp.where(i < tiles, 1 - s[1], s[1])
            return (0, side * count + local)

        return pl.BlockSpec((ROWS, WIDE), index)

    lefts = tuple((first, first + count) for _, _, first, count in parts)
    return pl.pallas_call(
        lambda *refs: weight_grad_kernel(tiles, lefts, *refs),
        grid_spec=pltpu.PrefetchScalarGridSpec(
            num_scalar_prefetch=1,
            grid=(2 * tiles,),
            in_specs=[full((ROWS, D))] * len(parts)
            + [right_block(first, count) for _, _, first, count in parts],
            out_specs=[
                pl.BlockSpec((D, WIDE), lambda i, s: (0, jnp.minimum(i, tiles - 1))),
                pl.BlockSpec((D, WIDE), lambda i, s: (0, jnp.maximum(i - tiles, 0))),
            ],
            scratch_shapes=[pltpu.VMEM((D, ROWS), LOW)] * len(parts),
        ),
        out_shape=[array((D, tiles * WIDE))] * 2,
        cost_estimate=cost(tiles * 6 * 10**8, 10 * 10**6),
        compiler_params=pltpu.CompilerParams(vmem_limit_bytes=18 * MIB),
    )(scalars, *[p[0] for p in parts], *[p[1] for p in parts])


def project_back_kernel(
    scalars, joined, tok, grad_mid, vec, mid_sums, up_sums, blocks, other, out, payload,
    weight, total, sums, column_sums, sems,
):
    step = pl.program_id(0)

    @pl.when(step == 0)
    def _():
        copies = fetch(column_jobs(scalars, blocks, other, weight, X_LAST, 0, 1152, 1152), sems)
        total[...] = jnp.zeros_like(total)
        wait(copies)

    columns = pl.ds(pl.multiple_of(step * D, D), D)
    total[...] += dot_nt(joined[...], weight[:, columns])
    column_sums[:, columns] = jnp.sum(joined[...].astype(F32), axis=0, keepdims=True)

    @pl.when(step == 2)
    def _():
        sums[...] = jnp.zeros_like(sums)

        def rows_of(rows):
            normal, rate = norm_parts(tok[rows, :].astype(F32) + vec[12:13, :])
            grad = total[rows, :]
            back = grad_mid[rows, :] + norm_back(grad, normal, rate, vec[0:1, :])
            out[rows, :] = back.astype(LOW)
            sums[0:1, :] += jnp.sum(grad * normal, axis=0, keepdims=True)
            sums[1:2, :] += jnp.sum(grad, axis=0, keepdims=True)
            sums[12:13, :] += jnp.sum(back, axis=0, keepdims=True)

        by_rows(rows_of)
        sums[2:3, :] = column_sums[:, :D]
        sums[3:4, :] = column_sums[:, 2 * D :]
        sums[4:5, :] = mid_sums[2:3, :]
        sums[5:7, :] = mid_sums[0:2, :]
        sums[7:8, :] = mid_sums[3:4, :]
        _, inner = spread((24, D))
        place = (inner == lax.broadcasted_iota(jnp.int32, (24, D), 0)).astype(F32)
        column, _ = spread((DEVICES, 16, D))
        mine = column // 24 == lax.broadcasted_iota(jnp.int32, (DEVICES, 16, D), 0)
        wide = jnp.where(mine, sums[...][None], 0.0).reshape(DEVICES * 16, D)
        narrow = lax.dot_general(
            wide, place, (((1,), (1,)), ((), ())),
            precision=lax.Precision.HIGHEST, preferred_element_type=F32,
        )
        payload[...] = narrow.reshape(DEVICES, 16, 24)
        payload[:, 8:12, :] = up_sums[...]


def project_back(scalars, joined, tok, grad_mid, vec, mid_sums, up_sums, blocks, other):
    return pl.pallas_call(
        project_back_kernel,
        grid_spec=pltpu.PrefetchScalarGridSpec(
            num_scalar_prefetch=1,
            grid=(3,),
            in_specs=[
                pl.BlockSpec((ROWS, D), lambda i, s: (0, i)),
                full((ROWS, D)), full((ROWS, D)), full((16, D)), full((8, D)),
                full((DEVICES, 4, 24)), anywhere(), anywhere(),
            ],
            out_specs=[full((ROWS, D)), full((DEVICES, 16, 24))],
            scratch_shapes=[
                pltpu.VMEM((D, 3 * D), LOW), pltpu.VMEM((ROWS, D), F32), pltpu.VMEM((16, D), F32),
                pltpu.VMEM((1, 3 * D), F32), pltpu.SemaphoreType.DMA((32,)),
            ],
        ),
        out_shape=[array((ROWS, D)), array((DEVICES, 16, 24), F32)],
        cost_estimate=cost(3 * 10**9, 12 * 10**6),
        compiler_params=pltpu.CompilerParams(vmem_limit_bytes=26 * MIB),
        name="project_back",
    )(scalars, joined, tok, grad_mid, vec, mid_sums, up_sums, blocks, other)


def quick_shards(*arguments):
    return quick_step(*arguments)


def quick_step(
    tokens, timesteps, starts, cotangent, ln1_gain, ln1_bias, w_qkv, bias_query,
    bias_value, w_out, bias_out, ln2_gain, ln2_bias, w_up, bias_up, w_down,
    bias_down, time_table,
):
    x, z, y, core = spot()
    chip = x * 8 + z * 2 + y
    sequence = ((lax.axis_index("dp") >> 1) << 1) | x

    def chip_half(shard):
        rows = join(core, shard, trade(shard, CORE), 0)
        return lax.dynamic_slice_in_dim(rows, core * (shard.shape[1] // 2), shard.shape[1] // 2, 1)

    qkv_own = gather_direct(gather_z(chip_half(w_qkv)))
    qkv_other = trade(qkv_own, CORE)
    tokens_here = swap_in(tokens[0])
    rest = gather_z(jnp.concatenate([chip_half(w_up), chip_half(w_out)], axis=1))
    up_a = grow(grow(rest[:, :, :UP_A], Y), X)
    up_b = grow(grow(rest[:, :, UP_A:], X), Y)
    up_pieces = (up_a, up_b, trade(up_a, CORE), trade(up_b, CORE))
    cot = swap_in(cotangent[0])
    rest = gather_z_two(w_down)
    down_a = grow(grow(rest[:, :, :384], Y), X)
    down_b = grow(grow(rest[:, :, 384:], X), Y)
    down_pieces = (down_a, down_b, trade(down_a, CORE), trade(down_b, CORE))

    row = jnp.concatenate([timesteps, starts[0], jnp.zeros((5,), jnp.int32)])
    notes = exchange(jnp.broadcast_to(row, (DEVICES, 8)))
    times = jnp.broadcast_to(notes[:16, 0].reshape(8, 2).T[:, :, None], (2, 8, 2)).reshape(DEVICES)
    levels = jnp.arange(TSTEPS, dtype=jnp.int32)
    rows_of = dense((times[:, None] == levels[None, :]).astype(LOW), time_table).astype(LOW)
    vectors = (ln1_gain, ln1_bias, bias_query, bias_value, bias_out, ln2_gain, ln2_bias, bias_down)
    shared = jnp.concatenate(vectors + (bias_up,)).reshape(1, 12, 24)
    owned = jnp.concatenate(
        [jnp.broadcast_to(shared, (DEVICES, 12, 24)), rows_of[:, None], jnp.zeros((DEVICES, 3, 24), LOW)],
        axis=1,
    )
    owned = exchange(owned)
    up_bias = owned[:, 8:12].reshape(1, FF).astype(F32)
    own_starts = lax.dynamic_slice_in_dim(notes, sequence, 1, 0)[0, 1:3]
    scalars = jnp.concatenate([jnp.stack([chip, core, sequence]).astype(jnp.int32), own_starts])

    vec, normed_one, query, kv = project(scalars, tokens_here, owned, qkv_own, qkv_other)
    kv_other = trade(kv, CORE)
    parts = [attend(scalars, query, kv, kv_other, part) for part in range(PAIRS // PART)]
    heads_out = jnp.concatenate([part[0] for part in parts], axis=1)
    lse = jnp.concatenate([part[1] for part in parts], axis=0)
    mid, normed_two, act, slope = mlp_up(
        scalars, heads_out, tokens_here, vec, up_bias, up_pieces
    )

    away, keep = down_grad(scalars, act, cot)
    got = trade(away, CORE).reshape(16, 96, D)
    keep = keep.reshape(16, 96, D)
    fours = jnp.concatenate(
        [scatter_two(keep[:, :48], got[:, :48], True),
         scatter_two(keep[:, 48:], got[:, 48:], False)],
        axis=1,
    )
    grad_down = scatter_z_two(fours)

    out, grad_up_low, up_sums, grad_mid, grad_attn, grad_heads, mid_sums = mlp_mid(
        scalars, act, slope, mid, cot, vec, down_pieces, up_pieces
    )
    block_out = swap_out(out)
    away, keep = weight_grad(
        scalars, 5, ((normed_two, grad_up_low, 0, 4), (heads_out, grad_attn, 4, 1))
    )
    got = trade(away, CORE)
    fours = jnp.concatenate(
        [scatter_two(keep[:, :UP_A], got[:, :UP_A], True),
         scatter_two(keep[:, UP_A:], got[:, UP_A:], False)],
        axis=2,
    )
    keep, got = settle(scatter_z_two(fours), core)
    grad_up = join(core, keep[:, :1536], got[:, :1536], 1)
    grad_out_w = join(core, keep[:, 1536:], got[:, 1536:], 1)

    dq, own, other = attend_back(scalars, query, grad_heads, lse, kv, kv_other)
    both = add_low(own, trade(other, CORE))
    joined = jnp.concatenate([dq, both[0], both[1]], axis=1)
    away, keep = weight_grad(scalars, 3, ((normed_one, joined, 0, 3),))
    fours = scatter_direct(keep, trade(away, CORE))
    grad_qkv = join(core, *settle(scatter_z(fours), core), 1)
    grad_start, payload = project_back(
        scalars, joined, tokens_here, grad_mid, vec, mid_sums, up_sums.reshape(DEVICES, 4, 24),
        qkv_own, qkv_other,
    )
    grad_tokens = swap_out(grad_start)
    final = exchange(payload)
    summed = jnp.sum(final[:, :12], axis=0)
    hit = (times[None, :] == levels[:, None]).astype(F32)
    grad_table = jnp.dot(hit, final[:, 12], precision=lax.Precision.HIGHEST)
    return (
        block_out[None],
        grad_tokens[None],
        summed[0],
        summed[1],
        grad_qkv,
        summed[2],
        summed[3],
        grad_out_w,
        summed[4],
        summed[5],
        summed[6],
        grad_up,
        summed[8:].reshape(96),
        grad_down,
        summed[7],
        grad_table,
    )


def solution(mesh):
    quick = mesh.shape["seq"] == 2 and mesh.shape["dp"] == 16
    return jax.shard_map(
        quick_shards if quick else shards,
        mesh=mesh,
        in_specs=(
            P("dp", "seq", None),
            P("dp"),
            P("dp", None),
            P("dp", "seq", None),
            P(("seq", "dp")),
            P(("seq", "dp")),
            P(("seq", "dp"), None),
            P(("seq", "dp")),
            P(("seq", "dp")),
            P(("seq", "dp"), None),
            P(("seq", "dp")),
            P(("seq", "dp")),
            P(("seq", "dp")),
            P(("seq", "dp"), None),
            P(("seq", "dp")),
            P(("seq", "dp"), None),
            P(("seq", "dp")),
            P(None, ("seq", "dp")),
        ),
        out_specs=(
            P("dp", "seq", None),
            P("dp", "seq", None),
            P(("seq", "dp")),
            P(("seq", "dp")),
            P(("seq", "dp"), None),
            P(("seq", "dp")),
            P(("seq", "dp")),
            P(("seq", "dp"), None),
            P(("seq", "dp")),
            P(("seq", "dp")),
            P(("seq", "dp")),
            P(("seq", "dp"), None),
            P(("seq", "dp")),
            P(("seq", "dp"), None),
            P(("seq", "dp")),
            P(None, ("seq", "dp")),
        ),
        check_vma=False,
    )
```

profile of v0, /device:TPU:0, one launch (start us, length us, event | category | flops | bytes accessed | tf_op | source)
XLA Modules:
  0.0 404.4 jit_solution(11671966626349908410)
XLA Ops:
  2.8 7.3 %all-to-all-start = ((s32[32,1,8]{2,1,0:T(1,128)}), s32[32,1,8]{2,1,0:T(1,128)S(1)}, u32[]{:S(2)}, u32[]{:S(2)}) async-start(s32[32,1,8]{2,1,0:T(1,128)} %broadcast_in_dim.33), calls=%async_computation | async-start | bytes 32768 | tf_op jit(solution)/shard_map/all_to_all | solution.py:368
  24.5 9.8 %collective-permute-done.4 = bf16[48,1152]{1,0:T(8,128)(2,1)S(1)} collective-permute-done((bf16[48,1152]{1,0:T(8,128)(2,1)S(1)}, bf16[48,1152]{1,0:T(8,128)(2,1)S(1)}, u32[]{:S(2)}, u32[]{:S(2)}) %collective-permute-start.4) | collective-permute-done | bytes 110624 | tf_op jit(solution)/shard_map/ppermute | solution.py:360
  37.9 7.1 %collective-permute-done.6 = bf16[4,48,1152]{2,1,0:T(8,128)(2,1)S(1)} collective-permute-done((bf16[4,48,1152]{2,1,0:T(8,128)(2,1)S(1)}, bf16[4,48,1152]{2,1,0:T(8,128)(2,1)S(1)}, u32[]{:S(2)}, u32[]{:S(2)}) %collective-permute-start.6) | collective-permute-done | bytes 442400 | tf_op jit(solution)/shard_map/ppermute | solution.py:360
  51.0 10.8 %all-to-all-start.1 = ((bf16[32,2,192]{2,1,0:T(2,128)(2,1)}), bf16[32,2,192]{2,1,0:T(2,128)(2,1)S(1)}, u32[]{:S(2)}, u32[]{:S(2)}) async-start(bf16[32,2,192]{2,1,0:T(2,128)(2,1)} %reshape.212), calls=%async_computation.1 | async-start | bytes 65536 | tf_op jit(solution)/shard_map/all_to_all | solution.py:368
  84.9 6.3 %collective-permute-done.25 = bf16[2,96,768]{2,1,0:T(8,128)(2,1)S(1)} collective-permute-done((bf16[2,96,768]{2,1,0:T(8,128)(2,1)S(1)}, bf16[2,96,768]{2,1,0:T(8,128)(2,1)S(1)}, u32[]{:S(2)}, u32[]{:S(2)}) %collective-permute-start.25) | collective-permute-done | bytes 294944 | tf_op jit(solution)/shard_map/ppermute | solution.py:360
  96.7 5.8 %project.1 = (f32[16,768]{1,0:T(8,128)S(1)}, bf16[512,768]{1,0:T(8,128)(2,1)S(1)}, bf16[512,768]{1,0:T(8,128)(2,1)S(1)}, bf16[512,1536]{1,0:T(8,128)(2,1)S(1)}) custom-call(s32[5]{0:T(128)S(1)} %pad_add_fusion.1.scalars.refs_0_, bf16[512,768]{1,0:T(8,128)(2,1)S(1)} %pad_maximum_fusion.5.tok, bf16[32,16,24]{2,1,0:T(8,128)(2,1)S(1)} %reshape.213.owned, ...), custom_call_target="tpu_custom_call" | custom-call | flops 2000000000 | bytes 8000000 | tf_op jit(solution)/shard_map/project/pallas_call | solution.py:791
  109.9 15.1 %collective-permute-start.23 = (bf16[256,768]{1,0:T(8,128)(2,1)}, bf16[256,768]{1,0:T(8,128)(2,1)S(1)}, u32[]{:S(2)}, u32[]{:S(2)}) collective-permute-start(bf16[256,768]{1,0:T(8,128)(2,1)} %get-tuple-element.104), channel_id=1, source_target_pairs={{0,1},{1,16},{16,0},{2,3},{3,18},{18,2},{4,5},{5,20},{20,4},{6,7},... | collective-permute-start | bytes 1179656 | tf_op jit(solution)/shard_map/ppermute | solution.py:360
  133.7 9.1 %collective-permute-done.27 = bf16[8,96,384]{2,1,0:T(8,128)(2,1)S(1)} collective-permute-done((bf16[8,96,384]{2,1,0:T(8,128)(2,1)S(1)}, bf16[8,96,384]{2,1,0:T(8,128)(2,1)S(1)}, u32[]{:S(2)}, u32[]{:S(2)}) %collective-permute-start.27) | collective-permute-done | bytes 589856 | tf_op jit(solution)/shard_map/ppermute | solution.py:360
  145.8 6.6 %shard_map.297 = (bf16[512,256]{1,0:T(8,128)(2,1)S(1)}, f32[2,2,512]{2,1,0:T(2,128)S(1)}) custom-call(s32[5]{0:T(128)S(1)} %pad_add_fusion.1.scalars.refs_0_, bf16[512,768]{1,0:T(8,128)(2,1)S(1)} %copy-done.3, bf16[512,1536]{1,0:T(8,128)(2,1)S(1)} %get-tuple-element.49.k_own.v_own, bf16[512,1536]{1,0:T(8,128)(2,1)S(1)} %collective-permute-done.10.k_other.v_other, ...), custom_call_target="tpu_custom_call" | custom-call | flops 1000000000 | bytes 2000000 | tf_op jit(solution)/shard_map/pallas_call | solution.py:636
  152.4 6.6 %shard_map.298 = (bf16[512,256]{1,0:T(8,128)(2,1)S(1)}, f32[2,2,512]{2,1,0:T(2,128)S(1)}) custom-call(s32[5]{0:T(128)S(1)} %pad_add_fusion.1.scalars.refs_0_, bf16[512,768]{1,0:T(8,128)(2,1)S(1)} %copy-done.3, bf16[512,1536]{1,0:T(8,128)(2,1)S(1)} %get-tuple-element.49.k_own.v_own, bf16[512,1536]{1,0:T(8,128)(2,1)S(1)} %collective-permute-done.10.k_other.v_other, ...), custom_call_target="tpu_custom_call" | custom-call | flops 1000000000 | bytes 2000000 | tf_op jit(solution)/shard_map/pallas_call | solution.py:636
  159.0 6.6 %shard_map.299 = (bf16[512,256]{1,0:T(8,128)(2,1)S(1)}, f32[2,2,512]{2,1,0:T(2,128)S(1)}) custom-call(s32[5]{0:T(128)S(1)} %pad_add_fusion.1.scalars.refs_0_, bf16[512,768]{1,0:T(8,128)(2,1)S(1)} %copy-done.3, bf16[512,1536]{1,0:T(8,128)(2,1)S(1)} %get-tuple-element.49.k_own.v_own, bf16[512,1536]{1,0:T(8,128)(2,1)S(1)} %collective-permute-done.10.k_other.v_other, ...), custom_call_target="tpu_custom_call" | custom-call | flops 1000000000 | bytes 2000000 | tf_op jit(solution)/shard_map/pallas_call | solution.py:636
  167.0 11.9 %mlp_up.1 = (f32[512,768]{1,0:T(8,128)S(1)}, bf16[512,768]{1,0:T(8,128)(2,1)S(1)}, bf16[512,3072]{1,0:T(8,128)(2,1)S(1)}, bf16[512,3072]{1,0:T(8,128)(2,1)S(1)}) custom-call(s32[5]{0:T(128)S(1)} %pad_add_fusion.1.scalars.refs_0_, bf16[512,768]{1,0:T(8,128)(2,1)S(1)} %constant_dynamic-update-slice_fusion.7.heads.refs_2_, bf16[512,768]{1,0:T(8,128)(2,1)S(1)} %copy-done.17, ...), custom_call_target="tpu_custom_call" | custom-call | flops 4000000000 | bytes 16000000 | tf_op jit(solution)/shard_map/mlp_up/pallas_call | solution.py:849
  182.4 19.4 %mlp_mid.1 = (bf16[512,768]{1,0:T(8,128)(2,1)S(1)}, bf16[512,3072]{1,0:T(8,128)(2,1)}, f32[1,3072]{1,0:T(1,128)S(1)}, f32[512,768]{1,0:T(8,128)S(1)}, bf16[512,7...) custom-call(s32[5]{0:T(128)S(1)} %pad_add_fusion.1.scalars.refs_0_, ...), custom_call_target="tpu_custom_call" | custom-call | flops 10000000000 | bytes 30000000 | tf_op jit(solution)/shard_map/mlp_mid/pallas_call | solution.py:972
  201.8 21.1 %attend_back.1 = (bf16[512,768]{1,0:T(8,128)(2,1)S(1)}, bf16[2,512,768]{2,1,0:T(8,128)(2,1)S(1)}, bf16[2,512,768]{2,1,0:T(8,128)(2,1)}) custom-call(s32[5]{0:T(128)S(1)} %pad_add_fusion.1.scalars.refs_0_, bf16[512,768]{1,0:T(8,128)(2,1)S(1)} %copy-done.3, bf16[512,768]{1,0:T(8,128)(2,1)S(1)} %get-tuple-element.58.grad, ...), custom_call_target="tpu_custom_call" | custom-call | flops 20000000000 | bytes 8000000 | tf_op jit(solution)/shard_map/attend_back/pallas_call | solution.py:653
  236.7 8.9 %shard_map.301 = (bf16[768,1920]{1,0:T(8,128)(2,1)S(1)}, bf16[768,1920]{1,0:T(8,128)(2,1)S(1)}) custom-call(s32[5]{0:T(128)S(1)} %pad_add_fusion.1.scalars.refs_0_, bf16[512,768]{1,0:T(8,128)(2,1)S(1)} %copy-done.37, bf16[512,768]{1,0:T(8,128)(2,1)S(1)} %copy-done.22, bf16[512,3072]{1,0:T(8,128)(2,1)S(1)} %copy-done.30, bf16[512,768]{1,0:T(8,128)(2,1)S(1)} %copy-done.39), custom_call_target="tpu_custom_call" | custom-call | flops 3000000000 | bytes 10000000 | tf_op jit(solution)/shard_map/pallas_call | solution.py:1042
  251.8 6.6 %down_grad.1 = (bf16[1536,768]{1,0:T(8,128)(2,1)}, bf16[1536,768]{1,0:T(8,128)(2,1)S(1)}) custom-call(s32[5]{0:T(128)S(1)} %pad_add_fusion.1.scalars.refs_0_, bf16[512,3072]{1,0:T(8,128)(2,1)S(1)} %copy-done.34, bf16[512,768]{1,0:T(8,128)(2,1)S(1)} %copy-done.20), custom_call_target="tpu_custom_call" | custom-call | flops 3000000000 | bytes 9000000 | tf_op jit(solution)/shard_map/down_grad/pallas_call | solution.py:885
  267.6 8.7 %project_back.1 = (bf16[512,768]{1,0:T(8,128)(2,1)S(1)}, f32[32,16,24]{2,1,0:T(8,128)S(1)}) custom-call(s32[5]{0:T(128)S(1)} %pad_add_fusion.1.scalars.refs_0_, bf16[512,2304]{1,0:T(8,128)(2,1)S(1)} %pad_maximum_fusion.joined.refs_2_, bf16[512,768]{1,0:T(8,128)(2,1)S(1)} %copy-done.18, f32[512,768]{1,0:T(8,128)S(1)} %copy-done.29, ...), custom_call_target="tpu_custom_call" | custom-call | flops 3000000000 | bytes 12000000 | tf_op jit(solution)/shard_map/project_back/pallas_call | solution.py:1110
  288.1 6.3 %shard_map.300 = (bf16[768,1152]{1,0:T(8,128)(2,1)}, bf16[768,1152]{1,0:T(8,128)(2,1)S(1)}) custom-call(s32[5]{0:T(128)S(1)} %pad_add_fusion.1.scalars.refs_0_, bf16[512,768]{1,0:T(8,128)(2,1)S(1)} %copy-done.32, bf16[512,2304]{1,0:T(8,128)(2,1)S(1)} %pad_maximum_fusion.joined.refs_2_), custom_call_target="tpu_custom_call" | custom-call | flops 1800000000 | bytes 10000000 | tf_op jit(solution)/shard_map/pallas_call | solution.py:1042
  310.6 8.3 %collective-permute-done.56 = bf16[2,4,48,768]{3,2,1,0:T(8,128)(2,1)S(1)} collective-permute-done((bf16[2,4,48,768]{3,2,1,0:T(8,128)(2,1)S(1)}, bf16[2,4,48,768]{3,2,1,0:T(8,128)(2,1)S(1)}, u32[]{:S(2)}, u32[]{:S(2)}) %collective-permute-start.56) | collective-permute-done | bytes 589856 | tf_op jit(solution)/shard_map/ppermute | solution.py:360
  329.5 9.8 %collective-permute-done.55 = bf16[4,48,768]{2,1,0:T(8,128)(2,1)S(1)} collective-permute-done((bf16[4,48,768]{2,1,0:T(8,128)(2,1)S(1)}, bf16[4,48,768]{2,1,0:T(8,128)(2,1)S(1)}, u32[]{:S(2)}, u32[]{:S(2)}) %collective-permute-start.55) | collective-permute-done | bytes 294944 | tf_op jit(solution)/shard_map/ppermute | solution.py:360
  345.5 9.7 %collective-permute-done.58 = bf16[2,96,768]{2,1,0:T(8,128)(2,1)S(1)} collective-permute-done((bf16[2,96,768]{2,1,0:T(8,128)(2,1)S(1)}, bf16[2,96,768]{2,1,0:T(8,128)(2,1)S(1)}, u32[]{:S(2)}, u32[]{:S(2)}) %collective-permute-start.58) | collective-permute-done | bytes 294944 | tf_op jit(solution)/shard_map/ppermute | solution.py:360
  377.5 11.1 %collective-permute-done.42 = bf16[48,1152]{1,0:T(8,128)(2,1)S(1)} collective-permute-done((bf16[48,1152]{1,0:T(8,128)(2,1)S(1)}, bf16[48,1152]{1,0:T(8,128)(2,1)S(1)}, u32[]{:S(2)}, u32[]{:S(2)}) %collective-permute-start.42) | collective-permute-done | bytes 110624 | tf_op jit(solution)/shard_map/ppermute | solution.py:360
  388.7 6.6 %collective-permute-done.50 = bf16[2,48,1920]{2,1,0:T(8,128)(2,1)S(1)} collective-permute-done((bf16[2,48,1920]{2,1,0:T(8,128)(2,1)S(1)}, bf16[2,48,1920]{2,1,0:T(8,128)(2,1)S(1)}, u32[]{:S(2)}, u32[]{:S(2)}) %collective-permute-start.50) | collective-permute-done | bytes 368672 | tf_op jit(solution)/shard_map/ppermute | solution.py:360
  396.3 4.8 %collective-permute-done.51 = bf16[48,1920]{1,0:T(8,128)(2,1)S(1)} collective-permute-done((bf16[48,1920]{1,0:T(8,128)(2,1)S(1)}, bf16[48,1920]{1,0:T(8,128)(2,1)S(1)}, u32[]{:S(2)}, u32[]{:S(2)}) %collective-permute-start.51) | collective-permute-done | bytes 184352 | tf_op jit(solution)/shard_map/ppermute | solution.py:360
  (379 shorter events, 177.2 us)
Async XLA Ops:
  11.0 58.4 %collective-permute-start.24 = (bf16[1,96,768]{2,1,0:T(8,128)(2,1)}, bf16[1,96,768]{2,1,0:T(8,128)(2,1)S(1)}, u32[]{:S(2)}, u32[]{:S(2)}) collective-permute-start(bf16[1,96,768]{2,1,0:T(8,128)(2,1)} %bitcast.256), channel_id=1, source_target_pairs={{0,4},{1,5},{2,6},{3,7},{4,0},{5,1},{6,2},{7,3},{8,12},{9,13},{10,... | collective-permute-start | bytes 442376 | tf_op jit(solution)/shard_map/ppermute | solution.py:360
  23.5 46.6 %collective-permute-start.15 = (bf16[48,1920]{1,0:T(8,128)(2,1)}, bf16[48,1920]{1,0:T(8,128)(2,1)S(1)}, u32[]{:S(2)}, u32[]{:S(2)}) collective-permute-start(bf16[48,1920]{1,0:T(8,128)(2,1)} %get-tuple-element.115), channel_id=1, source_target_pairs={{0,12},{1,13},{2,14},{3,15},{4,8},{5,9},{6,10},{7,11},{8,4},{9,5},... | collective-permute-start | bytes 552968 | tf_op jit(solution)/shard_map/ppermute | solution.py:360
  49.9 46.8 %collective-permute-start.9 = (bf16[16,48,1152]{2,1,0:T(8,128)(2,1)S(1)}, bf16[16,48,1152]{2,1,0:T(8,128)(2,1)}, u32[]{:S(2)}, u32[]{:S(2)}) collective-permute-start(bf16[16,48,1152]{2,1,0:T(8,128)(2,1)S(1)} %constant_dynamic-update-slice_fusion.blocks), channel_id=1, source_target_pairs={{0,1},{1,0},{2,3},{3,2},{4,5},{5,4},{6,7},{7,6},{8,9},{9,8},{10,11... | collective-permute-start | bytes 5308424 | tf_op jit(solution)/shard_map/ppermute | solution.py:360
  93.7 35.0 %collective-permute-start.19 = (bf16[8,48,896]{2,1,0:T(8,128)(2,1)}, bf16[8,48,896]{2,1,0:T(8,128)(2,1)}, u32[]{:S(2)}, u32[]{:S(2)}) collective-permute-start(bf16[8,48,896]{2,1,0:T(8,128)(2,1)} %pad_maximum_fusion.9), channel_id=1, source_target_pairs={{0,2},{1,3},{2,0},{3,1},{4,6},{5,7},{6,4},{7,5},{8,10},{9,11},{10,... | collective-permute-start | bytes 2064392 | tf_op jit(solution)/shard_map/ppermute | solution.py:360
  96.0 31.0 %collective-permute-start.17 = (bf16[8,48,1024]{2,1,0:T(8,128)(2,1)}, bf16[8,48,1024]{2,1,0:T(8,128)(2,1)}, u32[]{:S(2)}, u32[]{:S(2)}) collective-permute-start(bf16[8,48,1024]{2,1,0:T(8,128)(2,1)} %pad_maximum_fusion.6), channel_id=1, source_target_pairs={{0,16},{1,17},{2,18},{3,19},{4,20},{5,21},{6,22},{7,23},{8,24},{9,... | collective-permute-start | bytes 2359304 | tf_op jit(solution)/shard_map/ppermute | solution.py:360
  103.4 42.4 %collective-permute-start.10 = (bf16[512,1536]{1,0:T(8,128)(2,1)S(1)}, bf16[512,1536]{1,0:T(8,128)(2,1)S(1)}, u32[]{:S(2)}, u32[]{:S(2)}) collective-permute-start(bf16[512,1536]{1,0:T(8,128)(2,1)S(1)} %get-tuple-element.49.k_own.v_own), channel_id=1, source_target_pairs={{0,1},{1,0},{2,3},{3,2},{4,5},{5,4},{6,7},{7,6},{8,9},{9,8},{10,11... | collective-permute-start | bytes 4718600 | tf_op jit(solution)/shard_map/ppermute | solution.py:360
  109.9 22.7 %collective-permute-start.23 = (bf16[256,768]{1,0:T(8,128)(2,1)}, bf16[256,768]{1,0:T(8,128)(2,1)S(1)}, u32[]{:S(2)}, u32[]{:S(2)}) collective-permute-start(bf16[256,768]{1,0:T(8,128)(2,1)} %get-tuple-element.104), channel_id=1, source_target_pairs={{0,1},{1,16},{16,0},{2,3},{3,18},{18,2},{4,5},{5,20},{20,4},{6,7},... | collective-permute-start | bytes 1179656 | tf_op jit(solution)/shard_map/ppermute | solution.py:360
  128.7 37.0 %collective-permute-start.20 = (bf16[16,48,1024]{2,1,0:T(8,128)(2,1)S(1)}, bf16[16,48,1024]{2,1,0:T(8,128)(2,1)S(1)}, u32[]{:S(2)}, u32[]{:S(2)}) collective-permute-start(bf16[16,48,1024]{2,1,0:T(8,128)(2,1)S(1)} %pad_maximum_fusion.1.a.ua), channel_id=1, source_target_pairs={{0,1},{1,0},{2,3},{3,2},{4,5},{5,4},{6,7},{7,6},{8,9},{9,8},{10,11... | collective-permute-start | bytes 4718600 | tf_op jit(solution)/shard_map/ppermute | solution.py:360
  132.6 33.1 %collective-permute-start.21 = (bf16[16,48,896]{2,1,0:T(8,128)(2,1)S(1)}, bf16[16,48,896]{2,1,0:T(8,128)(2,1)S(1)}, u32[]{:S(2)}, u32[]{:S(2)}) collective-permute-start(bf16[16,48,896]{2,1,0:T(8,128)(2,1)S(1)} %pad_maximum_fusion.2.b.ub), channel_id=1, source_target_pairs={{0,1},{1,0},{2,3},{3,2},{4,5},{5,4},{6,7},{7,6},{8,9},{9,8},{10,11... | collective-permute-start | bytes 4128776 | tf_op jit(solution)/shard_map/ppermute | solution.py:360
  143.9 38.5 %collective-permute-start.30 = (bf16[16,96,384]{2,1,0:T(8,128)(2,1)S(1)}, bf16[16,96,384]{2,1,0:T(8,128)(2,1)S(1)}, u32[]{:S(2)}, u32[]{:S(2)}) collective-permute-start(bf16[16,96,384]{2,1,0:T(8,128)(2,1)S(1)} %pad_maximum_fusion.3.da), channel_id=1, source_target_pairs={{0,1},{1,0},{2,3},{3,2},{4,5},{5,4},{6,7},{7,6},{8,9},{9,8},{10,11... | collective-permute-start | bytes 3538952 | tf_op jit(solution)/shard_map/ppermute | solution.py:360
  145.2 37.1 %collective-permute-start.31 = (bf16[16,96,384]{2,1,0:T(8,128)(2,1)S(1)}, bf16[16,96,384]{2,1,0:T(8,128)(2,1)S(1)}, u32[]{:S(2)}, u32[]{:S(2)}) collective-permute-start(bf16[16,96,384]{2,1,0:T(8,128)(2,1)S(1)} %pad_maximum_fusion.4.db), channel_id=1, source_target_pairs={{0,1},{1,0},{2,3},{3,2},{4,5},{5,4},{6,7},{7,6},{8,9},{9,8},{10,11... | collective-permute-start | bytes 3538952 | tf_op jit(solution)/shard_map/ppermute | solution.py:360
  225.1 37.3 %collective-permute-start.34 = (bf16[2,512,768]{2,1,0:T(8,128)(2,1)}, bf16[2,512,768]{2,1,0:T(8,128)(2,1)}, u32[]{:S(2)}, u32[]{:S(2)}) collective-permute-start(bf16[2,512,768]{2,1,0:T(8,128)(2,1)} %get-tuple-element.64), channel_id=1, source_target_pairs={{0,1},{1,0},{2,3},{3,2},{4,5},{5,4},{6,7},{7,6},{8,9},{9,8},{10,11... | collective-permute-start | bytes 4718600 | tf_op jit(solution)/shard_map/ppermute | solution.py:360
  227.3 32.7 %collective-permute-start.32 = (bf16[256,768]{1,0:T(8,128)(2,1)}, bf16[256,768]{1,0:T(8,128)(2,1)}, u32[]{:S(2)}, u32[]{:S(2)}) collective-permute-start(bf16[256,768]{1,0:T(8,128)(2,1)} %get-tuple-element.101), channel_id=1, source_target_pairs={{1,16},{16,17},{17,1},{3,18},{18,19},{19,3},{5,20},{20,21},{21,5},... | collective-permute-start | bytes 1179656 | tf_op jit(solution)/shard_map/ppermute | solution.py:360
  228.7 31.3 %collective-permute-start.33 = (bf16[256,768]{1,0:T(8,128)(2,1)}, bf16[256,768]{1,0:T(8,128)(2,1)}, u32[]{:S(2)}, u32[]{:S(2)}) collective-permute-start(bf16[256,768]{1,0:T(8,128)(2,1)} %get-tuple-element.102), channel_id=1, source_target_pairs={{1,0},{16,1},{0,16},{3,2},{18,3},{2,18},{5,4},{20,5},{4,20},{7,6},... | collective-permute-start | bytes 1179656 | tf_op jit(solution)/shard_map/ppermute | solution.py:360
  248.6 59.8 %collective-permute-start.45 = (bf16[768,1920]{1,0:T(8,128)(2,1)}, bf16[768,1920]{1,0:T(8,128)(2,1)}, u32[]{:S(2)}, u32[]{:S(2)}) collective-permute-start(bf16[768,1920]{1,0:T(8,128)(2,1)} %copy-done.26), channel_id=1, source_target_pairs={{0,1},{1,0},{2,3},{3,2},{4,5},{5,4},{6,7},{7,6},{8,9},{9,8},{10,11... | collective-permute-start | bytes 8847368 | tf_op jit(solution)/shard_map/ppermute | solution.py:360
  258.4 42.4 %collective-permute-start.53 = (bf16[1536,768]{1,0:T(8,128)(2,1)}, bf16[1536,768]{1,0:T(8,128)(2,1)}, u32[]{:S(2)}, u32[]{:S(2)}) collective-permute-start(bf16[1536,768]{1,0:T(8,128)(2,1)} %get-tuple-element.79), channel_id=1, source_target_pairs={{0,1},{1,0},{2,3},{3,2},{4,5},{5,4},{6,7},{7,6},{8,9},{9,8},{10,11... | collective-permute-start | bytes 7077896 | tf_op jit(solution)/shard_map/ppermute | solution.py:360
  277.2 22.4 %collective-permute-start.35 = (bf16[256,768]{1,0:T(8,128)(2,1)}, bf16[256,768]{1,0:T(8,128)(2,1)}, u32[]{:S(2)}, u32[]{:S(2)}) collective-permute-start(bf16[256,768]{1,0:T(8,128)(2,1)} %get-tuple-element.99), channel_id=1, source_target_pairs={{1,16},{16,17},{17,1},{3,18},{18,19},{19,3},{5,20},{20,21},{21,5},... | collective-permute-start | bytes 1179656 | tf_op jit(solution)/shard_map/ppermute | solution.py:360
  278.6 21.0 %collective-permute-start.36 = (bf16[256,768]{1,0:T(8,128)(2,1)}, bf16[256,768]{1,0:T(8,128)(2,1)}, u32[]{:S(2)}, u32[]{:S(2)}) collective-permute-start(bf16[256,768]{1,0:T(8,128)(2,1)} %get-tuple-element.100), channel_id=1, source_target_pairs={{1,0},{16,1},{0,16},{3,2},{18,3},{2,18},{5,4},{20,5},{4,20},{7,6},... | collective-permute-start | bytes 1179656 | tf_op jit(solution)/shard_map/ppermute | solution.py:360
  295.6 46.5 %collective-permute-start.37 = (bf16[768,1152]{1,0:T(8,128)(2,1)}, bf16[768,1152]{1,0:T(8,128)(2,1)S(1)}, u32[]{:S(2)}, u32[]{:S(2)}) collective-permute-start(bf16[768,1152]{1,0:T(8,128)(2,1)} %get-tuple-element.72), channel_id=1, source_target_pairs={{0,1},{1,0},{2,3},{3,2},{4,5},{5,4},{6,7},{7,6},{8,9},{9,8},{10,11... | collective-permute-start | bytes 5308424 | tf_op jit(solution)/shard_map/ppermute | solution.py:360
  310.0 46.9 %collective-permute-start.48 = (bf16[2,4,48,896]{3,2,1,0:T(8,128)(2,1)S(1)}, bf16[2,4,48,896]{3,2,1,0:T(8,128)(2,1)S(1)}, u32[]{:S(2)}, u32[]{:S(2)}) collective-permute-start(bf16[2,4,48,896]{3,2,1,0:T(8,128)(2,1)S(1)} %fusion.10), channel_id=1, source_target_pairs={{0,2},{1,3},{2,0},{3,1},{4,6},{5,7},{6,4},{7,5},{8,10},{9,11},{10,... | collective-permute-start | bytes 2064392 | tf_op jit(solution)/shard_map/ppermute | solution.py:360
  325.9 38.5 %collective-permute-start.46 = (bf16[4,2,48,1024]{3,2,0,1:T(8,128)(2,1)S(1)}, bf16[4,2,48,1024]{3,2,0,1:T(8,128)(2,1)S(1)}, u32[]{:S(2)}, u32[]{:S(2)}) collective-permute-start(bf16[4,2,48,1024]{3,2,0,1:T(8,128)(2,1)S(1)} %copy.81), channel_id=1, source_target_pairs={{0,16},{1,17},{2,18},{3,19},{4,20},{5,21},{6,22},{7,23},{8,24},{9,... | collective-permute-start | bytes 2359304 | tf_op jit(solution)/shard_map/ppermute | solution.py:360
  342.5 22.8 %collective-permute-start.40 = (bf16[4,48,1152]{2,1,0:T(8,128)(2,1)S(1)}, bf16[4,48,1152]{2,1,0:T(8,128)(2,1)S(1)}, u32[]{:S(2)}, u32[]{:S(2)}) collective-permute-start(bf16[4,48,1152]{2,1,0:T(8,128)(2,1)S(1)} %get-tuple-element.88), channel_id=1, source_target_pairs={{0,18},{1,19},{2,16},{3,17},{4,22},{5,23},{6,20},{7,21},{8,26},{9,... | collective-permute-start | bytes 1327112 | tf_op jit(solution)/shard_map/ppermute | solution.py:360
  345.0 21.0 %collective-permute-start.39 = (bf16[4,48,1152]{2,1,0:T(8,128)(2,1)S(1)}, bf16[4,48,1152]{2,1,0:T(8,128)(2,1)S(1)}, u32[]{:S(2)}, u32[]{:S(2)}) collective-permute-start(bf16[4,48,1152]{2,1,0:T(8,128)(2,1)S(1)} %get-tuple-element.87), channel_id=1, source_target_pairs={{0,16},{1,17},{2,18},{3,19},{4,20},{5,21},{6,22},{7,23},{8,24},{9,... | collective-permute-start | bytes 1327112 | tf_op jit(solution)/shard_map/ppermute | solution.py:360
  374.8 20.6 %collective-permute-start.50 = (bf16[2,48,1920]{2,1,0:T(8,128)(2,1)S(1)}, bf16[2,48,1920]{2,1,0:T(8,128)(2,1)S(1)}, u32[]{:S(2)}, u32[]{:S(2)}) collective-permute-start(bf16[2,48,1920]{2,1,0:T(8,128)(2,1)S(1)} %pad_maximum_fusion.14), channel_id=1, source_target_pairs={{0,8},{1,9},{2,10},{3,11},{4,12},{5,13},{6,14},{7,15},{8,0},{9,1},... | collective-permute-start | bytes 1105928 | tf_op jit(solution)/shard_map/ppermute | solution.py:360
  (111 other events, 1155.5 us)
where the time goes:
time: 411 us; the launch traced here: 404 us
  waiting for transfers between devices  115 us (28%)
  Pallas kernels  108 us (26%)
  starting transfers between devices  105 us (26%)
  other arithmetic  37.2 us (9%)
  local copies, waits for them, and re-layouts  34.8 us (8%)
    ppermute x60, waiting for transfers between devices, send(): return lax.ppermute(array, AXES, pairs)  109 us
    ppermute x60, starting transfers between devices, send(): return lax.ppermute(array, AXES, pairs)  84.1 us
    unnamed x155, local copies, waits for them, and re-layouts  24.3 us
    pallas_call x1, Pallas kernels, attend_back(): pl.pallas_call(backward_kernel, grid_spec=pltpu.PrefetchScalarGridSpec(nu...  21.1 us
    all_to_all x3, starting transfers between devices, exchange(): return lax.all_to_all(array, AXES, 0, 0, tiled=True)  20.9 us
    pallas_call x3, Pallas kernels, attend(): pl.pallas_call(forward_kernel, grid_spec=pltpu.PrefetchScalarGridSpec(num...  19.8 us
    pallas_call x1, Pallas kernels, mlp_mid(): pl.pallas_call(mlp_mid_kernel, grid_spec=pltpu.PrefetchScalarGridSpec(num...  19.4 us
    pallas_call x2, Pallas kernels, weight_grad(): pl.pallas_call(lambda *refs: weight_grad_kernel(tiles, lefts, *refs), gri...  15.2 us
  transfers between devices with their start and end apart: 63, of which 26 were waited for; matrix products, arithmetic and copies ran while one was open for 12% of the time, Pallas kernels for 17%

commit v1 on v0

--- a/solution.py
+++ b/solution.py
@@ -433,9 +433,8 @@
     return jnp.concatenate([blocks, trade(blocks, mask)], axis=0)
 
 
-def gather_direct(blocks):
-    got = [trade(blocks, m) for m in (Y, X, X | Y)]
-    return jnp.concatenate([blocks] + got, axis=0)
+def both_cores(pieces):
+    return tuple(pieces) + tuple(trade(p, CORE) for p in pieces)
 
 
 def add_low(left, right):
@@ -449,10 +448,12 @@
     if x_first:
         away = trade(add_low(keep[1], got[1]), X)
         half = add_low(add_low(keep[0], got[0]), away)
-        return add_low(half[:, 0], trade(half[:, 1], Y))
+        away = trade(half[:, 1], Y)
+        return add_low(half[:, 0], away)
     away = trade(add_low(keep[:, :, 1], got[:, :, 1]), Y)
     half = add_low(add_low(keep[:, :, 0], got[:, :, 0]), away)
-    return add_low(half[0], trade(half[1], X))
+    away = trade(half[1], X)
+    return add_low(half[0], away)
 
 
 def scatter_direct(keep, got):
@@ -679,22 +680,34 @@
         copy.wait()
 
 
-def column_jobs(scalars, source, other, target, masks, start, width, half, skip=0):
+def placed(pieces, masks):
+    return [
+        (ref, j, masks[start + j])
+        for ref, start in zip(pieces, range(0, 16, 16 // len(pieces)))
+        for j in range(16 // len(pieces))
+    ]
+
+
+def column_jobs(scalars, own, other, target, masks, start, width, half, skip=0):
     chip, core = scalars[0], scalars[1]
     jobs = []
-    for blocks, side in ((source, core), (other, 1 - core)):
+    for pieces, side in ((own, core), (other, 1 - core)):
         columns = pl.ds(pl.multiple_of(side * half + skip, 128), width)
-        for j, mask in enumerate(masks):
+        for ref, j, mask in placed(pieces, masks):
             rows = pl.ds(pl.multiple_of((chip ^ mask) * 48, 16), 48)
-            jobs.append((blocks.at[j, :, pl.ds(start, width)], target.at[rows, columns]))
+            jobs.append((ref.at[j, :, pl.ds(start, width)], target.at[rows, columns]))
     return jobs
 
 
+def qkv_jobs(scalars, pieces, weight):
+    return column_jobs(scalars, pieces[:4], pieces[4:], weight, X_LAST, 0, 1152, 1152)
+
+
 UP_A = 1024
 
 
 def up_jobs(scalars, pieces, w_up, w_out):
-    a, b, a2, b2 = pieces
+    a, b, a2, b2 = pieces[:2], pieces[2:4], pieces[4:6], pieces[6:]
     jobs = column_jobs(scalars, b, b2, w_out, Y_LAST, 1536 - UP_A, 384, 384)
     jobs += column_jobs(scalars, a, a2, w_up, X_LAST, 0, UP_A, 1536)
     return jobs + column_jobs(scalars, b, b2, w_up, Y_LAST, 0, 1536 - UP_A, 1536, UP_A)
@@ -702,14 +715,13 @@
 
 def down_jobs(scalars, pieces, target):
     chip, core = scalars[0], scalars[1]
-    a, b, a2, b2 = pieces
     jobs = []
-    for blocks, side, masks, half in (
-        (a, core, X_LAST, 0), (b, core, Y_LAST, 1), (a2, 1 - core, X_LAST, 0), (b2, 1 - core, Y_LAST, 1)
+    for k, (side, masks, half) in enumerate(
+        ((core, X_LAST, 0), (core, Y_LAST, 1), (1 - core, X_LAST, 0), (1 - core, Y_LAST, 1))
     ):
-        for j, mask in enumerate(masks):
+        for ref, j, mask in placed(pieces[2 * k : 2 * k + 2], masks):
             first = pl.multiple_of((chip ^ mask) * 192 + side * 96, 16)
-            jobs.append((blocks.at[j], target.at[pl.ds(first, 96), pl.ds(half * 384, 384)]))
+            jobs.append((ref.at[j], target.at[pl.ds(first, 96), pl.ds(half * 384, 384)]))
     return jobs
 
 
@@ -739,7 +751,9 @@
 
 
 def full(shape):
-    return pl.BlockSpec(shape, lambda i, s: (0,) * len(shape))
+    return pl.BlockSpec(
+        shape, lambda i, s: (0,) * len(shape), pipeline_mode=pl.Buffered(1)
+    )
 
 
 def anywhere():
@@ -751,12 +765,13 @@
     return column, column - column // 24 * 24
 
 
-def project_kernel(scalars, tok, owned, blocks, other, vec, normed, q, kv, weight, sems):
+def project_kernel(scalars, tok, owned, *refs):
+    pieces, (vec, normed, q, kv, weight, sems) = refs[:8], refs[8:]
     step = pl.program_id(0)
 
     @pl.when(step == 0)
     def _():
-        copies = fetch(column_jobs(scalars, blocks, other, weight, X_LAST, 0, 1152, 1152), sems)
+        copies = fetch(qkv_jobs(scalars, pieces, weight), sems)
         _, inner = spread((24, D))
         place = (inner == lax.broadcasted_iota(jnp.int32, (24, D), 0)).astype(LOW)
         wide = dot_nn(owned[...].reshape(DEVICES * 16, 24), place).reshape(DEVICES, 16, D)
@@ -787,13 +802,13 @@
         kv[...] = (result + vec[3:4, :]).astype(LOW)
 
 
-def project(scalars, tok, owned, blocks, other):
+def project(scalars, tok, owned, pieces):
     return pl.pallas_call(
         project_kernel,
         grid_spec=pltpu.PrefetchScalarGridSpec(
             num_scalar_prefetch=1,
             grid=(3,),
-            in_specs=[full((ROWS, D)), full((DEVICES, 16, 24)), anywhere(), anywhere()],
+            in_specs=[full((ROWS, D)), full((DEVICES, 16, 24))] + [anywhere()] * 8,
             out_specs=[
                 full((16, D)),
                 full((ROWS, D)),
@@ -806,21 +821,19 @@
         cost_estimate=cost(2 * 10**9, 8 * 10**6),
         compiler_params=pltpu.CompilerParams(vmem_limit_bytes=18 * MIB),
         name="project",
-    )(scalars, tok, owned, blocks, other)
+    )(scalars, tok, owned, *pieces)
 
 
 GELU = 0.7978845608028654
 
 
-def mlp_up_kernel(
-    scalars, heads, tok, vec, up_bias, a, b, a2, b2, mid, normed, act, slope,
-    w_up, w_out, sems,
-):
+def mlp_up_kernel(scalars, heads, tok, vec, up_bias, *refs):
+    pieces, (mid, normed, act, slope, w_up, w_out, sems) = refs[:8], refs[8:]
     step = pl.program_id(0)
 
     @pl.when(step == 0)
     def _():
-        copies = fetch(up_jobs(scalars, (a, b, a2, b2), w_up, w_out), sems)
+        copies = fetch(up_jobs(scalars, pieces, w_up, w_out), sems)
         wait(copies[:32])
         mid[...] = dot_nn(heads[...], w_out[...])
 
@@ -854,7 +867,7 @@
             in_specs=[
                 full((ROWS, D)), full((ROWS, D)), full((16, D)),
                 pl.BlockSpec((1, TILE), lambda i, s: (0, i)),
-            ] + [anywhere()] * 4,
+            ] + [anywhere()] * 8,
             out_specs=[full((ROWS, D)), full((ROWS, D)), tile, tile],
             scratch_shapes=[
                 pltpu.VMEM((D, FF), LOW), pltpu.VMEM((D, D), LOW), pltpu.SemaphoreType.DMA((96,)),
@@ -862,7 +875,7 @@
         ),
         out_shape=[array((ROWS, D), F32), array((ROWS, D)), array((ROWS, FF)), array((ROWS, FF))],
         cost_estimate=cost(4 * 10**9, 16 * 10**6),
-        compiler_params=pltpu.CompilerParams(vmem_limit_bytes=24 * MIB),
+        compiler_params=pltpu.CompilerParams(vmem_limit_bytes=20 * MIB),
         name="mlp_up",
     )(scalars, heads, tok, vec, up_bias, *pieces)
 
@@ -900,19 +913,18 @@
 TILES = FF // TILE
 
 
-def mlp_mid_kernel(
-    scalars, act, slope, mid, cot, vec, da, db, da2, db2, ua, ub, ua2, ub2,
-    out, grad_up, bias_sum, grad_mid, grad_attn, grad_heads, sums,
-    w_down, w_up, w_out, held, total, down_sems, up_sems,
-):
+def mlp_mid_kernel(scalars, act, slope, mid, cot, vec, *refs):
+    down_pieces, up_pieces, refs = refs[:8], refs[8:16], refs[16:]
+    out, grad_up, bias_sum, grad_mid, grad_attn, grad_heads, sums = refs[:7]
+    w_down, w_up, w_out, held, total, down_sems, up_sems = refs[7:]
     step = pl.program_id(0)
     down = lambda: [
         pltpu.make_async_copy(s, d, down_sems.at[i])
-        for i, (s, d) in enumerate(down_jobs(scalars, (da, db, da2, db2), w_down))
+        for i, (s, d) in enumerate(down_jobs(scalars, down_pieces, w_down))
     ]
     up = lambda: [
         pltpu.make_async_copy(s, d, up_sems.at[i])
-        for i, (s, d) in enumerate(up_jobs(scalars, (ua, ub, ua2, ub2), w_up, w_out))
+        for i, (s, d) in enumerate(up_jobs(scalars, up_pieces, w_up, w_out))
     ]
 
     @pl.when(step == 0)
@@ -975,7 +987,7 @@
             num_scalar_prefetch=1,
             grid=(2 * TILES,),
             in_specs=[tile, tile, full((ROWS, D)), full((ROWS, D)), full((16, D))]
-            + [anywhere()] * 8,
+            + [anywhere()] * 16,
             out_specs=[full((ROWS, D)), tile, pl.BlockSpec((1, TILE), index)]
             + [full((ROWS, D))] * 3
             + [full((8, D))],
@@ -990,7 +1002,7 @@
             array((ROWS, D)), array((ROWS, D)), array((8, D), F32),
         ],
         cost_estimate=cost(10**10, 30 * 10**6),
-        compiler_params=pltpu.CompilerParams(vmem_limit_bytes=38 * MIB),
+        compiler_params=pltpu.CompilerParams(vmem_limit_bytes=31 * MIB),
         name="mlp_mid",
     )(scalars, act, slope, mid, cot, vec, *down_pieces, *up_pieces)
 
@@ -1058,15 +1070,13 @@
     )(scalars, *[p[0] for p in parts], *[p[1] for p in parts])
 
 
-def project_back_kernel(
-    scalars, joined, tok, grad_mid, vec, mid_sums, up_sums, blocks, other, out, payload,
-    weight, total, sums, column_sums, sems,
-):
+def project_back_kernel(scalars, joined, tok, grad_mid, vec, mid_sums, up_sums, *refs):
+    pieces, (out, payload, weight, total, sums, column_sums, sems) = refs[:8], refs[8:]
     step = pl.program_id(0)
 
     @pl.when(step == 0)
     def _():
-        copies = fetch(column_jobs(scalars, blocks, other, weight, X_LAST, 0, 1152, 1152), sems)
+        copies = fetch(qkv_jobs(scalars, pieces, weight), sems)
         total[...] = jnp.zeros_like(total)
         wait(copies)
 
@@ -1103,10 +1113,19 @@
             precision=lax.Precision.HIGHEST, preferred_element_type=F32,
         )
         payload[...] = narrow.reshape(DEVICES, 16, 24)
-        payload[:, 8:12, :] = up_sums[...]
-
-
-def project_back(scalars, joined, tok, grad_mid, vec, mid_sums, up_sums, blocks, other):
+        column = lax.broadcasted_iota(jnp.int32, (DEVICES * 4, FF), 1)
+        mine = column // 24 == lax.broadcasted_iota(jnp.int32, (DEVICES * 4, FF), 0)
+        inner = lax.broadcasted_iota(jnp.int32, (24, FF), 1)
+        inner = inner - inner // 24 * 24
+        place = (inner == lax.broadcasted_iota(jnp.int32, (24, FF), 0)).astype(F32)
+        narrow = lax.dot_general(
+            jnp.where(mine, up_sums[...], 0.0), place, (((1,), (1,)), ((), ())),
+            precision=lax.Precision.HIGHEST, preferred_element_type=F32,
+        )
+        payload[:, 8:12, :] = narrow.reshape(DEVICES, 4, 24)
+
+
+def project_back(scalars, joined, tok, grad_mid, vec, mid_sums, up_sums, pieces):
     return pl.pallas_call(
         project_back_kernel,
         grid_spec=pltpu.PrefetchScalarGridSpec(
@@ -1115,8 +1134,8 @@
             in_specs=[
                 pl.BlockSpec((ROWS, D), lambda i, s: (0, i)),
                 full((ROWS, D)), full((ROWS, D)), full((16, D)), full((8, D)),
-                full((DEVICES, 4, 24)), anywhere(), anywhere(),
-            ],
+                full((1, FF)),
+            ] + [anywhere()] * 8,
             out_specs=[full((ROWS, D)), full((DEVICES, 16, 24))],
             scratch_shapes=[
                 pltpu.VMEM((D, 3 * D), LOW), pltpu.VMEM((ROWS, D), F32), pltpu.VMEM((16, D), F32),
@@ -1125,9 +1144,9 @@
         ),
         out_shape=[array((ROWS, D)), array((DEVICES, 16, 24), F32)],
         cost_estimate=cost(3 * 10**9, 12 * 10**6),
-        compiler_params=pltpu.CompilerParams(vmem_limit_bytes=26 * MIB),
+        compiler_params=pltpu.CompilerParams(vmem_limit_bytes=20 * MIB),
         name="project_back",
-    )(scalars, joined, tok, grad_mid, vec, mid_sums, up_sums, blocks, other)
+    )(scalars, joined, tok, grad_mid, vec, mid_sums, up_sums, *pieces)
 
 
 def quick_shards(*arguments):
@@ -1143,22 +1162,27 @@
     chip = x * 8 + z * 2 + y
     sequence = ((lax.axis_index("dp") >> 1) << 1) | x
 
-    def chip_half(shard):
-        rows = join(core, shard, trade(shard, CORE), 0)
-        return lax.dynamic_slice_in_dim(rows, core * (shard.shape[1] // 2), shard.shape[1] // 2, 1)
-
-    qkv_own = gather_direct(gather_z(chip_half(w_qkv)))
-    qkv_other = trade(qkv_own, CORE)
+    def half_of(rows):
+        half = rows.shape[1] // 2
+        return lax.dynamic_slice_in_dim(rows, core * half, half, 1)
+
+    fours = gather_z(half_of(join(core, w_qkv, trade(w_qkv, CORE), 0)))
+    qkv_pieces = both_cores([fours] + [trade(fours, m) for m in (Y, X, X | Y)])
     tokens_here = swap_in(tokens[0])
-    rest = gather_z(jnp.concatenate([chip_half(w_up), chip_half(w_out)], axis=1))
-    up_a = grow(grow(rest[:, :, :UP_A], Y), X)
-    up_b = grow(grow(rest[:, :, UP_A:], X), Y)
-    up_pieces = (up_a, up_b, trade(up_a, CORE), trade(up_b, CORE))
+    up_shard, out_shard = trade(w_up, CORE), trade(w_out, CORE)
+    rest = jnp.concatenate(
+        [half_of(join(core, w_up, up_shard, 0)), half_of(join(core, w_out, out_shard, 0))],
+        axis=1,
+    )
+    rest = gather_z(rest)
+    up_a = grow(rest[:, :, :UP_A], Y)
+    up_b = grow(rest[:, :, UP_A:], X)
+    up_pieces = both_cores([up_a, trade(up_a, X), up_b, trade(up_b, Y)])
     cot = swap_in(cotangent[0])
     rest = gather_z_two(w_down)
-    down_a = grow(grow(rest[:, :, :384], Y), X)
-    down_b = grow(grow(rest[:, :, 384:], X), Y)
-    down_pieces = (down_a, down_b, trade(down_a, CORE), trade(down_b, CORE))
+    down_a = grow(rest[:, :, :384], Y)
+    down_b = grow(rest[:, :, 384:], X)
+    down_pieces = both_cores([down_a, trade(down_a, X), down_b, trade(down_b, Y)])
 
     row = jnp.concatenate([timesteps, starts[0], jnp.zeros((5,), jnp.int32)])
     notes = exchange(jnp.broadcast_to(row, (DEVICES, 8)))
@@ -1176,7 +1200,7 @@
     own_starts = lax.dynamic_slice_in_dim(notes, sequence, 1, 0)[0, 1:3]
     scalars = jnp.concatenate([jnp.stack([chip, core, sequence]).astype(jnp.int32), own_starts])
 
-    vec, normed_one, query, kv = project(scalars, tokens_here, owned, qkv_own, qkv_other)
+    vec, normed_one, query, kv = project(scalars, tokens_here, owned, qkv_pieces)
     kv_other = trade(kv, CORE)
     parts = [attend(scalars, query, kv, kv_other, part) for part in range(PAIRS // PART)]
     heads_out = jnp.concatenate([part[0] for part in parts], axis=1)
@@ -1219,8 +1243,8 @@
     fours = scatter_direct(keep, trade(away, CORE))
     grad_qkv = join(core, *settle(scatter_z(fours), core), 1)
     grad_start, payload = project_back(
-        scalars, joined, tokens_here, grad_mid, vec, mid_sums, up_sums.reshape(DEVICES, 4, 24),
-        qkv_own, qkv_other,
+        scalars, joined, tokens_here, grad_mid, vec, mid_sums, up_sums,
+        qkv_pieces,
     )
     grad_tokens = swap_out(grad_start)
     final = exchange(payload)

time: 411 us -> 404 us (0.983)
  waiting for transfers between devices: 115 us -> 148 us
  starting transfers between devices: 105 us -> 82.6 us
  other arithmetic: 37.2 us -> 27.3 us
  local copies, waits for them, and re-layouts: 34.8 us -> 28.8 us
    ppermute x60 -> x67, waiting for transfers between devices: 109 us -> 140 us  [send(): return lax.ppermute(array, AXES, pairs)]
    ppermute x60 -> x67, starting transfers between devices: 84.1 us -> 67.9 us  [send(): return lax.ppermute(array, AXES, pairs)]
    all_to_all x3, starting transfers between devices: 20.9 us -> 14.7 us  [exchange(): return lax.all_to_all(array, AXES, 0, 0, tiled=True)]
    concatenate x10 -> x6, other arithmetic: 9.29 us -> 3.99 us  [grow(): return jnp.concatenate([blocks, trade(blocks, mask)], axis=0)]
    unnamed x155 -> x144, local copies, waits for them, and re-layouts: 24.3 us -> 19 us
  transfers between devices with their start and end apart: 63 -> 70, of which waited for: 26 -> 24; matrix products, arithmetic and copies ran while one was open for 12% -> 9% of each run, Pallas kernels for 17% -> 17%
where the time goes in v1:
time: 404 us; the launch traced here: 398 us
  waiting for transfers between devices  148 us (37%)
  Pallas kernels  108 us (27%)
  starting transfers between devices  82.6 us (20%)
  local copies, waits for them, and re-layouts  28.8 us (7%)
  other arithmetic  27.3 us (7%)
    ppermute x67, waiting for transfers between devices, send(): return lax.ppermute(array, AXES, pairs)  140 us
    ppermute x67, starting transfers between devices, send(): return lax.ppermute(array, AXES, pairs)  67.9 us
    pallas_call x1, Pallas kernels, attend_back(): pl.pallas_call(backward_kernel, grid_spec=pltpu.PrefetchScalarGridSpec(nu...  21 us
    pallas_call x3, Pallas kernels, attend(): pl.pallas_call(forward_kernel, grid_spec=pltpu.PrefetchScalarGridSpec(num...  19.8 us
    unnamed x144, local copies, waits for them, and re-layouts  19 us
    pallas_call x1, Pallas kernels, mlp_mid(): pl.pallas_call(mlp_mid_kernel, grid_spec=pltpu.PrefetchScalarGridSpec(num...  18.2 us
    pallas_call x2, Pallas kernels, weight_grad(): pl.pallas_call(lambda *refs: weight_grad_kernel(tiles, lefts, *refs), gri...  16 us
    all_to_all x3, starting transfers between devices, exchange(): return lax.all_to_all(array, AXES, 0, 0, tiled=True)  14.7 us
  transfers between devices with their start and end apart: 70, of which 24 were waited for; matrix products, arithmetic and copies ran while one was open for 9% of the time, Pallas kernels for 17%

profile of v1, /device:TPU:0, one launch (start us, length us, event | category | flops | bytes accessed | tf_op | source)
XLA Modules:
  0.0 398.4 jit_solution(17862075076336738009)
XLA Ops:
  3.0 7.3 %all-to-all-start = ((s32[32,1,8]{2,1,0:T(1,128)}), s32[32,1,8]{2,1,0:T(1,128)S(1)}, u32[]{:S(2)}, u32[]{:S(2)}) async-start(s32[32,1,8]{2,1,0:T(1,128)} %broadcast_in_dim.33), calls=%async_computation | async-start | bytes 32768 | tf_op jit(solution)/shard_map/all_to_all | solution.py:368
  23.2 7.2 %all-to-all-done.1 = bf16[32,2,192]{2,1,0:T(2,128)(2,1)S(1)} async-done(((bf16[32,2,192]{2,1,0:T(2,128)(2,1)}), bf16[32,2,192]{2,1,0:T(2,128)(2,1)S(1)}, u32[]{:S(2)}, u32[]{:S(2)}) %all-to-all-start.1) | async-done | bytes 24608 | tf_op jit(solution)/shard_map/all_to_all | solution.py:368
  39.0 10.5 %collective-permute-done.4 = bf16[48,1152]{1,0:T(8,128)(2,1)S(1)} collective-permute-done((bf16[48,1152]{1,0:T(8,128)(2,1)S(1)}, bf16[48,1152]{1,0:T(8,128)(2,1)S(1)}, u32[]{:S(2)}, u32[]{:S(2)}) %collective-permute-start.4) | collective-permute-done | bytes 110624 | tf_op jit(solution)/shard_map/ppermute | solution.py:360
  66.5 5.2 %collective-permute-done.7.refs_2_ = bf16[4,48,1152]{2,1,0:T(8,128)(2,1)S(1)} collective-permute-done((bf16[4,48,1152]{2,1,0:T(8,128)(2,1)S(1)}, bf16[4,48,1152]{2,1,0:T(8,128)(2,1)S(1)}, u32[]{:S(2)}, u32[]{:S(2)}) %collective-permute-start.7) | collective-permute-done | bytes 442400 | tf_op jit(solution)/shard_map/ppermute | solution.py:360
  71.7 8.6 %collective-permute-done.8.refs_3_ = bf16[4,48,1152]{2,1,0:T(8,128)(2,1)S(1)} collective-permute-done((bf16[4,48,1152]{2,1,0:T(8,128)(2,1)S(1)}, bf16[4,48,1152]{2,1,0:T(8,128)(2,1)S(1)}, u32[]{:S(2)}, u32[]{:S(2)}) %collective-permute-start.8) | collective-permute-done | bytes 442400 | tf_op jit(solution)/shard_map/ppermute | solution.py:360
  82.4 6.0 %project.1 = (f32[16,768]{1,0:T(8,128)S(1)}, bf16[512,768]{1,0:T(8,128)(2,1)S(1)}, bf16[512,768]{1,0:T(8,128)(2,1)S(1)}, bf16[512,1536]{1,0:T(8,128)(2,1)S(1)}) custom-call(s32[5]{0:T(128)S(1)} %pad_add_fusion.1.scalars.refs_0_, bf16[512,768]{1,0:T(8,128)(2,1)S(1)} %pad_maximum_fusion.1.tok, bf16[32,16,24]{2,1,0:T(8,128)(2,1)S(1)} %reshape.200.owned, ...), custom_call_target="tpu_custom_call" | custom-call | flops 2000000000 | bytes 8000000 | tf_op jit(solution)/shard_map/project/pallas_call | solution.py:806
  106.4 33.7 %collective-permute-done.33 = bf16[4,96,384]{2,1,0:T(8,128)(2,1)} collective-permute-done((bf16[4,96,384]{2,1,0:T(8,128)(2,1)}, bf16[4,96,384]{2,1,0:T(8,128)(2,1)}, u32[]{:S(2)}, u32[]{:S(2)}) %collective-permute-start.33) | collective-permute-done | bytes 294944 | tf_op jit(solution)/shard_map/ppermute | solution.py:360
  144.6 6.6 %shard_map.297 = (bf16[512,256]{1,0:T(8,128)(2,1)S(1)}, f32[2,2,512]{2,1,0:T(2,128)S(1)}) custom-call(s32[5]{0:T(128)S(1)} %pad_add_fusion.1.scalars.refs_0_, bf16[512,768]{1,0:T(8,128)(2,1)S(1)} %copy-done.3, bf16[512,1536]{1,0:T(8,128)(2,1)S(1)} %get-tuple-element.49.k_own.v_own, bf16[512,1536]{1,0:T(8,128)(2,1)S(1)} %collective-permute-done.13.k_other.v_other, ...), custom_call_target="tpu_custom_call" | custom-call | flops 1000000000 | bytes 2000000 | tf_op jit(solution)/shard_map/pallas_call | solution.py:637
  151.2 6.6 %shard_map.298 = (bf16[512,256]{1,0:T(8,128)(2,1)S(1)}, f32[2,2,512]{2,1,0:T(2,128)S(1)}) custom-call(s32[5]{0:T(128)S(1)} %pad_add_fusion.1.scalars.refs_0_, bf16[512,768]{1,0:T(8,128)(2,1)S(1)} %copy-done.3, bf16[512,1536]{1,0:T(8,128)(2,1)S(1)} %get-tuple-element.49.k_own.v_own, bf16[512,1536]{1,0:T(8,128)(2,1)S(1)} %collective-permute-done.13.k_other.v_other, ...), custom_call_target="tpu_custom_call" | custom-call | flops 1000000000 | bytes 2000000 | tf_op jit(solution)/shard_map/pallas_call | solution.py:637
  157.8 6.6 %shard_map.299 = (bf16[512,256]{1,0:T(8,128)(2,1)S(1)}, f32[2,2,512]{2,1,0:T(2,128)S(1)}) custom-call(s32[5]{0:T(128)S(1)} %pad_add_fusion.1.scalars.refs_0_, bf16[512,768]{1,0:T(8,128)(2,1)S(1)} %copy-done.3, bf16[512,1536]{1,0:T(8,128)(2,1)S(1)} %get-tuple-element.49.k_own.v_own, bf16[512,1536]{1,0:T(8,128)(2,1)S(1)} %collective-permute-done.13.k_other.v_other, ...), custom_call_target="tpu_custom_call" | custom-call | flops 1000000000 | bytes 2000000 | tf_op jit(solution)/shard_map/pallas_call | solution.py:637
  165.7 11.2 %mlp_up.1 = (f32[512,768]{1,0:T(8,128)S(1)}, bf16[512,768]{1,0:T(8,128)(2,1)S(1)}, bf16[512,3072]{1,0:T(8,128)(2,1)S(1)}, bf16[512,3072]{1,0:T(8,128)(2,1)S(1)}) custom-call(s32[5]{0:T(128)S(1)} %pad_add_fusion.1.scalars.refs_0_, bf16[512,768]{1,0:T(8,128)(2,1)S(1)} %constant_dynamic-update-slice_fusion.heads.refs_2_, bf16[512,768]{1,0:T(8,128)(2,1)S(1)} %copy-done.17, ...), custom_call_target="tpu_custom_call" | custom-call | flops 4000000000 | bytes 16000000 | tf_op jit(solution)/shard_map/mlp_up/pallas_call | solution.py:862
  179.5 18.2 %mlp_mid.1 = (bf16[512,768]{1,0:T(8,128)(2,1)S(1)}, bf16[512,3072]{1,0:T(8,128)(2,1)S(1)}, f32[1,3072]{1,0:T(1,128)S(1)}, f32[512,768]{1,0:T(8,128)S(1)}, bf16[5...) custom-call(s32[5]{0:T(128)S(1)} %pad_add_fusion.1.scalars.refs_0_, ...), custom_call_target="tpu_custom_call" | custom-call | flops 10000000000 | bytes 30000000 | tf_op jit(solution)/shard_map/mlp_mid/pallas_call | solution.py:984
  197.8 21.0 %attend_back.1 = (bf16[512,768]{1,0:T(8,128)(2,1)S(1)}, bf16[2,512,768]{2,1,0:T(8,128)(2,1)S(1)}, bf16[2,512,768]{2,1,0:T(8,128)(2,1)}) custom-call(s32[5]{0:T(128)S(1)} %pad_add_fusion.1.scalars.refs_0_, bf16[512,768]{1,0:T(8,128)(2,1)S(1)} %copy-done.3, bf16[512,768]{1,0:T(8,128)(2,1)S(1)} %get-tuple-element.58.grad, ...), custom_call_target="tpu_custom_call" | custom-call | flops 20000000000 | bytes 8000000 | tf_op jit(solution)/shard_map/attend_back/pallas_call | solution.py:654
  230.7 9.7 %shard_map.301 = (bf16[768,1920]{1,0:T(8,128)(2,1)}, bf16[768,1920]{1,0:T(8,128)(2,1)S(1)}) custom-call(s32[5]{0:T(128)S(1)} %pad_add_fusion.1.scalars.refs_0_, bf16[512,768]{1,0:T(8,128)(2,1)S(1)} %copy-done.49, bf16[512,768]{1,0:T(8,128)(2,1)S(1)} %copy-done.24, bf16[512,3072]{1,0:T(8,128)(2,1)S(1)} %copy-done.42, bf16[512,768]{1,0:T(8,128)(2,1)S(1)} %copy-done.51), custom_call_target="tpu_custom_call" | custom-call | flops 3000000000 | bytes 10000000 | tf_op jit(solution)/shard_map/pallas_call | solution.py:1054
  242.1 6.6 %down_grad.1 = (bf16[1536,768]{1,0:T(8,128)(2,1)}, bf16[1536,768]{1,0:T(8,128)(2,1)S(1)}) custom-call(s32[5]{0:T(128)S(1)} %pad_add_fusion.1.scalars.refs_0_, bf16[512,3072]{1,0:T(8,128)(2,1)S(1)} %copy-done.46, bf16[512,768]{1,0:T(8,128)(2,1)S(1)} %copy-done.20), custom_call_target="tpu_custom_call" | custom-call | flops 3000000000 | bytes 9000000 | tf_op jit(solution)/shard_map/down_grad/pallas_call | solution.py:898
  257.4 9.0 %project_back.1 = (bf16[512,768]{1,0:T(8,128)(2,1)S(1)}, f32[32,16,24]{2,1,0:T(8,128)S(1)}) custom-call(s32[5]{0:T(128)S(1)} %pad_add_fusion.1.scalars.refs_0_, bf16[512,2304]{1,0:T(8,128)(2,1)S(1)} %pad_maximum_fusion.joined.refs_2_, bf16[512,768]{1,0:T(8,128)(2,1)S(1)} %copy-done.18, f32[512,768]{1,0:T(8,128)S(1)} %copy-done.40, ...), custom_call_target="tpu_custom_call" | custom-call | flops 3000000000 | bytes 12000000 | tf_op jit(solution)/shard_map/project_back/pallas_call | solution.py:1129
  268.8 4.7 %collective-permute-start.43 = (bf16[256,768]{1,0:T(8,128)(2,1)}, bf16[256,768]{1,0:T(8,128)(2,1)}, u32[]{:S(2)}, u32[]{:S(2)}) collective-permute-start(bf16[256,768]{1,0:T(8,128)(2,1)} %get-tuple-element.98), channel_id=1, source_target_pairs={{1,0},{16,1},{0,16},{3,2},{18,3},{2,18},{5,4},{20,5},{4,20},{7,6},... | collective-permute-start | bytes 1179656 | tf_op jit(solution)/shard_map/ppermute | solution.py:360
  280.6 6.3 %shard_map.300 = (bf16[768,1152]{1,0:T(8,128)(2,1)}, bf16[768,1152]{1,0:T(8,128)(2,1)S(1)}) custom-call(s32[5]{0:T(128)S(1)} %pad_add_fusion.1.scalars.refs_0_, bf16[512,768]{1,0:T(8,128)(2,1)S(1)} %copy-done.44, bf16[512,2304]{1,0:T(8,128)(2,1)S(1)} %copy-done.9), custom_call_target="tpu_custom_call" | custom-call | flops 1800000000 | bytes 10000000 | tf_op jit(solution)/shard_map/pallas_call | solution.py:1054
  303.3 8.3 %collective-permute-done.63 = bf16[2,4,48,768]{3,2,1,0:T(8,128)(2,1)S(1)} collective-permute-done((bf16[2,4,48,768]{3,2,1,0:T(8,128)(2,1)S(1)}, bf16[2,4,48,768]{3,2,1,0:T(8,128)(2,1)S(1)}, u32[]{:S(2)}, u32[]{:S(2)}) %collective-permute-start.63) | collective-permute-done | bytes 589856 | tf_op jit(solution)/shard_map/ppermute | solution.py:360
  322.1 9.8 %collective-permute-done.62 = bf16[4,48,768]{2,1,0:T(8,128)(2,1)S(1)} collective-permute-done((bf16[4,48,768]{2,1,0:T(8,128)(2,1)S(1)}, bf16[4,48,768]{2,1,0:T(8,128)(2,1)S(1)}, u32[]{:S(2)}, u32[]{:S(2)}) %collective-permute-start.62) | collective-permute-done | bytes 294944 | tf_op jit(solution)/shard_map/ppermute | solution.py:360
  339.4 8.4 %collective-permute-done.65 = bf16[2,96,768]{2,1,0:T(8,128)(2,1)S(1)} collective-permute-done((bf16[2,96,768]{2,1,0:T(8,128)(2,1)S(1)}, bf16[2,96,768]{2,1,0:T(8,128)(2,1)S(1)}, u32[]{:S(2)}, u32[]{:S(2)}) %collective-permute-start.65) | collective-permute-done | bytes 294944 | tf_op jit(solution)/shard_map/ppermute | solution.py:360
  370.1 12.3 %collective-permute-done.49 = bf16[48,1152]{1,0:T(8,128)(2,1)S(1)} collective-permute-done((bf16[48,1152]{1,0:T(8,128)(2,1)S(1)}, bf16[48,1152]{1,0:T(8,128)(2,1)S(1)}, u32[]{:S(2)}, u32[]{:S(2)}) %collective-permute-start.49) | collective-permute-done | bytes 110624 | tf_op jit(solution)/shard_map/ppermute | solution.py:360
  382.5 6.8 %collective-permute-done.57 = bf16[2,48,1920]{2,1,0:T(8,128)(2,1)S(1)} collective-permute-done((bf16[2,48,1920]{2,1,0:T(8,128)(2,1)S(1)}, bf16[2,48,1920]{2,1,0:T(8,128)(2,1)S(1)}, u32[]{:S(2)}, u32[]{:S(2)}) %collective-permute-start.57) | collective-permute-done | bytes 368672 | tf_op jit(solution)/shard_map/ppermute | solution.py:360
  390.2 5.0 %collective-permute-done.58 = bf16[48,1920]{1,0:T(8,128)(2,1)S(1)} collective-permute-done((bf16[48,1920]{1,0:T(8,128)(2,1)S(1)}, bf16[48,1920]{1,0:T(8,128)(2,1)S(1)}, u32[]{:S(2)}, u32[]{:S(2)}) %collective-permute-start.58) | collective-permute-done | bytes 184352 | tf_op jit(solution)/shard_map/ppermute | solution.py:360
  (374 shorter events, 159.8 us)
Async XLA Ops:
  11.5 49.3 %collective-permute-start = (bf16[256,768]{1,0:T(8,128)(2,1)S(1)}, bf16[256,768]{1,0:T(8,128)(2,1)S(1)}, u32[]{:S(2)}, u32[]{:S(2)}) collective-permute-start(bf16[256,768]{1,0:T(8,128)(2,1)S(1)} %get-tuple-element.103), channel_id=1, source_target_pairs={{16,1},{17,16},{1,17},{18,3},{19,18},{3,19},{20,5},{21,20},{5,21},... | collective-permute-start | bytes 1179656 | tf_op jit(solution)/shard_map/ppermute | solution.py:360
  15.7 36.0 %collective-permute-start.29 = (bf16[1,96,768]{2,1,0:T(8,128)(2,1)S(1)}, bf16[1,96,768]{2,1,0:T(8,128)(2,1)S(1)}, u32[]{:S(2)}, u32[]{:S(2)}) collective-permute-start(bf16[1,96,768]{2,1,0:T(8,128)(2,1)S(1)} %bitcast.252), channel_id=1, source_target_pairs={{0,4},{1,5},{2,6},{3,7},{4,0},{5,1},{6,2},{7,3},{8,12},{9,13},{10,... | collective-permute-start | bytes 442376 | tf_op jit(solution)/shard_map/ppermute | solution.py:360
  59.2 21.1 %collective-permute-start.8 = (bf16[4,48,1152]{2,1,0:T(8,128)(2,1)S(1)}, bf16[4,48,1152]{2,1,0:T(8,128)(2,1)S(1)}, u32[]{:S(2)}, u32[]{:S(2)}) collective-permute-start(bf16[4,48,1152]{2,1,0:T(8,128)(2,1)S(1)} %pad_maximum_fusion.9.refs_0_), channel_id=1, source_target_pairs={{0,18},{1,19},{2,16},{3,17},{4,22},{5,23},{6,20},{7,21},{8,26},{9,... | collective-permute-start | bytes 1327112 | tf_op jit(solution)/shard_map/ppermute | solution.py:360
  88.5 55.9 %collective-permute-start.13 = (bf16[512,1536]{1,0:T(8,128)(2,1)S(1)}, bf16[512,1536]{1,0:T(8,128)(2,1)S(1)}, u32[]{:S(2)}, u32[]{:S(2)}) collective-permute-start(bf16[512,1536]{1,0:T(8,128)(2,1)S(1)} %get-tuple-element.49.k_own.v_own), channel_id=1, source_target_pairs={{0,1},{1,0},{2,3},{3,2},{4,5},{5,4},{6,7},{7,6},{8,9},{9,8},{10,11... | collective-permute-start | bytes 4718600 | tf_op jit(solution)/shard_map/ppermute | solution.py:360
  97.1 45.1 %collective-permute-start.22 = (bf16[8,48,896]{2,1,0:T(8,128)(2,1)}, bf16[8,48,896]{2,1,0:T(8,128)(2,1)}, u32[]{:S(2)}, u32[]{:S(2)}) collective-permute-start(bf16[8,48,896]{2,1,0:T(8,128)(2,1)} %pad_maximum_fusion.5.refs_2_.refs_10_), channel_id=1, source_target_pairs={{0,2},{1,3},{2,0},{3,1},{4,6},{5,7},{6,4},{7,5},{8,10},{9,11},{10,... | collective-permute-start | bytes 2064392 | tf_op jit(solution)/shard_map/ppermute | solution.py:360
  99.6 43.8 %collective-permute-start.20 = (bf16[8,48,1024]{2,1,0:T(8,128)(2,1)}, bf16[8,48,1024]{2,1,0:T(8,128)(2,1)}, u32[]{:S(2)}, u32[]{:S(2)}) collective-permute-start(bf16[8,48,1024]{2,1,0:T(8,128)(2,1)} %pad_maximum_fusion.2.refs_0_.refs_8_), channel_id=1, source_target_pairs={{0,16},{1,17},{2,18},{3,19},{4,20},{5,21},{6,22},{7,23},{8,24},{9,... | collective-permute-start | bytes 2359304 | tf_op jit(solution)/shard_map/ppermute | solution.py:360
  101.8 39.9 %collective-permute-start.32 = (bf16[8,96,384]{2,1,0:T(8,128)(2,1)}, bf16[8,96,384]{2,1,0:T(8,128)(2,1)}, u32[]{:S(2)}, u32[]{:S(2)}) collective-permute-start(bf16[8,96,384]{2,1,0:T(8,128)(2,1)} %pad_maximum_fusion.7.refs_0_), channel_id=1, source_target_pairs={{0,16},{1,17},{2,18},{3,19},{4,20},{5,21},{6,22},{7,23},{8,24},{9,... | collective-permute-start | bytes 1769480 | tf_op jit(solution)/shard_map/ppermute | solution.py:360
  106.3 33.9 %collective-permute-start.33 = (bf16[4,96,384]{2,1,0:T(8,128)(2,1)}, bf16[4,96,384]{2,1,0:T(8,128)(2,1)}, u32[]{:S(2)}, u32[]{:S(2)}) collective-permute-start(bf16[4,96,384]{2,1,0:T(8,128)(2,1)} %get-tuple-element.105), channel_id=1, source_target_pairs={{0,16},{1,17},{2,18},{3,19},{4,20},{5,21},{6,22},{7,23},{8,24},{9,... | collective-permute-start | bytes 884744 | tf_op jit(solution)/shard_map/ppermute | solution.py:360
  140.2 24.9 %collective-permute-start.23 = (bf16[8,48,1024]{2,1,0:T(8,128)(2,1)}, bf16[8,48,1024]{2,1,0:T(8,128)(2,1)S(1)}, u32[]{:S(2)}, u32[]{:S(2)}) collective-permute-start(bf16[8,48,1024]{2,1,0:T(8,128)(2,1)} %pad_maximum_fusion.2.refs_0_.refs_8_), channel_id=1, source_target_pairs={{0,1},{1,0},{2,3},{3,2},{4,5},{5,4},{6,7},{7,6},{8,9},{9,8},{10,11... | collective-permute-start | bytes 2359304 | tf_op jit(solution)/shard_map/ppermute | solution.py:360
  141.6 23.3 %collective-permute-start.25 = (bf16[8,48,896]{2,1,0:T(8,128)(2,1)}, bf16[8,48,896]{2,1,0:T(8,128)(2,1)S(1)}, u32[]{:S(2)}, u32[]{:S(2)}) collective-permute-start(bf16[8,48,896]{2,1,0:T(8,128)(2,1)} %pad_maximum_fusion.5.refs_2_.refs_10_), channel_id=1, source_target_pairs={{0,1},{1,0},{2,3},{3,2},{4,5},{5,4},{6,7},{7,6},{8,9},{9,8},{10,11... | collective-permute-start | bytes 2064392 | tf_op jit(solution)/shard_map/ppermute | solution.py:360
  142.2 23.2 %collective-permute-start.26 = (bf16[8,48,896]{2,1,0:T(8,128)(2,1)}, bf16[8,48,896]{2,1,0:T(8,128)(2,1)S(1)}, u32[]{:S(2)}, u32[]{:S(2)}) collective-permute-start(bf16[8,48,896]{2,1,0:T(8,128)(2,1)} %collective-permute-done.22.refs_3_.refs_11_), channel_id=1, source_target_pairs={{0,1},{1,0},{2,3},{3,2},{4,5},{5,4},{6,7},{7,6},{8,9},{9,8},{10,11... | collective-permute-start | bytes 2064392 | tf_op jit(solution)/shard_map/ppermute | solution.py:360
  144.4 21.2 %collective-permute-start.24 = (bf16[8,48,1024]{2,1,0:T(8,128)(2,1)}, bf16[8,48,1024]{2,1,0:T(8,128)(2,1)S(1)}, u32[]{:S(2)}, u32[]{:S(2)}) collective-permute-start(bf16[8,48,1024]{2,1,0:T(8,128)(2,1)} %collective-permute-done.20.refs_1_.refs_9_), channel_id=1, source_target_pairs={{0,1},{1,0},{2,3},{3,2},{4,5},{5,4},{6,7},{7,6},{8,9},{9,8},{10,11... | collective-permute-start | bytes 2359304 | tf_op jit(solution)/shard_map/ppermute | solution.py:360
  220.9 30.2 %collective-permute-start.41 = (bf16[2,512,768]{2,1,0:T(8,128)(2,1)}, bf16[2,512,768]{2,1,0:T(8,128)(2,1)}, u32[]{:S(2)}, u32[]{:S(2)}) collective-permute-start(bf16[2,512,768]{2,1,0:T(8,128)(2,1)} %get-tuple-element.64), channel_id=1, source_target_pairs={{0,1},{1,0},{2,3},{3,2},{4,5},{5,4},{6,7},{7,6},{8,9},{9,8},{10,11... | collective-permute-start | bytes 4718600 | tf_op jit(solution)/shard_map/ppermute | solution.py:360
  222.6 27.3 %collective-permute-start.39 = (bf16[256,768]{1,0:T(8,128)(2,1)S(1)}, bf16[256,768]{1,0:T(8,128)(2,1)S(1)}, u32[]{:S(2)}, u32[]{:S(2)}) collective-permute-start(bf16[256,768]{1,0:T(8,128)(2,1)S(1)} %get-tuple-element.99), channel_id=1, source_target_pairs={{1,16},{16,17},{17,1},{3,18},{18,19},{19,3},{5,20},{20,21},{21,5},... | collective-permute-start | bytes 1179656 | tf_op jit(solution)/shard_map/ppermute | solution.py:360
  223.3 26.6 %collective-permute-start.40 = (bf16[256,768]{1,0:T(8,128)(2,1)S(1)}, bf16[256,768]{1,0:T(8,128)(2,1)S(1)}, u32[]{:S(2)}, u32[]{:S(2)}) collective-permute-start(bf16[256,768]{1,0:T(8,128)(2,1)S(1)} %get-tuple-element.100), channel_id=1, source_target_pairs={{1,0},{16,1},{0,16},{3,2},{18,3},{2,18},{5,4},{20,5},{4,20},{7,6},... | collective-permute-start | bytes 1179656 | tf_op jit(solution)/shard_map/ppermute | solution.py:360
  240.5 60.5 %collective-permute-start.52 = (bf16[768,1920]{1,0:T(8,128)(2,1)}, bf16[768,1920]{1,0:T(8,128)(2,1)}, u32[]{:S(2)}, u32[]{:S(2)}) collective-permute-start(bf16[768,1920]{1,0:T(8,128)(2,1)} %get-tuple-element.77), channel_id=1, source_target_pairs={{0,1},{1,0},{2,3},{3,2},{4,5},{5,4},{6,7},{7,6},{8,9},{9,8},{10,11... | collective-permute-start | bytes 8847368 | tf_op jit(solution)/shard_map/ppermute | solution.py:360
  248.7 44.8 %collective-permute-start.60 = (bf16[1536,768]{1,0:T(8,128)(2,1)}, bf16[1536,768]{1,0:T(8,128)(2,1)}, u32[]{:S(2)}, u32[]{:S(2)}) collective-permute-start(bf16[1536,768]{1,0:T(8,128)(2,1)} %get-tuple-element.79), channel_id=1, source_target_pairs={{0,1},{1,0},{2,3},{3,2},{4,5},{5,4},{6,7},{7,6},{8,9},{9,8},{10,11... | collective-permute-start | bytes 7077896 | tf_op jit(solution)/shard_map/ppermute | solution.py:360
  267.4 24.9 %collective-permute-start.42 = (bf16[256,768]{1,0:T(8,128)(2,1)}, bf16[256,768]{1,0:T(8,128)(2,1)}, u32[]{:S(2)}, u32[]{:S(2)}) collective-permute-start(bf16[256,768]{1,0:T(8,128)(2,1)} %get-tuple-element.97), channel_id=1, source_target_pairs={{1,16},{16,17},{17,1},{3,18},{18,19},{19,3},{5,20},{20,21},{21,5},... | collective-permute-start | bytes 1179656 | tf_op jit(solution)/shard_map/ppermute | solution.py:360
  268.8 23.5 %collective-permute-start.43 = (bf16[256,768]{1,0:T(8,128)(2,1)}, bf16[256,768]{1,0:T(8,128)(2,1)}, u32[]{:S(2)}, u32[]{:S(2)}) collective-permute-start(bf16[256,768]{1,0:T(8,128)(2,1)} %get-tuple-element.98), channel_id=1, source_target_pairs={{1,0},{16,1},{0,16},{3,2},{18,3},{2,18},{5,4},{20,5},{4,20},{7,6},... | collective-permute-start | bytes 1179656 | tf_op jit(solution)/shard_map/ppermute | solution.py:360
  288.2 46.5 %collective-permute-start.44 = (bf16[768,1152]{1,0:T(8,128)(2,1)}, bf16[768,1152]{1,0:T(8,128)(2,1)}, u32[]{:S(2)}, u32[]{:S(2)}) collective-permute-start(bf16[768,1152]{1,0:T(8,128)(2,1)} %get-tuple-element.72), channel_id=1, source_target_pairs={{0,1},{1,0},{2,3},{3,2},{4,5},{5,4},{6,7},{7,6},{8,9},{9,8},{10,11... | collective-permute-start | bytes 5308424 | tf_op jit(solution)/shard_map/ppermute | solution.py:360
  302.6 47.0 %collective-permute-start.55 = (bf16[2,4,48,896]{3,2,1,0:T(8,128)(2,1)S(1)}, bf16[2,4,48,896]{3,2,1,0:T(8,128)(2,1)S(1)}, u32[]{:S(2)}, u32[]{:S(2)}) collective-permute-start(bf16[2,4,48,896]{3,2,1,0:T(8,128)(2,1)S(1)} %fusion.10), channel_id=1, source_target_pairs={{0,2},{1,3},{2,0},{3,1},{4,6},{5,7},{6,4},{7,5},{8,10},{9,11},{10,... | collective-permute-start | bytes 2064392 | tf_op jit(solution)/shard_map/ppermute | solution.py:360
  317.9 39.1 %collective-permute-start.53 = (bf16[4,2,48,1024]{3,2,0,1:T(8,128)(2,1)S(1)}, bf16[4,2,48,1024]{3,2,0,1:T(8,128)(2,1)S(1)}, u32[]{:S(2)}, u32[]{:S(2)}) collective-permute-start(bf16[4,2,48,1024]{3,2,0,1:T(8,128)(2,1)S(1)} %copy.81), channel_id=1, source_target_pairs={{0,16},{1,17},{2,18},{3,19},{4,20},{5,21},{6,22},{7,23},{8,24},{9,... | collective-permute-start | bytes 2359304 | tf_op jit(solution)/shard_map/ppermute | solution.py:360
  336.4 21.6 %collective-permute-start.47 = (bf16[4,48,1152]{2,1,0:T(8,128)(2,1)S(1)}, bf16[4,48,1152]{2,1,0:T(8,128)(2,1)S(1)}, u32[]{:S(2)}, u32[]{:S(2)}) collective-permute-start(bf16[4,48,1152]{2,1,0:T(8,128)(2,1)S(1)} %get-tuple-element.86), channel_id=1, source_target_pairs={{0,18},{1,19},{2,16},{3,17},{4,22},{5,23},{6,20},{7,21},{8,26},{9,... | collective-permute-start | bytes 1327112 | tf_op jit(solution)/shard_map/ppermute | solution.py:360
  368.0 21.2 %collective-permute-start.57 = (bf16[2,48,1920]{2,1,0:T(8,128)(2,1)S(1)}, bf16[2,48,1920]{2,1,0:T(8,128)(2,1)S(1)}, u32[]{:S(2)}, u32[]{:S(2)}) collective-permute-start(bf16[2,48,1920]{2,1,0:T(8,128)(2,1)S(1)} %pad_maximum_fusion.10), channel_id=1, source_target_pairs={{0,8},{1,9},{2,10},{3,11},{4,12},{5,13},{6,14},{7,15},{8,0},{9,1},... | collective-permute-start | bytes 1105928 | tf_op jit(solution)/shard_map/ppermute | solution.py:360
  (115 other events, 1222.0 us)

commit v2 on v1

--- a/solution.py
+++ b/solution.py
@@ -89,20 +89,20 @@
     time_table,
 ):
     gathered = (
-        lax.all_gather(ln1_gain, ("seq", "dp"), axis=0, tiled=True),
-        lax.all_gather(ln1_bias, ("seq", "dp"), axis=0, tiled=True),
-        lax.all_gather(w_qkv, ("seq", "dp"), axis=0, tiled=True),
-        lax.all_gather(bias_query, ("seq", "dp"), axis=0, tiled=True),
-        lax.all_gather(bias_value, ("seq", "dp"), axis=0, tiled=True),
-        lax.all_gather(w_out, ("seq", "dp"), axis=0, tiled=True),
-        lax.all_gather(bias_out, ("seq", "dp"), axis=0, tiled=True),
-        lax.all_gather(ln2_gain, ("seq", "dp"), axis=0, tiled=True),
-        lax.all_gather(ln2_bias, ("seq", "dp"), axis=0, tiled=True),
-        lax.all_gather(w_up, ("seq", "dp"), axis=0, tiled=True),
-        lax.all_gather(bias_up, ("seq", "dp"), axis=0, tiled=True),
-        lax.all_gather(w_down, ("seq", "dp"), axis=0, tiled=True),
-        lax.all_gather(bias_down, ("seq", "dp"), axis=0, tiled=True),
-        lax.all_gather(time_table, ("seq", "dp"), axis=1, tiled=True),
+        lax.all_gather(ln1_gain, AXES, axis=0, tiled=True),
+        lax.all_gather(ln1_bias, AXES, axis=0, tiled=True),
+        lax.all_gather(w_qkv, AXES, axis=0, tiled=True),
+        lax.all_gather(bias_query, AXES, axis=0, tiled=True),
+        lax.all_gather(bias_value, AXES, axis=0, tiled=True),
+        lax.all_gather(w_out, AXES, axis=0, tiled=True),
+        lax.all_gather(bias_out, AXES, axis=0, tiled=True),
+        lax.all_gather(ln2_gain, AXES, axis=0, tiled=True),
+        lax.all_gather(ln2_bias, AXES, axis=0, tiled=True),
+        lax.all_gather(w_up, AXES, axis=0, tiled=True),
+        lax.all_gather(bias_up, AXES, axis=0, tiled=True),
+        lax.all_gather(w_down, AXES, axis=0, tiled=True),
+        lax.all_gather(bias_down, AXES, axis=0, tiled=True),
+        lax.all_gather(time_table, AXES, axis=1, tiled=True),
     )
     (
         gain_one,
@@ -184,10 +184,10 @@
     act = act_value.astype(jnp.bfloat16)
     block_out = (mid + dense(act, down_full) + down_shift.astype(jnp.float32)).astype(jnp.bfloat16)
     qkv_back, out_back, up_back, down_back = (
-        lax.all_gather(w_qkv, ("seq", "dp"), axis=0, tiled=True),
-        lax.all_gather(w_out, ("seq", "dp"), axis=0, tiled=True),
-        lax.all_gather(w_up, ("seq", "dp"), axis=0, tiled=True),
-        lax.all_gather(w_down, ("seq", "dp"), axis=0, tiled=True),
+        lax.all_gather(w_qkv, AXES, axis=0, tiled=True),
+        lax.all_gather(w_out, AXES, axis=0, tiled=True),
+        lax.all_gather(w_up, AXES, axis=0, tiled=True),
+        lax.all_gather(w_down, AXES, axis=0, tiled=True),
     )
     grad_mlp = cotangent.reshape(flat_rows, D)
     grad_down = dense_left(act, grad_mlp)
@@ -295,29 +295,29 @@
     grad_tokens = grad_start.astype(jnp.bfloat16).reshape(seq_count, row_count, D)
     seq_sums = jnp.sum(grad_start.reshape(seq_count, row_count, D), axis=1)
     every_sums, every_times = (
-        lax.all_gather(seq_sums, ("seq", "dp"), axis=0, tiled=True),
-        lax.all_gather(timesteps, ("seq", "dp"), axis=0, tiled=True),
-    )
-    own_width = D // lax.axis_size(("seq", "dp"))
+        lax.all_gather(seq_sums, AXES, axis=0, tiled=True),
+        lax.all_gather(timesteps, AXES, axis=0, tiled=True),
+    )
+    own_width = D // lax.axis_size(AXES)
     own_sums = lax.dynamic_slice_in_dim(
-        every_sums, lax.axis_index(("seq", "dp")) * own_width, own_width, 1
+        every_sums, lax.axis_index(AXES) * own_width, own_width, 1
     )
     every_onehot = (every_times[None, :] == levels[:, None]).astype(jnp.float32)
     grad_table = jnp.dot(every_onehot, own_sums, precision=lax.Precision.HIGHEST)
     summed = (
-        lax.psum_scatter(grad_gain_one, ("seq", "dp"), scatter_dimension=0, tiled=True),
-        lax.psum_scatter(grad_shift_one, ("seq", "dp"), scatter_dimension=0, tiled=True),
-        lax.psum_scatter(grad_qkv, ("seq", "dp"), scatter_dimension=0, tiled=True),
-        lax.psum_scatter(grad_query_shift, ("seq", "dp"), scatter_dimension=0, tiled=True),
-        lax.psum_scatter(grad_value_shift, ("seq", "dp"), scatter_dimension=0, tiled=True),
-        lax.psum_scatter(grad_out_w, ("seq", "dp"), scatter_dimension=0, tiled=True),
-        lax.psum_scatter(grad_out_shift, ("seq", "dp"), scatter_dimension=0, tiled=True),
-        lax.psum_scatter(grad_gain_two, ("seq", "dp"), scatter_dimension=0, tiled=True),
-        lax.psum_scatter(grad_shift_two, ("seq", "dp"), scatter_dimension=0, tiled=True),
-        lax.psum_scatter(grad_up, ("seq", "dp"), scatter_dimension=0, tiled=True),
-        lax.psum_scatter(grad_up_shift, ("seq", "dp"), scatter_dimension=0, tiled=True),
-        lax.psum_scatter(grad_down, ("seq", "dp"), scatter_dimension=0, tiled=True),
-        lax.psum_scatter(grad_down_shift, ("seq", "dp"), scatter_dimension=0, tiled=True),
+        lax.psum_scatter(grad_gain_one, AXES, scatter_dimension=0, tiled=True),
+        lax.psum_scatter(grad_shift_one, AXES, scatter_dimension=0, tiled=True),
+        lax.psum_scatter(grad_qkv, AXES, scatter_dimension=0, tiled=True),
+        lax.psum_scatter(grad_query_shift, AXES, scatter_dimension=0, tiled=True),
+        lax.psum_scatter(grad_value_shift, AXES, scatter_dimension=0, tiled=True),
+        lax.psum_scatter(grad_out_w, AXES, scatter_dimension=0, tiled=True),
+        lax.psum_scatter(grad_out_shift, AXES, scatter_dimension=0, tiled=True),
+        lax.psum_scatter(grad_gain_two, AXES, scatter_dimension=0, tiled=True),
+        lax.psum_scatter(grad_shift_two, AXES, scatter_dimension=0, tiled=True),
+        lax.psum_scatter(grad_up, AXES, scatter_dimension=0, tiled=True),
+        lax.psum_scatter(grad_up_shift, AXES, scatter_dimension=0, tiled=True),
+        lax.psum_scatter(grad_down, AXES, scatter_dimension=0, tiled=True),
+        lax.psum_scatter(grad_down_shift, AXES, scatter_dimension=0, tiled=True),
     )
     return (
         block_out.reshape(seq_count, row_count, D),
@@ -352,8 +352,15 @@
 LOW = jnp.bfloat16
 
 Z_MASKS = (0, Z0, Z1, Z0 | Z1)
-X_LAST = tuple((xy | z) >> 1 for xy in (0, Y, X, X | Y) for z in Z_MASKS)
-Y_LAST = tuple((xy | z) >> 1 for xy in (0, X, Y, X | Y) for z in Z_MASKS)
+FAR_FIRST = (0, Z1, Z0, Z0 | Z1)
+
+
+def chip_masks(middle, last, z_masks):
+    return tuple((xy | z) >> 1 for xy in (0, middle, last, X | Y) for z in z_masks)
+
+
+X_LAST, Y_LAST = chip_masks(Y, X, Z_MASKS), chip_masks(X, Y, Z_MASKS)
+DOWN_X_LAST, DOWN_Y_LAST = chip_masks(Y, X, FAR_FIRST), chip_masks(X, Y, FAR_FIRST)
 
 
 def send(array, pairs):
@@ -425,10 +432,6 @@
     return jnp.stack([block] + got, axis=0)
 
 
-def gather_z_two(block):
-    return grow(grow(block[None], Z0), Z1)
-
-
 def grow(blocks, mask):
     return jnp.concatenate([blocks, trade(blocks, mask)], axis=0)
 
@@ -443,17 +446,15 @@
 
 def scatter_two(keep, got, x_first):
     n = keep.shape[-1]
-    cube = lambda array: array.reshape(2, 4, 2, -1, n)
-    keep, got = cube(keep), cube(got)
+    keep, got = (array.reshape(2, 4, 2, -1, n) for array in (keep, got))
     if x_first:
         away = trade(add_low(keep[1], got[1]), X)
-        half = add_low(add_low(keep[0], got[0]), away)
-        away = trade(half[:, 1], Y)
-        return add_low(half[:, 0], away)
-    away = trade(add_low(keep[:, :, 1], got[:, :, 1]), Y)
-    half = add_low(add_low(keep[:, :, 0], got[:, :, 0]), away)
-    away = trade(half[1], X)
-    return add_low(half[0], away)
+        part = lambda y: add_low(add_low(keep[0, :, y], got[0, :, y]), away[:, y])
+    else:
+        away = trade(add_low(keep[:, :, 1], got[:, :, 1]), Y)
+        part = lambda x: add_low(add_low(keep[x, :, 0], got[x, :, 0]), away[x])
+    last = trade(part(1), Y if x_first else X)
+    return add_low(part(0), last)
 
 
 def scatter_direct(keep, got):
@@ -475,8 +476,10 @@
 
 
 def scatter_z_two(fours):
-    half = add_low(fours[:2], trade(fours[2:], Z1))
-    return half[0].astype(F32) + trade(half[1], Z0).astype(F32)
+    fours = fours.reshape((2, 2) + fours.shape[1:])
+    away = trade(fours[:, 1], Z0)
+    got = trade(add_low(fours[1, 0], away[1]), Z1)
+    return add_low(fours[0, 0], away[0]).astype(F32) + got.astype(F32)
 
 
 def settle(block, core):
@@ -604,7 +607,7 @@
 PAIRS = HEADS // 2
 
 
-PART = 2
+PART = 3
 
 
 def pair_block(skip=0):
@@ -717,7 +720,10 @@
     chip, core = scalars[0], scalars[1]
     jobs = []
     for k, (side, masks, half) in enumerate(
-        ((core, X_LAST, 0), (core, Y_LAST, 1), (1 - core, X_LAST, 0), (1 - core, Y_LAST, 1))
+        (
+            (core, DOWN_X_LAST, 0), (core, DOWN_Y_LAST, 1),
+            (1 - core, DOWN_X_LAST, 0), (1 - core, DOWN_Y_LAST, 1),
+        )
     ):
         for ref, j, mask in placed(pieces[2 * k : 2 * k + 2], masks):
             first = pl.multiple_of((chip ^ mask) * 192 + side * 96, 16)
@@ -1179,7 +1185,7 @@
     up_b = grow(rest[:, :, UP_A:], X)
     up_pieces = both_cores([up_a, trade(up_a, X), up_b, trade(up_b, Y)])
     cot = swap_in(cotangent[0])
-    rest = gather_z_two(w_down)
+    rest = grow(grow(w_down[None], Z1), Z0)
     down_a = grow(rest[:, :, :384], Y)
     down_b = grow(rest[:, :, 384:], X)
     down_pieces = both_cores([down_a, trade(down_a, X), down_b, trade(down_b, Y)])
@@ -1232,7 +1238,7 @@
          scatter_two(keep[:, UP_A:], got[:, UP_A:], False)],
         axis=2,
     )
-    keep, got = settle(scatter_z_two(fours), core)
+    keep, got = settle(scatter_z(fours), core)
     grad_up = join(core, keep[:, :1536], got[:, :1536], 1)
     grad_out_w = join(core, keep[:, 1536:], got[:, 1536:], 1)
 
@@ -1281,38 +1287,38 @@
             P("dp"),
             P("dp", None),
             P("dp", "seq", None),
-            P(("seq", "dp")),
-            P(("seq", "dp")),
-            P(("seq", "dp"), None),
-            P(("seq", "dp")),
-            P(("seq", "dp")),
-            P(("seq", "dp"), None),
-            P(("seq", "dp")),
-            P(("seq", "dp")),
-            P(("seq", "dp")),
-            P(("seq", "dp"), None),
-            P(("seq", "dp")),
-            P(("seq", "dp"), None),
-            P(("seq", "dp")),
-            P(None, ("seq", "dp")),
+            P(AXES),
+            P(AXES),
+            P(AXES, None),
+            P(AXES),
+            P(AXES),
+            P(AXES, None),
+            P(AXES),
+            P(AXES),
+            P(AXES),
+            P(AXES, None),
+            P(AXES),
+            P(AXES, None),
+            P(AXES),
+            P(None, AXES),
         ),
         out_specs=(
             P("dp", "seq", None),
             P("dp", "seq", None),
-            P(("seq", "dp")),
-            P(("seq", "dp")),
-            P(("seq", "dp"), None),
-            P(("seq", "dp")),
-            P(("seq", "dp")),
-            P(("seq", "dp"), None),
-            P(("seq", "dp")),
-            P(("seq", "dp")),
-            P(("seq", "dp")),
-            P(("seq", "dp"), None),
-            P(("seq", "dp")),
-            P(("seq", "dp"), None),
-            P(("seq", "dp")),
-            P(None, ("seq", "dp")),
+            P(AXES),
+            P(AXES),
+            P(AXES, None),
+            P(AXES),
+            P(AXES),
+            P(AXES, None),
+            P(AXES),
+            P(AXES),
+            P(AXES),
+            P(AXES, None),
+            P(AXES),
+            P(AXES, None),
+            P(AXES),
+            P(None, AXES),
         ),
         check_vma=False,
     )

time: 404 us -> 401 us (level)
  waiting for transfers between devices: 148 us -> 129 us
  starting transfers between devices: 82.6 us -> 93.6 us
  local copies, waits for them, and re-layouts: 28.8 us -> 32.9 us
    ppermute x67 -> x68, starting transfers between devices: 67.9 us -> 80.6 us  [send(): return lax.ppermute(array, AXES, pairs)]
    ppermute x67 -> x68, waiting for transfers between devices: 140 us -> 129 us  [send(): return lax.ppermute(array, AXES, pairs)]
    all_to_all x3, waiting for transfers between devices: 7.16 us -> 0.01 us  [exchange(): return lax.all_to_all(array, AXES, 0, 0, tiled=True)]
    pallas_call x3 -> x2, Pallas kernels: 19.8 us -> 18.2 us  [attend(): pl.pallas_call(forward_kernel, grid_spec=pltpu.PrefetchScalarGridSpec(num...]
    convert_element_type x16 -> x15, other arithmetic: 8.61 us -> 7.82 us  [add_low(): return (left.astype(F32) + right.astype(F32)).astype(LOW)]
    unnamed x144 -> x163, local copies, waits for them, and re-layouts: 19 us -> 19.3 us
  transfers between devices with their start and end apart: 70 -> 71, of which waited for: 24 -> 20; matrix products, arithmetic and copies ran while one was open for 9% -> 11% of each run, Pallas kernels for 17% -> 17%
where the time goes in v2:
time: 401 us; the launch traced here: 395 us
  waiting for transfers between devices  129 us (32%)
  Pallas kernels  106 us (26%)
  starting transfers between devices  93.6 us (23%)
  local copies, waits for them, and re-layouts  32.9 us (8%)
  other arithmetic  29.4 us (7%)
    ppermute x68, waiting for transfers between devices, send(): return lax.ppermute(array, AXES, pairs)  129 us
    ppermute x68, starting transfers between devices, send(): return lax.ppermute(array, AXES, pairs)  80.6 us
    pallas_call x1, Pallas kernels, attend_back(): pl.pallas_call(backward_kernel, grid_spec=pltpu.PrefetchScalarGridSpec(nu...  21 us
    unnamed x163, local copies, waits for them, and re-layouts  19.3 us
    pallas_call x1, Pallas kernels, mlp_mid(): pl.pallas_call(mlp_mid_kernel, grid_spec=pltpu.PrefetchScalarGridSpec(num...  18.2 us
    pallas_call x2, Pallas kernels, attend(): pl.pallas_call(forward_kernel, grid_spec=pltpu.PrefetchScalarGridSpec(num...  18.2 us
    pallas_call x2, Pallas kernels, weight_grad(): pl.pallas_call(lambda *refs: weight_grad_kernel(tiles, lefts, *refs), gri...  15.9 us
    all_to_all x3, starting transfers between devices, exchange(): return lax.all_to_all(array, AXES, 0, 0, tiled=True)  13 us
  transfers between devices with their start and end apart: 71, of which 20 were waited for; matrix products, arithmetic and copies ran while one was open for 11% of the time, Pallas kernels for 17%

profile of v2, /device:TPU:0, one launch (start us, length us, event | category | flops | bytes accessed | tf_op | source)
XLA Modules:
  0.0 395.1 jit_solution(11703514606293518426)
XLA Ops:
  3.0 7.3 %all-to-all-start = ((s32[32,1,8]{2,1,0:T(1,128)}), s32[32,1,8]{2,1,0:T(1,128)S(1)}, u32[]{:S(2)}, u32[]{:S(2)}) async-start(s32[32,1,8]{2,1,0:T(1,128)} %broadcast_in_dim.33), calls=%async_computation | async-start | bytes 32768 | tf_op jit(solution)/shard_map/all_to_all | solution.py:375
  35.6 9.0 %collective-permute-done.4 = bf16[48,1152]{1,0:T(8,128)(2,1)S(1)} collective-permute-done((bf16[48,1152]{1,0:T(8,128)(2,1)S(1)}, bf16[48,1152]{1,0:T(8,128)(2,1)S(1)}, u32[]{:S(2)}, u32[]{:S(2)}) %collective-permute-start.4) | collective-permute-done | bytes 110624 | tf_op jit(solution)/shard_map/ppermute | solution.py:367
  48.4 5.6 %collective-permute-done.17 = bf16[48,1920]{1,0:T(8,128)(2,1)S(1)} collective-permute-done((bf16[48,1920]{1,0:T(8,128)(2,1)S(1)}, bf16[48,1920]{1,0:T(8,128)(2,1)S(1)}, u32[]{:S(2)}, u32[]{:S(2)}) %collective-permute-start.17) | collective-permute-done | bytes 184352 | tf_op jit(solution)/shard_map/ppermute | solution.py:367
  61.0 5.9 %collective-permute-done.8.refs_3_ = bf16[4,48,1152]{2,1,0:T(8,128)(2,1)S(1)} collective-permute-done((bf16[4,48,1152]{2,1,0:T(8,128)(2,1)S(1)}, bf16[4,48,1152]{2,1,0:T(8,128)(2,1)S(1)}, u32[]{:S(2)}, u32[]{:S(2)}) %collective-permute-start.8) | collective-permute-done | bytes 442400 | tf_op jit(solution)/shard_map/ppermute | solution.py:367
  70.6 5.1 %collective-permute-start.30 = (bf16[2,96,768]{2,1,0:T(8,128)(2,1)S(1)}, bf16[2,96,768]{2,1,0:T(8,128)(2,1)S(1)}, u32[]{:S(2)}, u32[]{:S(2)}) collective-permute-start(bf16[2,96,768]{2,1,0:T(8,128)(2,1)S(1)} %pad_maximum_fusion.12), channel_id=1, source_target_pairs={{0,4},{1,5},{2,6},{3,7},{4,0},{5,1},{6,2},{7,3},{8,12},{9,13},{10,... | collective-permute-start | bytes 884744 | tf_op jit(solution)/shard_map/ppermute | solution.py:367
  80.0 6.0 %project.1 = (f32[16,768]{1,0:T(8,128)S(1)}, bf16[512,768]{1,0:T(8,128)(2,1)S(1)}, bf16[512,768]{1,0:T(8,128)(2,1)S(1)}, bf16[512,1536]{1,0:T(8,128)(2,1)S(1)}) custom-call(s32[5]{0:T(128)S(1)} %pad_add_fusion.1.scalars.refs_0_, bf16[512,768]{1,0:T(8,128)(2,1)S(1)} %pad_maximum_fusion.1.tok, bf16[32,16,24]{2,1,0:T(8,128)(2,1)S(1)} %reshape.257.owned, ...), custom_call_target="tpu_custom_call" | custom-call | flops 2000000000 | bytes 8000000 | tf_op jit(solution)/shard_map/project/pallas_call | solution.py:812
  98.6 6.6 %collective-permute-done.28 = bf16[256,768]{1,0:T(8,128)(2,1)S(1)} collective-permute-done((bf16[256,768]{1,0:T(8,128)(2,1)S(1)}, bf16[256,768]{1,0:T(8,128)(2,1)S(1)}, u32[]{:S(2)}, u32[]{:S(2)}) %collective-permute-start.28) | collective-permute-done | bytes 393248 | tf_op jit(solution)/shard_map/ppermute | solution.py:367
  106.2 31.1 %collective-permute-done.33 = bf16[4,96,384]{2,1,0:T(8,128)(2,1)} collective-permute-done((bf16[4,96,384]{2,1,0:T(8,128)(2,1)}, bf16[4,96,384]{2,1,0:T(8,128)(2,1)}, u32[]{:S(2)}, u32[]{:S(2)}) %collective-permute-start.33) | collective-permute-done | bytes 294944 | tf_op jit(solution)/shard_map/ppermute | solution.py:367
  142.3 9.1 %shard_map.297 = (bf16[512,384]{1,0:T(8,128)(2,1)S(1)}, f32[3,2,512]{2,1,0:T(2,128)S(1)}) custom-call(s32[5]{0:T(128)S(1)} %pad_add_fusion.1.scalars.refs_0_, bf16[512,768]{1,0:T(8,128)(2,1)S(1)} %copy-done.4, bf16[512,1536]{1,0:T(8,128)(2,1)S(1)} %get-tuple-element.47.k_own.v_own, bf16[512,1536]{1,0:T(8,128)(2,1)S(1)} %collective-permute-done.13.k_other.v_other, ...), custom_call_target="tpu_custom_call" | custom-call | flops 1000000000 | bytes 2000000 | tf_op jit(solution)/shard_map/pallas_call | solution.py:640
  151.4 9.1 %shard_map.298 = (bf16[512,384]{1,0:T(8,128)(2,1)S(1)}, f32[3,2,512]{2,1,0:T(2,128)S(1)}) custom-call(s32[5]{0:T(128)S(1)} %pad_add_fusion.1.scalars.refs_0_, bf16[512,768]{1,0:T(8,128)(2,1)S(1)} %copy-done.4, bf16[512,1536]{1,0:T(8,128)(2,1)S(1)} %get-tuple-element.47.k_own.v_own, bf16[512,1536]{1,0:T(8,128)(2,1)S(1)} %collective-permute-done.13.k_other.v_other, ...), custom_call_target="tpu_custom_call" | custom-call | flops 1000000000 | bytes 2000000 | tf_op jit(solution)/shard_map/pallas_call | solution.py:640
  161.8 11.0 %mlp_up.1 = (f32[512,768]{1,0:T(8,128)S(1)}, bf16[512,768]{1,0:T(8,128)(2,1)S(1)}, bf16[512,3072]{1,0:T(8,128)(2,1)S(1)}, bf16[512,3072]{1,0:T(8,128)(2,1)S(1)}) custom-call(s32[5]{0:T(128)S(1)} %pad_add_fusion.1.scalars.refs_0_, bf16[512,768]{1,0:T(8,128)(2,1)S(1)} %constant_dynamic-update-slice_fusion.heads.refs_2_, bf16[512,768]{1,0:T(8,128)(2,1)S(1)} %copy-done.17, ...), custom_call_target="tpu_custom_call" | custom-call | flops 4000000000 | bytes 16000000 | tf_op jit(solution)/shard_map/mlp_up/pallas_call | solution.py:868
  175.5 18.2 %mlp_mid.1 = (bf16[512,768]{1,0:T(8,128)(2,1)S(1)}, bf16[512,3072]{1,0:T(8,128)(2,1)S(1)}, f32[1,3072]{1,0:T(1,128)S(1)}, f32[512,768]{1,0:T(8,128)S(1)}, bf16[5...) custom-call(s32[5]{0:T(128)S(1)} %pad_add_fusion.1.scalars.refs_0_, ...), custom_call_target="tpu_custom_call" | custom-call | flops 10000000000 | bytes 30000000 | tf_op jit(solution)/shard_map/mlp_mid/pallas_call | solution.py:990
  193.8 21.0 %attend_back.1 = (bf16[512,768]{1,0:T(8,128)(2,1)S(1)}, bf16[2,512,768]{2,1,0:T(8,128)(2,1)S(1)}, bf16[2,512,768]{2,1,0:T(8,128)(2,1)}) custom-call(s32[5]{0:T(128)S(1)} %pad_add_fusion.1.scalars.refs_0_, bf16[512,768]{1,0:T(8,128)(2,1)S(1)} %copy-done.4, bf16[512,768]{1,0:T(8,128)(2,1)S(1)} %get-tuple-element.55.grad, ...), custom_call_target="tpu_custom_call" | custom-call | flops 20000000000 | bytes 8000000 | tf_op jit(solution)/shard_map/attend_back/pallas_call | solution.py:657
  224.1 6.8 %down_grad.1 = (bf16[1536,768]{1,0:T(8,128)(2,1)}, bf16[1536,768]{1,0:T(8,128)(2,1)S(1)}) custom-call(s32[5]{0:T(128)S(1)} %pad_add_fusion.1.scalars.refs_0_, bf16[512,3072]{1,0:T(8,128)(2,1)S(1)} %copy-done.47, bf16[512,768]{1,0:T(8,128)(2,1)S(1)} %copy-done.20), custom_call_target="tpu_custom_call" | custom-call | flops 3000000000 | bytes 9000000 | tf_op jit(solution)/shard_map/down_grad/pallas_call | solution.py:904
  230.8 9.6 %shard_map.300 = (bf16[768,1920]{1,0:T(8,128)(2,1)}, bf16[768,1920]{1,0:T(8,128)(2,1)S(1)}) custom-call(s32[5]{0:T(128)S(1)} %pad_add_fusion.1.scalars.refs_0_, bf16[512,768]{1,0:T(8,128)(2,1)S(1)} %copy-done.50, bf16[512,768]{1,0:T(8,128)(2,1)S(1)} %copy-done.24, bf16[512,3072]{1,0:T(8,128)(2,1)S(1)} %copy-done.43, bf16[512,768]{1,0:T(8,128)(2,1)S(1)} %copy-done.52), custom_call_target="tpu_custom_call" | custom-call | flops 3000000000 | bytes 10000000 | tf_op jit(solution)/shard_map/pallas_call | solution.py:1060
  253.1 8.9 %project_back.1 = (bf16[512,768]{1,0:T(8,128)(2,1)S(1)}, f32[32,16,24]{2,1,0:T(8,128)S(1)}) custom-call(s32[5]{0:T(128)S(1)} %pad_add_fusion.1.scalars.refs_0_, bf16[512,2304]{1,0:T(8,128)(2,1)S(1)} %pad_maximum_fusion.joined.refs_2_, bf16[512,768]{1,0:T(8,128)(2,1)S(1)} %copy-done.18, f32[512,768]{1,0:T(8,128)S(1)} %copy-done.41, ...), custom_call_target="tpu_custom_call" | custom-call | flops 3000000000 | bytes 12000000 | tf_op jit(solution)/shard_map/project_back/pallas_call | solution.py:1135
  265.2 4.5 %collective-permute-start.43 = (bf16[256,768]{1,0:T(8,128)(2,1)}, bf16[256,768]{1,0:T(8,128)(2,1)}, u32[]{:S(2)}, u32[]{:S(2)}) collective-permute-start(bf16[256,768]{1,0:T(8,128)(2,1)} %get-tuple-element.94), channel_id=1, source_target_pairs={{1,0},{16,1},{0,16},{3,2},{18,3},{2,18},{5,4},{20,5},{4,20},{7,6},... | collective-permute-start | bytes 1179656 | tf_op jit(solution)/shard_map/ppermute | solution.py:367
  276.2 6.2 %shard_map.299 = (bf16[768,1152]{1,0:T(8,128)(2,1)}, bf16[768,1152]{1,0:T(8,128)(2,1)S(1)}) custom-call(s32[5]{0:T(128)S(1)} %pad_add_fusion.1.scalars.refs_0_, bf16[512,768]{1,0:T(8,128)(2,1)S(1)} %copy-done.45, bf16[512,2304]{1,0:T(8,128)(2,1)S(1)} %copy-done.9), custom_call_target="tpu_custom_call" | custom-call | flops 1800000000 | bytes 10000000 | tf_op jit(solution)/shard_map/pallas_call | solution.py:1060
  298.8 7.9 %collective-permute-done.64 = bf16[2,4,48,768]{3,2,1,0:T(8,128)(2,1)S(1)} collective-permute-done((bf16[2,4,48,768]{3,2,1,0:T(8,128)(2,1)S(1)}, bf16[2,4,48,768]{3,2,1,0:T(8,128)(2,1)S(1)}, u32[]{:S(2)}, u32[]{:S(2)}) %collective-permute-start.64) | collective-permute-done | bytes 589856 | tf_op jit(solution)/shard_map/ppermute | solution.py:367
  316.0 16.9 %collective-permute-done.65 = bf16[4,48,768]{2,1,0:T(8,128)(2,1)S(1)} collective-permute-done((bf16[4,48,768]{2,1,0:T(8,128)(2,1)S(1)}, bf16[4,48,768]{2,1,0:T(8,128)(2,1)S(1)}, u32[]{:S(2)}, u32[]{:S(2)}) %collective-permute-start.65) | collective-permute-done | bytes 294944 | tf_op jit(solution)/shard_map/ppermute | solution.py:367
  344.8 5.2 %collective-permute-done.67 = bf16[96,768]{1,0:T(8,128)(2,1)S(1)} collective-permute-done((bf16[96,768]{1,0:T(8,128)(2,1)S(1)}, bf16[96,768]{1,0:T(8,128)(2,1)S(1)}, u32[]{:S(2)}, u32[]{:S(2)}) %collective-permute-start.67) | collective-permute-done | bytes 147488 | tf_op jit(solution)/shard_map/ppermute | solution.py:367
  352.4 6.8 %collective-permute-done.46 = bf16[4,48,1152]{2,1,0:T(8,128)(2,1)S(1)} collective-permute-done((bf16[4,48,1152]{2,1,0:T(8,128)(2,1)S(1)}, bf16[4,48,1152]{2,1,0:T(8,128)(2,1)S(1)}, u32[]{:S(2)}, u32[]{:S(2)}) %collective-permute-start.46) | collective-permute-done | bytes 442400 | tf_op jit(solution)/shard_map/ppermute | solution.py:367
  367.9 4.5 %collective-permute-done.49 = bf16[48,1152]{1,0:T(8,128)(2,1)S(1)} collective-permute-done((bf16[48,1152]{1,0:T(8,128)(2,1)S(1)}, bf16[48,1152]{1,0:T(8,128)(2,1)S(1)}, u32[]{:S(2)}, u32[]{:S(2)}) %collective-permute-start.49) | collective-permute-done | bytes 110624 | tf_op jit(solution)/shard_map/ppermute | solution.py:367
  384.1 7.8 %collective-permute-done.58 = bf16[48,1920]{1,0:T(8,128)(2,1)S(1)} collective-permute-done((bf16[48,1920]{1,0:T(8,128)(2,1)S(1)}, bf16[48,1920]{1,0:T(8,128)(2,1)S(1)}, u32[]{:S(2)}, u32[]{:S(2)}) %collective-permute-start.58) | collective-permute-done | bytes 184352 | tf_op jit(solution)/shard_map/ppermute | solution.py:367
  (391 shorter events, 161.7 us)
Async XLA Ops:
  12.4 47.3 %collective-permute-start = (bf16[256,768]{1,0:T(8,128)(2,1)}, bf16[256,768]{1,0:T(8,128)(2,1)}, u32[]{:S(2)}, u32[]{:S(2)}) collective-permute-start(bf16[256,768]{1,0:T(8,128)(2,1)} %get-tuple-element.99), channel_id=1, source_target_pairs={{16,1},{17,16},{1,17},{18,3},{19,18},{3,19},{20,5},{21,20},{5,21},... | collective-permute-start | bytes 1179656 | tf_op jit(solution)/shard_map/ppermute | solution.py:367
  16.5 28.8 %collective-permute-start.29 = (bf16[1,96,768]{2,1,0:T(8,128)(2,1)S(1)}, bf16[1,96,768]{2,1,0:T(8,128)(2,1)S(1)}, u32[]{:S(2)}, u32[]{:S(2)}) collective-permute-start(bf16[1,96,768]{2,1,0:T(8,128)(2,1)S(1)} %bitcast.381), channel_id=1, source_target_pairs={{0,8},{1,9},{2,10},{3,11},{4,12},{5,13},{6,14},{7,15},{8,0},{9,1},... | collective-permute-start | bytes 442376 | tf_op jit(solution)/shard_map/ppermute | solution.py:367
  21.0 35.4 %all-to-all-start.1 = ((bf16[32,2,192]{2,1,0:T(2,128)(2,1)}), bf16[32,2,192]{2,1,0:T(2,128)(2,1)S(1)}, u32[]{:S(2)}, u32[]{:S(2)}) async-start(bf16[32,2,192]{2,1,0:T(2,128)(2,1)} %reshape.256), calls=%async_computation.1 | async-start | bytes 65536 | tf_op jit(solution)/shard_map/all_to_all | solution.py:375
  86.1 54.4 %collective-permute-start.13 = (bf16[512,1536]{1,0:T(8,128)(2,1)S(1)}, bf16[512,1536]{1,0:T(8,128)(2,1)S(1)}, u32[]{:S(2)}, u32[]{:S(2)}) collective-permute-start(bf16[512,1536]{1,0:T(8,128)(2,1)S(1)} %get-tuple-element.47.k_own.v_own), channel_id=1, source_target_pairs={{0,1},{1,0},{2,3},{3,2},{4,5},{5,4},{6,7},{7,6},{8,9},{9,8},{10,11... | collective-permute-start | bytes 4718600 | tf_op jit(solution)/shard_map/ppermute | solution.py:367
  93.3 47.2 %collective-permute-start.20 = (bf16[8,48,1024]{2,1,0:T(8,128)(2,1)}, bf16[8,48,1024]{2,1,0:T(8,128)(2,1)}, u32[]{:S(2)}, u32[]{:S(2)}) collective-permute-start(bf16[8,48,1024]{2,1,0:T(8,128)(2,1)} %pad_maximum_fusion.2.refs_0_.refs_8_), channel_id=1, source_target_pairs={{0,16},{1,17},{2,18},{3,19},{4,20},{5,21},{6,22},{7,23},{8,24},{9,... | collective-permute-start | bytes 2359304 | tf_op jit(solution)/shard_map/ppermute | solution.py:367
  96.4 42.6 %collective-permute-start.22 = (bf16[8,48,896]{2,1,0:T(8,128)(2,1)}, bf16[8,48,896]{2,1,0:T(8,128)(2,1)}, u32[]{:S(2)}, u32[]{:S(2)}) collective-permute-start(bf16[8,48,896]{2,1,0:T(8,128)(2,1)} %pad_maximum_fusion.5.refs_2_.refs_10_), channel_id=1, source_target_pairs={{0,2},{1,3},{2,0},{3,1},{4,6},{5,7},{6,4},{7,5},{8,10},{9,11},{10,... | collective-permute-start | bytes 2064392 | tf_op jit(solution)/shard_map/ppermute | solution.py:367
  97.9 40.5 %collective-permute-start.32 = (bf16[8,96,384]{2,1,0:T(8,128)(2,1)}, bf16[8,96,384]{2,1,0:T(8,128)(2,1)}, u32[]{:S(2)}, u32[]{:S(2)}) collective-permute-start(bf16[8,96,384]{2,1,0:T(8,128)(2,1)} %pad_maximum_fusion.7.refs_0_), channel_id=1, source_target_pairs={{0,16},{1,17},{2,18},{3,19},{4,20},{5,21},{6,22},{7,23},{8,24},{9,... | collective-permute-start | bytes 1769480 | tf_op jit(solution)/shard_map/ppermute | solution.py:367
  105.3 32.1 %collective-permute-start.33 = (bf16[4,96,384]{2,1,0:T(8,128)(2,1)}, bf16[4,96,384]{2,1,0:T(8,128)(2,1)}, u32[]{:S(2)}, u32[]{:S(2)}) collective-permute-start(bf16[4,96,384]{2,1,0:T(8,128)(2,1)} %get-tuple-element.104), channel_id=1, source_target_pairs={{0,16},{1,17},{2,18},{3,19},{4,20},{5,21},{6,22},{7,23},{8,24},{9,... | collective-permute-start | bytes 884744 | tf_op jit(solution)/shard_map/ppermute | solution.py:367
  137.3 23.8 %collective-permute-start.23 = (bf16[8,48,1024]{2,1,0:T(8,128)(2,1)}, bf16[8,48,1024]{2,1,0:T(8,128)(2,1)S(1)}, u32[]{:S(2)}, u32[]{:S(2)}) collective-permute-start(bf16[8,48,1024]{2,1,0:T(8,128)(2,1)} %pad_maximum_fusion.2.refs_0_.refs_8_), channel_id=1, source_target_pairs={{0,1},{1,0},{2,3},{3,2},{4,5},{5,4},{6,7},{7,6},{8,9},{9,8},{10,11... | collective-permute-start | bytes 2359304 | tf_op jit(solution)/shard_map/ppermute | solution.py:367
  138.5 22.2 %collective-permute-start.25 = (bf16[8,48,896]{2,1,0:T(8,128)(2,1)}, bf16[8,48,896]{2,1,0:T(8,128)(2,1)S(1)}, u32[]{:S(2)}, u32[]{:S(2)}) collective-permute-start(bf16[8,48,896]{2,1,0:T(8,128)(2,1)} %pad_maximum_fusion.5.refs_2_.refs_10_), channel_id=1, source_target_pairs={{0,1},{1,0},{2,3},{3,2},{4,5},{5,4},{6,7},{7,6},{8,9},{9,8},{10,11... | collective-permute-start | bytes 2064392 | tf_op jit(solution)/shard_map/ppermute | solution.py:367
  139.1 21.5 %collective-permute-start.34 = (bf16[8,96,384]{2,1,0:T(8,128)(2,1)S(1)}, bf16[8,96,384]{2,1,0:T(8,128)(2,1)S(1)}, u32[]{:S(2)}, u32[]{:S(2)}) collective-permute-start(bf16[8,96,384]{2,1,0:T(8,128)(2,1)S(1)} %pad_maximum_fusion.8.refs_2_), channel_id=1, source_target_pairs={{0,2},{1,3},{2,0},{3,1},{4,6},{5,7},{6,4},{7,5},{8,10},{9,11},{10,... | collective-permute-start | bytes 1769480 | tf_op jit(solution)/shard_map/ppermute | solution.py:367
  216.8 29.5 %collective-permute-start.41 = (bf16[2,512,768]{2,1,0:T(8,128)(2,1)}, bf16[2,512,768]{2,1,0:T(8,128)(2,1)}, u32[]{:S(2)}, u32[]{:S(2)}) collective-permute-start(bf16[2,512,768]{2,1,0:T(8,128)(2,1)} %get-tuple-element.60), channel_id=1, source_target_pairs={{0,1},{1,0},{2,3},{3,2},{4,5},{5,4},{6,7},{7,6},{8,9},{9,8},{10,11... | collective-permute-start | bytes 4718600 | tf_op jit(solution)/shard_map/ppermute | solution.py:367
  218.1 27.1 %collective-permute-start.39 = (bf16[256,768]{1,0:T(8,128)(2,1)S(1)}, bf16[256,768]{1,0:T(8,128)(2,1)S(1)}, u32[]{:S(2)}, u32[]{:S(2)}) collective-permute-start(bf16[256,768]{1,0:T(8,128)(2,1)S(1)} %get-tuple-element.95), channel_id=1, source_target_pairs={{1,16},{16,17},{17,1},{3,18},{18,19},{19,3},{5,20},{20,21},{21,5},... | collective-permute-start | bytes 1179656 | tf_op jit(solution)/shard_map/ppermute | solution.py:367
  218.8 26.4 %collective-permute-start.40 = (bf16[256,768]{1,0:T(8,128)(2,1)S(1)}, bf16[256,768]{1,0:T(8,128)(2,1)S(1)}, u32[]{:S(2)}, u32[]{:S(2)}) collective-permute-start(bf16[256,768]{1,0:T(8,128)(2,1)S(1)} %get-tuple-element.96), channel_id=1, source_target_pairs={{1,0},{16,1},{0,16},{3,2},{18,3},{2,18},{5,4},{20,5},{4,20},{7,6},... | collective-permute-start | bytes 1179656 | tf_op jit(solution)/shard_map/ppermute | solution.py:367
  243.1 53.7 %collective-permute-start.52 = (bf16[768,1920]{1,0:T(8,128)(2,1)}, bf16[768,1920]{1,0:T(8,128)(2,1)}, u32[]{:S(2)}, u32[]{:S(2)}) collective-permute-start(bf16[768,1920]{1,0:T(8,128)(2,1)} %get-tuple-element.73), channel_id=1, source_target_pairs={{0,1},{1,0},{2,3},{3,2},{4,5},{5,4},{6,7},{7,6},{8,9},{9,8},{10,11... | collective-permute-start | bytes 8847368 | tf_op jit(solution)/shard_map/ppermute | solution.py:367
  243.6 45.4 %collective-permute-start.61 = (bf16[1536,768]{1,0:T(8,128)(2,1)}, bf16[1536,768]{1,0:T(8,128)(2,1)}, u32[]{:S(2)}, u32[]{:S(2)}) collective-permute-start(bf16[1536,768]{1,0:T(8,128)(2,1)} %get-tuple-element.75), channel_id=1, source_target_pairs={{0,1},{1,0},{2,3},{3,2},{4,5},{5,4},{6,7},{7,6},{8,9},{9,8},{10,11... | collective-permute-start | bytes 7077896 | tf_op jit(solution)/shard_map/ppermute | solution.py:367
  263.8 23.7 %collective-permute-start.42 = (bf16[256,768]{1,0:T(8,128)(2,1)}, bf16[256,768]{1,0:T(8,128)(2,1)}, u32[]{:S(2)}, u32[]{:S(2)}) collective-permute-start(bf16[256,768]{1,0:T(8,128)(2,1)} %get-tuple-element.93), channel_id=1, source_target_pairs={{1,16},{16,17},{17,1},{3,18},{18,19},{19,3},{5,20},{20,21},{21,5},... | collective-permute-start | bytes 1179656 | tf_op jit(solution)/shard_map/ppermute | solution.py:367
  265.2 22.3 %collective-permute-start.43 = (bf16[256,768]{1,0:T(8,128)(2,1)}, bf16[256,768]{1,0:T(8,128)(2,1)}, u32[]{:S(2)}, u32[]{:S(2)}) collective-permute-start(bf16[256,768]{1,0:T(8,128)(2,1)} %get-tuple-element.94), channel_id=1, source_target_pairs={{1,0},{16,1},{0,16},{3,2},{18,3},{2,18},{5,4},{20,5},{4,20},{7,6},... | collective-permute-start | bytes 1179656 | tf_op jit(solution)/shard_map/ppermute | solution.py:367
  283.6 51.3 %collective-permute-start.44 = (bf16[768,1152]{1,0:T(8,128)(2,1)}, bf16[768,1152]{1,0:T(8,128)(2,1)}, u32[]{:S(2)}, u32[]{:S(2)}) collective-permute-start(bf16[768,1152]{1,0:T(8,128)(2,1)} %get-tuple-element.68), channel_id=1, source_target_pairs={{0,1},{1,0},{2,3},{3,2},{4,5},{5,4},{6,7},{7,6},{8,9},{9,8},{10,11... | collective-permute-start | bytes 5308424 | tf_op jit(solution)/shard_map/ppermute | solution.py:367
  298.2 66.7 %collective-permute-start.53 = (bf16[4,2,48,1024]{3,2,0,1:T(8,128)(2,1)S(1)}, bf16[4,2,48,1024]{3,2,0,1:T(8,128)(2,1)S(1)}, u32[]{:S(2)}, u32[]{:S(2)}) collective-permute-start(bf16[4,2,48,1024]{3,2,0,1:T(8,128)(2,1)S(1)} %copy.110), channel_id=1, source_target_pairs={{0,16},{1,17},{2,18},{3,19},{4,20},{5,21},{6,22},{7,23},{8,24},{9,... | collective-permute-start | bytes 2359304 | tf_op jit(solution)/shard_map/ppermute | solution.py:367
  306.9 26.0 %collective-permute-start.65 = (bf16[4,48,768]{2,1,0:T(8,128)(2,1)S(1)}, bf16[4,48,768]{2,1,0:T(8,128)(2,1)S(1)}, u32[]{:S(2)}, u32[]{:S(2)}) collective-permute-start(bf16[4,48,768]{2,1,0:T(8,128)(2,1)S(1)} %fusion.10), channel_id=1, source_target_pairs={{0,16},{1,17},{2,18},{3,19},{4,20},{5,21},{6,22},{7,23},{8,24},{9,... | collective-permute-start | bytes 884744 | tf_op jit(solution)/shard_map/ppermute | solution.py:367
  310.7 22.3 %collective-permute-start.63 = (bf16[4,48,768]{2,1,0:T(8,128)(2,1)S(1)}, bf16[4,48,768]{2,1,0:T(8,128)(2,1)S(1)}, u32[]{:S(2)}, u32[]{:S(2)}) collective-permute-start(bf16[4,48,768]{2,1,0:T(8,128)(2,1)S(1)} %fusion.12), channel_id=1, source_target_pairs={{0,2},{1,3},{2,0},{3,1},{4,6},{5,7},{6,4},{7,5},{8,10},{9,11},{10,... | collective-permute-start | bytes 884744 | tf_op jit(solution)/shard_map/ppermute | solution.py:367
  312.8 29.1 %collective-permute-start.55 = (bf16[2,4,48,896]{3,2,1,0:T(8,128)(2,1)S(1)}, bf16[2,4,48,896]{3,2,1,0:T(8,128)(2,1)S(1)}, u32[]{:S(2)}, u32[]{:S(2)}) collective-permute-start(bf16[2,4,48,896]{3,2,1,0:T(8,128)(2,1)S(1)} %fusion.6), channel_id=1, source_target_pairs={{0,2},{1,3},{2,0},{3,1},{4,6},{5,7},{6,4},{7,5},{8,10},{9,11},{10,... | collective-permute-start | bytes 2064392 | tf_op jit(solution)/shard_map/ppermute | solution.py:367
  350.0 22.6 %collective-permute-start.56 = (bf16[4,48,896]{2,1,0:T(8,128)(2,1)S(1)}, bf16[4,48,896]{2,1,0:T(8,128)(2,1)S(1)}, u32[]{:S(2)}, u32[]{:S(2)}) collective-permute-start(bf16[4,48,896]{2,1,0:T(8,128)(2,1)S(1)} %fusion.7), channel_id=1, source_target_pairs={{0,16},{1,17},{2,18},{3,19},{4,20},{5,21},{6,22},{7,23},{8,24},{9,... | collective-permute-start | bytes 1032200 | tf_op jit(solution)/shard_map/ppermute | solution.py:367
  (126 other events, 1391.0 us)

commit v3 on v2

--- a/solution.py
+++ b/solution.py
@@ -539,6 +539,15 @@
     return low, high
 
 
+def masked(scores, bias, part):
+    if part == 0:
+        return scores + bias[...]
+    chunks = [scores[k * QUARTER : (k + 1) * QUARTER] for k in range(4)]
+    for k in (1, 3):
+        chunks[k] = chunks[k] + bias[k * QUARTER : (k + 1) * QUARTER]
+    return jnp.concatenate(chunks, axis=0)
+
+
 def forward_kernel(scalars, q, k_own, k_other, v_own, v_other, out, lse, low_bias, high_bias):
     @pl.when(pl.program_id(0) == 0)
     def _():
@@ -552,7 +561,7 @@
         query = q[rows, :] * jnp.bfloat16(scale)
         tops = []
         for head in range(2):
-            scores = dot_nt(key, head_lanes(query, head)) + bias[...]
+            scores = masked(dot_nt(key, head_lanes(query, head)), bias, part)
             top = jnp.max(scores, axis=0, keepdims=True)
             expo = jnp.exp(scores - top)
             total = jnp.sum(expo, axis=0, keepdims=True)
@@ -584,7 +593,7 @@
         for head in range(2):
             query_head = head_lanes(query, head)
             grad_head = head_lanes(grad_out, head)
-            scores = dot_nt(key, query_head) + bias[...]
+            scores = masked(dot_nt(key, query_head), bias, part)
             probs = jnp.exp(scores - lse[0, pl.ds(head, 1), rows])
             grad_probs = dot_nt(value, grad_head)
             delta = jnp.sum(probs * grad_probs, axis=0, keepdims=True)
@@ -881,7 +890,7 @@
         ),
         out_shape=[array((ROWS, D), F32), array((ROWS, D)), array((ROWS, FF)), array((ROWS, FF))],
         cost_estimate=cost(4 * 10**9, 16 * 10**6),
-        compiler_params=pltpu.CompilerParams(vmem_limit_bytes=20 * MIB),
+        compiler_params=pltpu.CompilerParams(vmem_limit_bytes=17 * MIB),
         name="mlp_up",
     )(scalars, heads, tok, vec, up_bias, *pieces)
 
@@ -1008,7 +1017,7 @@
             array((ROWS, D)), array((ROWS, D)), array((8, D), F32),
         ],
         cost_estimate=cost(10**10, 30 * 10**6),
-        compiler_params=pltpu.CompilerParams(vmem_limit_bytes=31 * MIB),
+        compiler_params=pltpu.CompilerParams(vmem_limit_bytes=29 * MIB),
         name="mlp_mid",
     )(scalars, act, slope, mid, cot, vec, *down_pieces, *up_pieces)
 

time: 401 us -> 400 us (level)
  no operation moved by 1% of the time
where the time goes in v3:
time: 400 us; the launch traced here: 394 us
  waiting for transfers between devices  129 us (32%)
  Pallas kernels  105 us (26%)
  starting transfers between devices  93.6 us (23%)
  local copies, waits for them, and re-layouts  32.9 us (8%)
  other arithmetic  29.5 us (7%)
    ppermute x68, waiting for transfers between devices, send(): return lax.ppermute(array, AXES, pairs)  129 us
    ppermute x68, starting transfers between devices, send(): return lax.ppermute(array, AXES, pairs)  80.6 us
    pallas_call x1, Pallas kernels, attend_back(): pl.pallas_call(backward_kernel, grid_spec=pltpu.PrefetchScalarGridSpec(nu...  20.6 us
    unnamed x163, local copies, waits for them, and re-layouts  19.3 us
    pallas_call x1, Pallas kernels, mlp_mid(): pl.pallas_call(mlp_mid_kernel, grid_spec=pltpu.PrefetchScalarGridSpec(num...  18.2 us
    pallas_call x2, Pallas kernels, attend(): pl.pallas_call(forward_kernel, grid_spec=pltpu.PrefetchScalarGridSpec(num...  17.5 us
    pallas_call x2, Pallas kernels, weight_grad(): pl.pallas_call(lambda *refs: weight_grad_kernel(tiles, lefts, *refs), gri...  15.9 us
    all_to_all x3, starting transfers between devices, exchange(): return lax.all_to_all(array, AXES, 0, 0, tiled=True)  13 us
  transfers between devices with their start and end apart: 71, of which 20 were waited for; matrix products, arithmetic and copies ran while one was open for 11% of the time, Pallas kernels for 17%

profile of v3, /device:TPU:0, one launch (start us, length us, event | category | flops | bytes accessed | tf_op | source)
XLA Modules:
  0.0 394.1 jit_solution(659680866859087972)
XLA Ops:
  3.0 7.3 %all-to-all-start = ((s32[32,1,8]{2,1,0:T(1,128)}), s32[32,1,8]{2,1,0:T(1,128)S(1)}, u32[]{:S(2)}, u32[]{:S(2)}) async-start(s32[32,1,8]{2,1,0:T(1,128)} %broadcast_in_dim.33), calls=%async_computation | async-start | bytes 32768 | tf_op jit(solution)/shard_map/all_to_all | solution.py:375
  35.6 9.0 %collective-permute-done.4 = bf16[48,1152]{1,0:T(8,128)(2,1)S(1)} collective-permute-done((bf16[48,1152]{1,0:T(8,128)(2,1)S(1)}, bf16[48,1152]{1,0:T(8,128)(2,1)S(1)}, u32[]{:S(2)}, u32[]{:S(2)}) %collective-permute-start.4) | collective-permute-done | bytes 110624 | tf_op jit(solution)/shard_map/ppermute | solution.py:367
  48.4 5.6 %collective-permute-done.17 = bf16[48,1920]{1,0:T(8,128)(2,1)S(1)} collective-permute-done((bf16[48,1920]{1,0:T(8,128)(2,1)S(1)}, bf16[48,1920]{1,0:T(8,128)(2,1)S(1)}, u32[]{:S(2)}, u32[]{:S(2)}) %collective-permute-start.17) | collective-permute-done | bytes 184352 | tf_op jit(solution)/shard_map/ppermute | solution.py:367
  61.0 5.9 %collective-permute-done.8.refs_3_ = bf16[4,48,1152]{2,1,0:T(8,128)(2,1)S(1)} collective-permute-done((bf16[4,48,1152]{2,1,0:T(8,128)(2,1)S(1)}, bf16[4,48,1152]{2,1,0:T(8,128)(2,1)S(1)}, u32[]{:S(2)}, u32[]{:S(2)}) %collective-permute-start.8) | collective-permute-done | bytes 442400 | tf_op jit(solution)/shard_map/ppermute | solution.py:367
  70.6 5.1 %collective-permute-start.30 = (bf16[2,96,768]{2,1,0:T(8,128)(2,1)S(1)}, bf16[2,96,768]{2,1,0:T(8,128)(2,1)S(1)}, u32[]{:S(2)}, u32[]{:S(2)}) collective-permute-start(bf16[2,96,768]{2,1,0:T(8,128)(2,1)S(1)} %pad_maximum_fusion.12), channel_id=1, source_target_pairs={{0,4},{1,5},{2,6},{3,7},{4,0},{5,1},{6,2},{7,3},{8,12},{9,13},{10,... | collective-permute-start | bytes 884744 | tf_op jit(solution)/shard_map/ppermute | solution.py:367
  80.0 6.0 %project.1 = (f32[16,768]{1,0:T(8,128)S(1)}, bf16[512,768]{1,0:T(8,128)(2,1)S(1)}, bf16[512,768]{1,0:T(8,128)(2,1)S(1)}, bf16[512,1536]{1,0:T(8,128)(2,1)S(1)}) custom-call(s32[5]{0:T(128)S(1)} %pad_add_fusion.1.scalars.refs_0_, bf16[512,768]{1,0:T(8,128)(2,1)S(1)} %pad_maximum_fusion.1.tok, bf16[32,16,24]{2,1,0:T(8,128)(2,1)S(1)} %reshape.257.owned, ...), custom_call_target="tpu_custom_call" | custom-call | flops 2000000000 | bytes 8000000 | tf_op jit(solution)/shard_map/project/pallas_call | solution.py:821
  98.6 6.6 %collective-permute-done.28 = bf16[256,768]{1,0:T(8,128)(2,1)S(1)} collective-permute-done((bf16[256,768]{1,0:T(8,128)(2,1)S(1)}, bf16[256,768]{1,0:T(8,128)(2,1)S(1)}, u32[]{:S(2)}, u32[]{:S(2)}) %collective-permute-start.28) | collective-permute-done | bytes 393248 | tf_op jit(solution)/shard_map/ppermute | solution.py:367
  106.2 31.1 %collective-permute-done.33 = bf16[4,96,384]{2,1,0:T(8,128)(2,1)} collective-permute-done((bf16[4,96,384]{2,1,0:T(8,128)(2,1)}, bf16[4,96,384]{2,1,0:T(8,128)(2,1)}, u32[]{:S(2)}, u32[]{:S(2)}) %collective-permute-start.33) | collective-permute-done | bytes 294944 | tf_op jit(solution)/shard_map/ppermute | solution.py:367
  142.3 8.7 %shard_map.297 = (bf16[512,384]{1,0:T(8,128)(2,1)S(1)}, f32[3,2,512]{2,1,0:T(2,128)S(1)}) custom-call(s32[5]{0:T(128)S(1)} %pad_add_fusion.1.scalars.refs_0_, bf16[512,768]{1,0:T(8,128)(2,1)S(1)} %copy-done.4, bf16[512,1536]{1,0:T(8,128)(2,1)S(1)} %get-tuple-element.47.k_own.v_own, bf16[512,1536]{1,0:T(8,128)(2,1)S(1)} %collective-permute-done.13.k_other.v_other, ...), custom_call_target="tpu_custom_call" | custom-call | flops 1000000000 | bytes 2000000 | tf_op jit(solution)/shard_map/pallas_call | solution.py:649
  151.0 8.8 %shard_map.298 = (bf16[512,384]{1,0:T(8,128)(2,1)S(1)}, f32[3,2,512]{2,1,0:T(2,128)S(1)}) custom-call(s32[5]{0:T(128)S(1)} %pad_add_fusion.1.scalars.refs_0_, bf16[512,768]{1,0:T(8,128)(2,1)S(1)} %copy-done.4, bf16[512,1536]{1,0:T(8,128)(2,1)S(1)} %get-tuple-element.47.k_own.v_own, bf16[512,1536]{1,0:T(8,128)(2,1)S(1)} %collective-permute-done.13.k_other.v_other, ...), custom_call_target="tpu_custom_call" | custom-call | flops 1000000000 | bytes 2000000 | tf_op jit(solution)/shard_map/pallas_call | solution.py:649
  161.1 11.0 %mlp_up.1 = (f32[512,768]{1,0:T(8,128)S(1)}, bf16[512,768]{1,0:T(8,128)(2,1)S(1)}, bf16[512,3072]{1,0:T(8,128)(2,1)S(1)}, bf16[512,3072]{1,0:T(8,128)(2,1)S(1)}) custom-call(s32[5]{0:T(128)S(1)} %pad_add_fusion.1.scalars.refs_0_, bf16[512,768]{1,0:T(8,128)(2,1)S(1)} %constant_dynamic-update-slice_fusion.heads.refs_2_, bf16[512,768]{1,0:T(8,128)(2,1)S(1)} %copy-done.17, ...), custom_call_target="tpu_custom_call" | custom-call | flops 4000000000 | bytes 16000000 | tf_op jit(solution)/shard_map/mlp_up/pallas_call | solution.py:877
  174.8 18.2 %mlp_mid.1 = (bf16[512,768]{1,0:T(8,128)(2,1)S(1)}, bf16[512,3072]{1,0:T(8,128)(2,1)S(1)}, f32[1,3072]{1,0:T(1,128)S(1)}, f32[512,768]{1,0:T(8,128)S(1)}, bf16[5...) custom-call(s32[5]{0:T(128)S(1)} %pad_add_fusion.1.scalars.refs_0_, ...), custom_call_target="tpu_custom_call" | custom-call | flops 10000000000 | bytes 30000000 | tf_op jit(solution)/shard_map/mlp_mid/pallas_call | solution.py:999
  193.1 20.6 %attend_back.1 = (bf16[512,768]{1,0:T(8,128)(2,1)S(1)}, bf16[2,512,768]{2,1,0:T(8,128)(2,1)S(1)}, bf16[2,512,768]{2,1,0:T(8,128)(2,1)}) custom-call(s32[5]{0:T(128)S(1)} %pad_add_fusion.1.scalars.refs_0_, bf16[512,768]{1,0:T(8,128)(2,1)S(1)} %copy-done.4, bf16[512,768]{1,0:T(8,128)(2,1)S(1)} %get-tuple-element.55.grad, ...), custom_call_target="tpu_custom_call" | custom-call | flops 20000000000 | bytes 8000000 | tf_op jit(solution)/shard_map/attend_back/pallas_call | solution.py:666
  223.0 6.8 %down_grad.1 = (bf16[1536,768]{1,0:T(8,128)(2,1)}, bf16[1536,768]{1,0:T(8,128)(2,1)S(1)}) custom-call(s32[5]{0:T(128)S(1)} %pad_add_fusion.1.scalars.refs_0_, bf16[512,3072]{1,0:T(8,128)(2,1)S(1)} %copy-done.47, bf16[512,768]{1,0:T(8,128)(2,1)S(1)} %copy-done.20), custom_call_target="tpu_custom_call" | custom-call | flops 3000000000 | bytes 9000000 | tf_op jit(solution)/shard_map/down_grad/pallas_call | solution.py:913
  229.8 9.6 %shard_map.300 = (bf16[768,1920]{1,0:T(8,128)(2,1)}, bf16[768,1920]{1,0:T(8,128)(2,1)S(1)}) custom-call(s32[5]{0:T(128)S(1)} %pad_add_fusion.1.scalars.refs_0_, bf16[512,768]{1,0:T(8,128)(2,1)S(1)} %copy-done.50, bf16[512,768]{1,0:T(8,128)(2,1)S(1)} %copy-done.24, bf16[512,3072]{1,0:T(8,128)(2,1)S(1)} %copy-done.43, bf16[512,768]{1,0:T(8,128)(2,1)S(1)} %copy-done.52), custom_call_target="tpu_custom_call" | custom-call | flops 3000000000 | bytes 10000000 | tf_op jit(solution)/shard_map/pallas_call | solution.py:1069
  252.0 8.9 %project_back.1 = (bf16[512,768]{1,0:T(8,128)(2,1)S(1)}, f32[32,16,24]{2,1,0:T(8,128)S(1)}) custom-call(s32[5]{0:T(128)S(1)} %pad_add_fusion.1.scalars.refs_0_, bf16[512,2304]{1,0:T(8,128)(2,1)S(1)} %pad_maximum_fusion.joined.refs_2_, bf16[512,768]{1,0:T(8,128)(2,1)S(1)} %copy-done.18, f32[512,768]{1,0:T(8,128)S(1)} %copy-done.41, ...), custom_call_target="tpu_custom_call" | custom-call | flops 3000000000 | bytes 12000000 | tf_op jit(solution)/shard_map/project_back/pallas_call | solution.py:1144
  264.2 4.5 %collective-permute-start.43 = (bf16[256,768]{1,0:T(8,128)(2,1)}, bf16[256,768]{1,0:T(8,128)(2,1)}, u32[]{:S(2)}, u32[]{:S(2)}) collective-permute-start(bf16[256,768]{1,0:T(8,128)(2,1)} %get-tuple-element.94), channel_id=1, source_target_pairs={{1,0},{16,1},{0,16},{3,2},{18,3},{2,18},{5,4},{20,5},{4,20},{7,6},... | collective-permute-start | bytes 1179656 | tf_op jit(solution)/shard_map/ppermute | solution.py:367
  275.2 6.2 %shard_map.299 = (bf16[768,1152]{1,0:T(8,128)(2,1)}, bf16[768,1152]{1,0:T(8,128)(2,1)S(1)}) custom-call(s32[5]{0:T(128)S(1)} %pad_add_fusion.1.scalars.refs_0_, bf16[512,768]{1,0:T(8,128)(2,1)S(1)} %copy-done.45, bf16[512,2304]{1,0:T(8,128)(2,1)S(1)} %copy-done.9), custom_call_target="tpu_custom_call" | custom-call | flops 1800000000 | bytes 10000000 | tf_op jit(solution)/shard_map/pallas_call | solution.py:1069
  297.8 7.9 %collective-permute-done.64 = bf16[2,4,48,768]{3,2,1,0:T(8,128)(2,1)S(1)} collective-permute-done((bf16[2,4,48,768]{3,2,1,0:T(8,128)(2,1)S(1)}, bf16[2,4,48,768]{3,2,1,0:T(8,128)(2,1)S(1)}, u32[]{:S(2)}, u32[]{:S(2)}) %collective-permute-start.64) | collective-permute-done | bytes 589856 | tf_op jit(solution)/shard_map/ppermute | solution.py:367
  315.0 16.9 %collective-permute-done.65 = bf16[4,48,768]{2,1,0:T(8,128)(2,1)S(1)} collective-permute-done((bf16[4,48,768]{2,1,0:T(8,128)(2,1)S(1)}, bf16[4,48,768]{2,1,0:T(8,128)(2,1)S(1)}, u32[]{:S(2)}, u32[]{:S(2)}) %collective-permute-start.65) | collective-permute-done | bytes 294944 | tf_op jit(solution)/shard_map/ppermute | solution.py:367
  343.8 5.2 %collective-permute-done.67 = bf16[96,768]{1,0:T(8,128)(2,1)S(1)} collective-permute-done((bf16[96,768]{1,0:T(8,128)(2,1)S(1)}, bf16[96,768]{1,0:T(8,128)(2,1)S(1)}, u32[]{:S(2)}, u32[]{:S(2)}) %collective-permute-start.67) | collective-permute-done | bytes 147488 | tf_op jit(solution)/shard_map/ppermute | solution.py:367
  351.3 6.8 %collective-permute-done.46 = bf16[4,48,1152]{2,1,0:T(8,128)(2,1)S(1)} collective-permute-done((bf16[4,48,1152]{2,1,0:T(8,128)(2,1)S(1)}, bf16[4,48,1152]{2,1,0:T(8,128)(2,1)S(1)}, u32[]{:S(2)}, u32[]{:S(2)}) %collective-permute-start.46) | collective-permute-done | bytes 442400 | tf_op jit(solution)/shard_map/ppermute | solution.py:367
  366.8 4.5 %collective-permute-done.49 = bf16[48,1152]{1,0:T(8,128)(2,1)S(1)} collective-permute-done((bf16[48,1152]{1,0:T(8,128)(2,1)S(1)}, bf16[48,1152]{1,0:T(8,128)(2,1)S(1)}, u32[]{:S(2)}, u32[]{:S(2)}) %collective-permute-start.49) | collective-permute-done | bytes 110624 | tf_op jit(solution)/shard_map/ppermute | solution.py:367
  383.0 7.8 %collective-permute-done.58 = bf16[48,1920]{1,0:T(8,128)(2,1)S(1)} collective-permute-done((bf16[48,1920]{1,0:T(8,128)(2,1)S(1)}, bf16[48,1920]{1,0:T(8,128)(2,1)S(1)}, u32[]{:S(2)}, u32[]{:S(2)}) %collective-permute-start.58) | collective-permute-done | bytes 184352 | tf_op jit(solution)/shard_map/ppermute | solution.py:367
  (391 shorter events, 161.7 us)
Async XLA Ops:
  12.4 47.3 %collective-permute-start = (bf16[256,768]{1,0:T(8,128)(2,1)}, bf16[256,768]{1,0:T(8,128)(2,1)}, u32[]{:S(2)}, u32[]{:S(2)}) collective-permute-start(bf16[256,768]{1,0:T(8,128)(2,1)} %get-tuple-element.99), channel_id=1, source_target_pairs={{16,1},{17,16},{1,17},{18,3},{19,18},{3,19},{20,5},{21,20},{5,21},... | collective-permute-start | bytes 1179656 | tf_op jit(solution)/shard_map/ppermute | solution.py:367
  16.5 28.8 %collective-permute-start.29 = (bf16[1,96,768]{2,1,0:T(8,128)(2,1)S(1)}, bf16[1,96,768]{2,1,0:T(8,128)(2,1)S(1)}, u32[]{:S(2)}, u32[]{:S(2)}) collective-permute-start(bf16[1,96,768]{2,1,0:T(8,128)(2,1)S(1)} %bitcast.381), channel_id=1, source_target_pairs={{0,8},{1,9},{2,10},{3,11},{4,12},{5,13},{6,14},{7,15},{8,0},{9,1},... | collective-permute-start | bytes 442376 | tf_op jit(solution)/shard_map/ppermute | solution.py:367
  21.0 35.4 %all-to-all-start.1 = ((bf16[32,2,192]{2,1,0:T(2,128)(2,1)}), bf16[32,2,192]{2,1,0:T(2,128)(2,1)S(1)}, u32[]{:S(2)}, u32[]{:S(2)}) async-start(bf16[32,2,192]{2,1,0:T(2,128)(2,1)} %reshape.256), calls=%async_computation.1 | async-start | bytes 65536 | tf_op jit(solution)/shard_map/all_to_all | solution.py:375
  86.1 54.4 %collective-permute-start.13 = (bf16[512,1536]{1,0:T(8,128)(2,1)S(1)}, bf16[512,1536]{1,0:T(8,128)(2,1)S(1)}, u32[]{:S(2)}, u32[]{:S(2)}) collective-permute-start(bf16[512,1536]{1,0:T(8,128)(2,1)S(1)} %get-tuple-element.47.k_own.v_own), channel_id=1, source_target_pairs={{0,1},{1,0},{2,3},{3,2},{4,5},{5,4},{6,7},{7,6},{8,9},{9,8},{10,11... | collective-permute-start | bytes 4718600 | tf_op jit(solution)/shard_map/ppermute | solution.py:367
  93.3 47.2 %collective-permute-start.20 = (bf16[8,48,1024]{2,1,0:T(8,128)(2,1)}, bf16[8,48,1024]{2,1,0:T(8,128)(2,1)}, u32[]{:S(2)}, u32[]{:S(2)}) collective-permute-start(bf16[8,48,1024]{2,1,0:T(8,128)(2,1)} %pad_maximum_fusion.2.refs_0_.refs_8_), channel_id=1, source_target_pairs={{0,16},{1,17},{2,18},{3,19},{4,20},{5,21},{6,22},{7,23},{8,24},{9,... | collective-permute-start | bytes 2359304 | tf_op jit(solution)/shard_map/ppermute | solution.py:367
  96.4 42.6 %collective-permute-start.22 = (bf16[8,48,896]{2,1,0:T(8,128)(2,1)}, bf16[8,48,896]{2,1,0:T(8,128)(2,1)}, u32[]{:S(2)}, u32[]{:S(2)}) collective-permute-start(bf16[8,48,896]{2,1,0:T(8,128)(2,1)} %pad_maximum_fusion.5.refs_2_.refs_10_), channel_id=1, source_target_pairs={{0,2},{1,3},{2,0},{3,1},{4,6},{5,7},{6,4},{7,5},{8,10},{9,11},{10,... | collective-permute-start | bytes 2064392 | tf_op jit(solution)/shard_map/ppermute | solution.py:367
  97.9 40.5 %collective-permute-start.32 = (bf16[8,96,384]{2,1,0:T(8,128)(2,1)}, bf16[8,96,384]{2,1,0:T(8,128)(2,1)}, u32[]{:S(2)}, u32[]{:S(2)}) collective-permute-start(bf16[8,96,384]{2,1,0:T(8,128)(2,1)} %pad_maximum_fusion.7.refs_0_), channel_id=1, source_target_pairs={{0,16},{1,17},{2,18},{3,19},{4,20},{5,21},{6,22},{7,23},{8,24},{9,... | collective-permute-start | bytes 1769480 | tf_op jit(solution)/shard_map/ppermute | solution.py:367
  105.3 32.1 %collective-permute-start.33 = (bf16[4,96,384]{2,1,0:T(8,128)(2,1)}, bf16[4,96,384]{2,1,0:T(8,128)(2,1)}, u32[]{:S(2)}, u32[]{:S(2)}) collective-permute-start(bf16[4,96,384]{2,1,0:T(8,128)(2,1)} %get-tuple-element.104), channel_id=1, source_target_pairs={{0,16},{1,17},{2,18},{3,19},{4,20},{5,21},{6,22},{7,23},{8,24},{9,... | collective-permute-start | bytes 884744 | tf_op jit(solution)/shard_map/ppermute | solution.py:367
  137.3 23.2 %collective-permute-start.23 = (bf16[8,48,1024]{2,1,0:T(8,128)(2,1)}, bf16[8,48,1024]{2,1,0:T(8,128)(2,1)S(1)}, u32[]{:S(2)}, u32[]{:S(2)}) collective-permute-start(bf16[8,48,1024]{2,1,0:T(8,128)(2,1)} %pad_maximum_fusion.2.refs_0_.refs_8_), channel_id=1, source_target_pairs={{0,1},{1,0},{2,3},{3,2},{4,5},{5,4},{6,7},{7,6},{8,9},{9,8},{10,11... | collective-permute-start | bytes 2359304 | tf_op jit(solution)/shard_map/ppermute | solution.py:367
  138.5 21.6 %collective-permute-start.25 = (bf16[8,48,896]{2,1,0:T(8,128)(2,1)}, bf16[8,48,896]{2,1,0:T(8,128)(2,1)S(1)}, u32[]{:S(2)}, u32[]{:S(2)}) collective-permute-start(bf16[8,48,896]{2,1,0:T(8,128)(2,1)} %pad_maximum_fusion.5.refs_2_.refs_10_), channel_id=1, source_target_pairs={{0,1},{1,0},{2,3},{3,2},{4,5},{5,4},{6,7},{7,6},{8,9},{9,8},{10,11... | collective-permute-start | bytes 2064392 | tf_op jit(solution)/shard_map/ppermute | solution.py:367
  215.8 29.5 %collective-permute-start.41 = (bf16[2,512,768]{2,1,0:T(8,128)(2,1)}, bf16[2,512,768]{2,1,0:T(8,128)(2,1)}, u32[]{:S(2)}, u32[]{:S(2)}) collective-permute-start(bf16[2,512,768]{2,1,0:T(8,128)(2,1)} %get-tuple-element.60), channel_id=1, source_target_pairs={{0,1},{1,0},{2,3},{3,2},{4,5},{5,4},{6,7},{7,6},{8,9},{9,8},{10,11... | collective-permute-start | bytes 4718600 | tf_op jit(solution)/shard_map/ppermute | solution.py:367
  217.1 27.1 %collective-permute-start.39 = (bf16[256,768]{1,0:T(8,128)(2,1)S(1)}, bf16[256,768]{1,0:T(8,128)(2,1)S(1)}, u32[]{:S(2)}, u32[]{:S(2)}) collective-permute-start(bf16[256,768]{1,0:T(8,128)(2,1)S(1)} %get-tuple-element.95), channel_id=1, source_target_pairs={{1,16},{16,17},{17,1},{3,18},{18,19},{19,3},{5,20},{20,21},{21,5},... | collective-permute-start | bytes 1179656 | tf_op jit(solution)/shard_map/ppermute | solution.py:367
  217.8 26.4 %collective-permute-start.40 = (bf16[256,768]{1,0:T(8,128)(2,1)S(1)}, bf16[256,768]{1,0:T(8,128)(2,1)S(1)}, u32[]{:S(2)}, u32[]{:S(2)}) collective-permute-start(bf16[256,768]{1,0:T(8,128)(2,1)S(1)} %get-tuple-element.96), channel_id=1, source_target_pairs={{1,0},{16,1},{0,16},{3,2},{18,3},{2,18},{5,4},{20,5},{4,20},{7,6},... | collective-permute-start | bytes 1179656 | tf_op jit(solution)/shard_map/ppermute | solution.py:367
  242.1 53.7 %collective-permute-start.52 = (bf16[768,1920]{1,0:T(8,128)(2,1)}, bf16[768,1920]{1,0:T(8,128)(2,1)}, u32[]{:S(2)}, u32[]{:S(2)}) collective-permute-start(bf16[768,1920]{1,0:T(8,128)(2,1)} %get-tuple-element.73), channel_id=1, source_target_pairs={{0,1},{1,0},{2,3},{3,2},{4,5},{5,4},{6,7},{7,6},{8,9},{9,8},{10,11... | collective-permute-start | bytes 8847368 | tf_op jit(solution)/shard_map/ppermute | solution.py:367
  242.6 45.4 %collective-permute-start.61 = (bf16[1536,768]{1,0:T(8,128)(2,1)}, bf16[1536,768]{1,0:T(8,128)(2,1)}, u32[]{:S(2)}, u32[]{:S(2)}) collective-permute-start(bf16[1536,768]{1,0:T(8,128)(2,1)} %get-tuple-element.75), channel_id=1, source_target_pairs={{0,1},{1,0},{2,3},{3,2},{4,5},{5,4},{6,7},{7,6},{8,9},{9,8},{10,11... | collective-permute-start | bytes 7077896 | tf_op jit(solution)/shard_map/ppermute | solution.py:367
  262.8 23.8 %collective-permute-start.42 = (bf16[256,768]{1,0:T(8,128)(2,1)}, bf16[256,768]{1,0:T(8,128)(2,1)}, u32[]{:S(2)}, u32[]{:S(2)}) collective-permute-start(bf16[256,768]{1,0:T(8,128)(2,1)} %get-tuple-element.93), channel_id=1, source_target_pairs={{1,16},{16,17},{17,1},{3,18},{18,19},{19,3},{5,20},{20,21},{21,5},... | collective-permute-start | bytes 1179656 | tf_op jit(solution)/shard_map/ppermute | solution.py:367
  264.2 22.3 %collective-permute-start.43 = (bf16[256,768]{1,0:T(8,128)(2,1)}, bf16[256,768]{1,0:T(8,128)(2,1)}, u32[]{:S(2)}, u32[]{:S(2)}) collective-permute-start(bf16[256,768]{1,0:T(8,128)(2,1)} %get-tuple-element.94), channel_id=1, source_target_pairs={{1,0},{16,1},{0,16},{3,2},{18,3},{2,18},{5,4},{20,5},{4,20},{7,6},... | collective-permute-start | bytes 1179656 | tf_op jit(solution)/shard_map/ppermute | solution.py:367
  282.6 51.3 %collective-permute-start.44 = (bf16[768,1152]{1,0:T(8,128)(2,1)}, bf16[768,1152]{1,0:T(8,128)(2,1)}, u32[]{:S(2)}, u32[]{:S(2)}) collective-permute-start(bf16[768,1152]{1,0:T(8,128)(2,1)} %get-tuple-element.68), channel_id=1, source_target_pairs={{0,1},{1,0},{2,3},{3,2},{4,5},{5,4},{6,7},{7,6},{8,9},{9,8},{10,11... | collective-permute-start | bytes 5308424 | tf_op jit(solution)/shard_map/ppermute | solution.py:367
  297.2 66.7 %collective-permute-start.53 = (bf16[4,2,48,1024]{3,2,0,1:T(8,128)(2,1)S(1)}, bf16[4,2,48,1024]{3,2,0,1:T(8,128)(2,1)S(1)}, u32[]{:S(2)}, u32[]{:S(2)}) collective-permute-start(bf16[4,2,48,1024]{3,2,0,1:T(8,128)(2,1)S(1)} %copy.110), channel_id=1, source_target_pairs={{0,16},{1,17},{2,18},{3,19},{4,20},{5,21},{6,22},{7,23},{8,24},{9,... | collective-permute-start | bytes 2359304 | tf_op jit(solution)/shard_map/ppermute | solution.py:367
  305.9 26.0 %collective-permute-start.65 = (bf16[4,48,768]{2,1,0:T(8,128)(2,1)S(1)}, bf16[4,48,768]{2,1,0:T(8,128)(2,1)S(1)}, u32[]{:S(2)}, u32[]{:S(2)}) collective-permute-start(bf16[4,48,768]{2,1,0:T(8,128)(2,1)S(1)} %fusion.10), channel_id=1, source_target_pairs={{0,16},{1,17},{2,18},{3,19},{4,20},{5,21},{6,22},{7,23},{8,24},{9,... | collective-permute-start | bytes 884744 | tf_op jit(solution)/shard_map/ppermute | solution.py:367
  309.7 22.3 %collective-permute-start.63 = (bf16[4,48,768]{2,1,0:T(8,128)(2,1)S(1)}, bf16[4,48,768]{2,1,0:T(8,128)(2,1)S(1)}, u32[]{:S(2)}, u32[]{:S(2)}) collective-permute-start(bf16[4,48,768]{2,1,0:T(8,128)(2,1)S(1)} %fusion.12), channel_id=1, source_target_pairs={{0,2},{1,3},{2,0},{3,1},{4,6},{5,7},{6,4},{7,5},{8,10},{9,11},{10,... | collective-permute-start | bytes 884744 | tf_op jit(solution)/shard_map/ppermute | solution.py:367
  311.7 29.1 %collective-permute-start.55 = (bf16[2,4,48,896]{3,2,1,0:T(8,128)(2,1)S(1)}, bf16[2,4,48,896]{3,2,1,0:T(8,128)(2,1)S(1)}, u32[]{:S(2)}, u32[]{:S(2)}) collective-permute-start(bf16[2,4,48,896]{3,2,1,0:T(8,128)(2,1)S(1)} %fusion.6), channel_id=1, source_target_pairs={{0,2},{1,3},{2,0},{3,1},{4,6},{5,7},{6,4},{7,5},{8,10},{9,11},{10,... | collective-permute-start | bytes 2064392 | tf_op jit(solution)/shard_map/ppermute | solution.py:367
  337.0 21.1 %collective-permute-start.46 = (bf16[4,48,1152]{2,1,0:T(8,128)(2,1)S(1)}, bf16[4,48,1152]{2,1,0:T(8,128)(2,1)S(1)}, u32[]{:S(2)}, u32[]{:S(2)}) collective-permute-start(bf16[4,48,1152]{2,1,0:T(8,128)(2,1)S(1)} %get-tuple-element.77), channel_id=1, source_target_pairs={{0,16},{1,17},{2,18},{3,19},{4,20},{5,21},{6,22},{7,23},{8,24},{9,... | collective-permute-start | bytes 1327112 | tf_op jit(solution)/shard_map/ppermute | solution.py:367
  348.9 22.6 %collective-permute-start.56 = (bf16[4,48,896]{2,1,0:T(8,128)(2,1)S(1)}, bf16[4,48,896]{2,1,0:T(8,128)(2,1)S(1)}, u32[]{:S(2)}, u32[]{:S(2)}) collective-permute-start(bf16[4,48,896]{2,1,0:T(8,128)(2,1)S(1)} %fusion.7), channel_id=1, source_target_pairs={{0,16},{1,17},{2,18},{3,19},{4,20},{5,21},{6,22},{7,23},{8,24},{9,... | collective-permute-start | bytes 1032200 | tf_op jit(solution)/shard_map/ppermute | solution.py:367
  (126 other events, 1387.3 us)
